TPU v7x, 32 devices: a whole 2x2x4 slice. The times are simulated.
32 devices in a mesh: row: 4 (over z), col: 4 (over y, core), rep: 2 (over x).
Axes of the slice: x: 2, y: 2, z: 4, core: 2. Of those that a mesh axis runs over, the one named last changes fastest.
Arguments:
- a_blocks: bfloat16 [96, 17, 128, 128], P(('row', 'col'), None, 'rep'), may hold values from -0.1875 to 0.1875
- b_blocks: bfloat16 [96, 17, 128, 128], P(('row', 'col'), None, 'rep'), may hold values from -6 to 6
- a_extent: int32 [96], P(('row', 'col')), may hold values from 1 to 8, as said below
- b_extent: int32 [96], P(('row', 'col')), may hold values from 1 to 8, as said below
Outputs:
- c_blocks: bfloat16 [96, 33, 128, 128], P(('row', 'col', 'rep'))
Inputs may be any that keep to these rules, and one draw needn't show every extreme that they name: Blocks of row i whose offset |a - 8| exceeds a_extent[i] are absent. Blocks of row j whose offset |b - 8| exceeds b_extent[j] are absent.
All inputs are finite; a program needn't handle non-finite values.
Results may differ from a plain program's by a relative error of at most 0.0052.
Values may be sent and summed in bfloat16 or wider, within the bound.
No kernel may reach another device: no remote copies, remote signals or barrier semaphores. Data moves between devices by JAX's collectives and lax.ppermute only.
A program may use at most 128 MiB of HBM per device.

v0:
```python
import jax
import jax.numpy as jnp
from jax import lax
from jax.sharding import PartitionSpec as P


def passed_along(x, axis, by):
    size = lax.axis_size(axis)
    return lax.ppermute(x, axis, [(i, (i + by) % size) for i in range(size)])


def band_live(extent, band_width):
    half_band = (band_width - 1) // 2
    distance = jnp.abs(jnp.arange(band_width) - half_band)
    return (distance[None, :] <= extent[:, None]).astype(jnp.bfloat16)


def local(a_blocks, b_blocks, a_extent, b_extent):
    row_count = a_blocks.shape[0]
    band_width = a_blocks.shape[1]
    half_band = (band_width - 1) // 2
    block_size = a_blocks.shape[3]
    hop_count = (half_band + row_count - 1) // row_count
    a_masked = a_blocks * band_live(a_extent, band_width)[:, :, None, None]
    below_blocks = []
    below_extent = []
    above_blocks = []
    above_extent = []
    for hop_index in range(1, hop_count + 1):
        far_blocks, far_extent = passed_along((b_blocks, b_extent), ("row", "col"), hop_index)
        below_blocks.insert(0, far_blocks)
        below_extent.insert(0, far_extent)
        near_blocks, near_extent = passed_along((b_blocks, b_extent), ("row", "col"), -hop_index)
        above_blocks.append(near_blocks)
        above_extent.append(near_extent)
    lower_blocks = jnp.concatenate(below_blocks, 0)[-half_band:]
    lower_extent = jnp.concatenate(below_extent, 0)[-half_band:]
    upper_blocks = jnp.concatenate(above_blocks, 0)[:half_band]
    upper_extent = jnp.concatenate(above_extent, 0)[:half_band]
    b_window = jnp.concatenate([lower_blocks, b_blocks, upper_blocks], 0)
    window_extent = jnp.concatenate([lower_extent, b_extent, upper_extent], 0)
    b_masked = b_window * band_live(window_extent, band_width)[:, :, None, None]

    def product_at(offset):
        left_operand = lax.dynamic_index_in_dim(a_masked, offset, 1, keepdims=False)
        right_operand = lax.dynamic_slice_in_dim(b_masked, offset, row_count, 0)
        return jnp.einsum(
            "ikm,ibkn->ibmn", left_operand, right_operand, preferred_element_type=jnp.float32
        )

    def add_pair(pair_index, totals):
        offset_one = 2 * pair_index
        product_one = product_at(offset_one)
        product_two = product_at(offset_one + 1)
        zero_block = jnp.zeros((row_count, 1, block_size, block_size), jnp.float32)
        window = lax.dynamic_slice_in_dim(totals, offset_one, band_width + 1, 1)
        window = (
            window
            + jnp.concatenate([product_one, zero_block], 1)
            + jnp.concatenate([zero_block, product_two], 1)
        )
        return lax.dynamic_update_slice_in_dim(totals, window, offset_one, 1)

    totals = jnp.zeros((row_count, 2 * band_width - 1, block_size, block_size), jnp.float32)
    totals = lax.fori_loop(0, half_band, add_pair, totals)
    final_product = product_at(2 * half_band)
    totals = totals.at[:, 2 * half_band :].add(final_product)
    summed = lax.psum_scatter(totals.astype(jnp.bfloat16), "rep", scatter_dimension=0, tiled=True)
    return summed


def solution(mesh):
    return jax.shard_map(
        local,
        mesh=mesh,
        in_specs=(
            P(("row", "col"), None, "rep", None),
            P(("row", "col"), None, "rep", None),
            P(("row", "col")),
            P(("row", "col")),
        ),
        out_specs=P(("row", "col", "rep"), None, None, None),
        check_vma=False,
    )
```

profile of v0, /device:TPU:0, one launch (start us, length us, event | category | flops | bytes accessed | tf_op | source)
XLA Modules:
  0.0 445.1 jit_solution(6006681998703100014)
XLA Ops:
  19.1 52.6 %collective-permute-done.5 = s32[6]{0:T(128)S(1)} collective-permute-done((s32[6]{0:T(128)}, s32[6]{0:T(128)S(1)}, u32[]{:S(2)}, u32[]{:S(2)}) %collective-permute-start.5) | collective-permute-done | bytes 56 | tf_op jit(solution)/shard_map/ppermute | solution.py:9
  71.7 48.4 %collective-permute-start.4 = (s32[6]{0:T(128)}, s32[6]{0:T(128)S(1)}, u32[]{:S(2)}, u32[]{:S(2)}) collective-permute-start(s32[6]{0:T(128)} %param.11), channel_id=1, source_target_pairs={{0,4},{2,6},{4,8},{6,10},{8,12},{10,14},{12,16},{14,18},{16,20},{1... | collective-permute-start | bytes 80 | tf_op jit(solution)/shard_map/ppermute | solution.py:9
  130.8 5.8 %fusion.9 = bf16[22,17,64,128]{3,2,1,0:T(8,128)(2,1)} fusion(bf16[6,17,64,128]{3,2,1,0:T(8,128)(2,1)} %collective-permute-done.3, bf16[6,17,64,128]{3,2,1,0:T(8,128)(2,1)S(1)} %collective-permute-done.2, bf16[6,17,64,128]{3,2,1,0:T(8,128)(2,1)} %collective-permute-done.1, bf16[6,17,64,128]{3,2,1,0:T(8,128)(2,1)} %collective-permute-done, ...), kind=kLoop, calls=%fused_computation.14 | loop fusion | flops 15319040 | bytes 14484204 | tf_op jit(solution)/shard_map/mul | solution.py:42
  136.7 6.3 %broadcast_in_dim.2 = f32[6,33,128,128]{2,3,1,0:T(8,128)} broadcast(f32[]{:T(128)} %constant.120.clone.1), dimensions={} | broadcast | bytes 12976132 | tf_op jit(solution)/shard_map/broadcast_in_dim | solution.py:64
  143.0 188.7 %while.16 = (s32[]{:T(128)}, f32[6,33,128,128]{2,3,1,0:T(8,128)}, bf16[22,17,64,128]{3,2,1,0:T(8,128)(2,1)}, bf16[6,17,64,128]{3,2,0,1:T(8,128)(2,1)S(1)}, s32[]...) while((s32[]{:T(128)}, f32[6,33,128,128]{2,3,1,0:T(8,128)}, ...), condition=%wide.region_1.2_spmd, body=%wide.region_0.1_spmd.sunk | while | flops 431357952 | bytes 44433712 | solution.py:65
  148.3 5.5 %convolution_bitcast_fusion.5 = f32[6,17,128,128]{2,3,1,0:T(8,128)} fusion(bf16[22,17,64,128]{3,2,1,0:T(8,128)(2,1)} %get-tuple-element.188, s32[]{:T(128)S(6)} %select_n.62, bf16[6,17,64,128]{3,2,0,1:T(8,128)(2,1)S(1)} %get-tuple-element.189, s32[]{:T(128)S(6)} %select_n.63), kind=kOutput, calls=%fused_computation.2.clone.1 | convolution fusion | flops 213909504 | bytes 8454152 | tf_op jit(solution)/shard_map/while/body/eval_jaxpr/ikm,ibkn->ibmn/dot_general | solution.py:47
  153.8 12.8 %add_dynamic-update-slice_fusion.2 = f32[6,33,128,128]{2,3,1,0:T(8,128)} fusion(f32[6,33,128,128]{2,3,1,0:T(8,128)} %get-tuple-element.175, s32[]{:T(128)S(6)} %select_n.59, f32[6,17,128,128]{2,3,1,0:T(8,128)} %convolution_bitcast_fusion.4, f32[6,17,128,128]{2,3,1,0:T(8,128)} %convolution_bitcast_fusion.5), kind=kLoop, calls=%fused_computation.clone.1 | loop fusion | flops 3538944 | bytes 27525124 | tf_op jit(solution)/shard_map/while/body/eval_jaxpr/dynamic_update_slice | solution.py:62
  171.9 5.5 %convolution_bitcast_fusion.5 = f32[6,17,128,128]{2,3,1,0:T(8,128)} fusion(bf16[22,17,64,128]{3,2,1,0:T(8,128)(2,1)} %get-tuple-element.188, s32[]{:T(128)S(6)} %select_n.62, bf16[6,17,64,128]{3,2,0,1:T(8,128)(2,1)S(1)} %get-tuple-element.189, s32[]{:T(128)S(6)} %select_n.63), kind=kOutput, calls=%fused_computation.2.clone.1 | convolution fusion | flops 213909504 | bytes 8454152 | tf_op jit(solution)/shard_map/while/body/eval_jaxpr/ikm,ibkn->ibmn/dot_general | solution.py:47
  177.4 12.8 %add_dynamic-update-slice_fusion.2 = f32[6,33,128,128]{2,3,1,0:T(8,128)} fusion(f32[6,33,128,128]{2,3,1,0:T(8,128)} %get-tuple-element.175, s32[]{:T(128)S(6)} %select_n.59, f32[6,17,128,128]{2,3,1,0:T(8,128)} %convolution_bitcast_fusion.4, f32[6,17,128,128]{2,3,1,0:T(8,128)} %convolution_bitcast_fusion.5), kind=kLoop, calls=%fused_computation.clone.1 | loop fusion | flops 3538944 | bytes 27525124 | tf_op jit(solution)/shard_map/while/body/eval_jaxpr/dynamic_update_slice | solution.py:62
  195.5 5.5 %convolution_bitcast_fusion.5 = f32[6,17,128,128]{2,3,1,0:T(8,128)} fusion(bf16[22,17,64,128]{3,2,1,0:T(8,128)(2,1)} %get-tuple-element.188, s32[]{:T(128)S(6)} %select_n.62, bf16[6,17,64,128]{3,2,0,1:T(8,128)(2,1)S(1)} %get-tuple-element.189, s32[]{:T(128)S(6)} %select_n.63), kind=kOutput, calls=%fused_computation.2.clone.1 | convolution fusion | flops 213909504 | bytes 8454152 | tf_op jit(solution)/shard_map/while/body/eval_jaxpr/ikm,ibkn->ibmn/dot_general | solution.py:47
  201.0 12.8 %add_dynamic-update-slice_fusion.2 = f32[6,33,128,128]{2,3,1,0:T(8,128)} fusion(f32[6,33,128,128]{2,3,1,0:T(8,128)} %get-tuple-element.175, s32[]{:T(128)S(6)} %select_n.59, f32[6,17,128,128]{2,3,1,0:T(8,128)} %convolution_bitcast_fusion.4, f32[6,17,128,128]{2,3,1,0:T(8,128)} %convolution_bitcast_fusion.5), kind=kLoop, calls=%fused_computation.clone.1 | loop fusion | flops 3538944 | bytes 27525124 | tf_op jit(solution)/shard_map/while/body/eval_jaxpr/dynamic_update_slice | solution.py:62
  219.1 5.5 %convolution_bitcast_fusion.5 = f32[6,17,128,128]{2,3,1,0:T(8,128)} fusion(bf16[22,17,64,128]{3,2,1,0:T(8,128)(2,1)} %get-tuple-element.188, s32[]{:T(128)S(6)} %select_n.62, bf16[6,17,64,128]{3,2,0,1:T(8,128)(2,1)S(1)} %get-tuple-element.189, s32[]{:T(128)S(6)} %select_n.63), kind=kOutput, calls=%fused_computation.2.clone.1 | convolution fusion | flops 213909504 | bytes 8454152 | tf_op jit(solution)/shard_map/while/body/eval_jaxpr/ikm,ibkn->ibmn/dot_general | solution.py:47
  224.6 12.7 %add_dynamic-update-slice_fusion.2 = f32[6,33,128,128]{2,3,1,0:T(8,128)} fusion(f32[6,33,128,128]{2,3,1,0:T(8,128)} %get-tuple-element.175, s32[]{:T(128)S(6)} %select_n.59, f32[6,17,128,128]{2,3,1,0:T(8,128)} %convolution_bitcast_fusion.4, f32[6,17,128,128]{2,3,1,0:T(8,128)} %convolution_bitcast_fusion.5), kind=kLoop, calls=%fused_computation.clone.1 | loop fusion | flops 3538944 | bytes 27525124 | tf_op jit(solution)/shard_map/while/body/eval_jaxpr/dynamic_update_slice | solution.py:62
  242.7 5.5 %convolution_bitcast_fusion.5 = f32[6,17,128,128]{2,3,1,0:T(8,128)} fusion(bf16[22,17,64,128]{3,2,1,0:T(8,128)(2,1)} %get-tuple-element.188, s32[]{:T(128)S(6)} %select_n.62, bf16[6,17,64,128]{3,2,0,1:T(8,128)(2,1)S(1)} %get-tuple-element.189, s32[]{:T(128)S(6)} %select_n.63), kind=kOutput, calls=%fused_computation.2.clone.1 | convolution fusion | flops 213909504 | bytes 8454152 | tf_op jit(solution)/shard_map/while/body/eval_jaxpr/ikm,ibkn->ibmn/dot_general | solution.py:47
  248.1 12.7 %add_dynamic-update-slice_fusion.2 = f32[6,33,128,128]{2,3,1,0:T(8,128)} fusion(f32[6,33,128,128]{2,3,1,0:T(8,128)} %get-tuple-element.175, s32[]{:T(128)S(6)} %select_n.59, f32[6,17,128,128]{2,3,1,0:T(8,128)} %convolution_bitcast_fusion.4, f32[6,17,128,128]{2,3,1,0:T(8,128)} %convolution_bitcast_fusion.5), kind=kLoop, calls=%fused_computation.clone.1 | loop fusion | flops 3538944 | bytes 27525124 | tf_op jit(solution)/shard_map/while/body/eval_jaxpr/dynamic_update_slice | solution.py:62
  266.2 5.5 %convolution_bitcast_fusion.5 = f32[6,17,128,128]{2,3,1,0:T(8,128)} fusion(bf16[22,17,64,128]{3,2,1,0:T(8,128)(2,1)} %get-tuple-element.188, s32[]{:T(128)S(6)} %select_n.62, bf16[6,17,64,128]{3,2,0,1:T(8,128)(2,1)S(1)} %get-tuple-element.189, s32[]{:T(128)S(6)} %select_n.63), kind=kOutput, calls=%fused_computation.2.clone.1 | convolution fusion | flops 213909504 | bytes 8454152 | tf_op jit(solution)/shard_map/while/body/eval_jaxpr/ikm,ibkn->ibmn/dot_general | solution.py:47
  271.7 12.7 %add_dynamic-update-slice_fusion.2 = f32[6,33,128,128]{2,3,1,0:T(8,128)} fusion(f32[6,33,128,128]{2,3,1,0:T(8,128)} %get-tuple-element.175, s32[]{:T(128)S(6)} %select_n.59, f32[6,17,128,128]{2,3,1,0:T(8,128)} %convolution_bitcast_fusion.4, f32[6,17,128,128]{2,3,1,0:T(8,128)} %convolution_bitcast_fusion.5), kind=kLoop, calls=%fused_computation.clone.1 | loop fusion | flops 3538944 | bytes 27525124 | tf_op jit(solution)/shard_map/while/body/eval_jaxpr/dynamic_update_slice | solution.py:62
  289.8 5.5 %convolution_bitcast_fusion.5 = f32[6,17,128,128]{2,3,1,0:T(8,128)} fusion(bf16[22,17,64,128]{3,2,1,0:T(8,128)(2,1)} %get-tuple-element.188, s32[]{:T(128)S(6)} %select_n.62, bf16[6,17,64,128]{3,2,0,1:T(8,128)(2,1)S(1)} %get-tuple-element.189, s32[]{:T(128)S(6)} %select_n.63), kind=kOutput, calls=%fused_computation.2.clone.1 | convolution fusion | flops 213909504 | bytes 8454152 | tf_op jit(solution)/shard_map/while/body/eval_jaxpr/ikm,ibkn->ibmn/dot_general | solution.py:47
  295.2 12.8 %add_dynamic-update-slice_fusion.2 = f32[6,33,128,128]{2,3,1,0:T(8,128)} fusion(f32[6,33,128,128]{2,3,1,0:T(8,128)} %get-tuple-element.175, s32[]{:T(128)S(6)} %select_n.59, f32[6,17,128,128]{2,3,1,0:T(8,128)} %convolution_bitcast_fusion.4, f32[6,17,128,128]{2,3,1,0:T(8,128)} %convolution_bitcast_fusion.5), kind=kLoop, calls=%fused_computation.clone.1 | loop fusion | flops 3538944 | bytes 27525124 | tf_op jit(solution)/shard_map/while/body/eval_jaxpr/dynamic_update_slice | solution.py:62
  313.4 5.5 %convolution_bitcast_fusion.5 = f32[6,17,128,128]{2,3,1,0:T(8,128)} fusion(bf16[22,17,64,128]{3,2,1,0:T(8,128)(2,1)} %get-tuple-element.188, s32[]{:T(128)S(6)} %select_n.62, bf16[6,17,64,128]{3,2,0,1:T(8,128)(2,1)S(1)} %get-tuple-element.189, s32[]{:T(128)S(6)} %select_n.63), kind=kOutput, calls=%fused_computation.2.clone.1 | convolution fusion | flops 213909504 | bytes 8454152 | tf_op jit(solution)/shard_map/while/body/eval_jaxpr/ikm,ibkn->ibmn/dot_general | solution.py:47
  318.8 12.8 %add_dynamic-update-slice_fusion.2 = f32[6,33,128,128]{2,3,1,0:T(8,128)} fusion(f32[6,33,128,128]{2,3,1,0:T(8,128)} %get-tuple-element.175, s32[]{:T(128)S(6)} %select_n.59, f32[6,17,128,128]{2,3,1,0:T(8,128)} %convolution_bitcast_fusion.4, f32[6,17,128,128]{2,3,1,0:T(8,128)} %convolution_bitcast_fusion.5), kind=kLoop, calls=%fused_computation.clone.1 | loop fusion | flops 3538944 | bytes 27525124 | tf_op jit(solution)/shard_map/while/body/eval_jaxpr/dynamic_update_slice | solution.py:62
  331.6 6.4 %bitcast_add_fusion = bf16[6,17,128,128]{2,3,1,0:T(8,128)(2,1)} fusion(f32[6,33,128,128]{2,3,1,0:T(8,128)} %get-tuple-element.128, bf16[22,17,64,128]{3,2,1,0:T(8,128)(2,1)} %get-tuple-element.199, bf16[6,17,64,128]{3,2,0,1:T(8,128)(2,1)S(1)} %get-tuple-element.202), kind=kOutput, calls=%fused_computation.11 | convolution fusion | flops 217251840 | bytes 16252928 | tf_op jit(solution)/shard_map/ikm,ibkn->ibmn/dot_general | solution.py:47
  338.1 11.3 %copy.6 = bf16[6,33,128,128]{3,2,1,0:T(8,128)(2,1)} copy(f32[6,33,128,128]{2,3,1,0:T(8,128)} %get-tuple-element.128) | data formatting | bytes 19464192 | tf_op jit(solution)/shard_map/while | solution.py:65
  356.3 82.0 %reduce-scatter.2.cloned.1.call-done = bf16[3,33,128,128]{3,2,1,0:T(8,128)(2,1)} async-done(((bf16[6,33,128,128]{3,2,1,0:T(8,128)(2,1)}), bf16[3,33,128,128]{3,2,1,0:T(8,128)(2,1)}) %reduce-scatter.2.cloned.1.call-update) | async-done | bytes 3244048 | tf_op jit(solution)/shard_map/reduce_scatter | solution.py:68
  (34 shorter events, 73.1 us)
Async XLA Ops:
  6.5 431.7 %reduce-scatter.2.cloned.1.call-start = ((), (), s32[]{:S(2)}) async-start(), calls=%async_computation.1 | async-start | bytes 9732096 | tf_op jit(solution)/shard_map/reduce_scatter | solution.py:68
  6.5 124.3 %collective-permute-start.2 = (bf16[6,17,64,128]{3,2,1,0:T(8,128)(2,1)}, bf16[6,17,64,128]{3,2,1,0:T(8,128)(2,1)S(1)}, u32[]{:S(2)}, u32[]{:S(2)}) collective-permute-start(bf16[6,17,64,128]{3,2,1,0:T(8,128)(2,1)} %param.9), channel_id=1, source_target_pairs={{0,30},{2,0},{4,2},{6,4},{8,6},{10,8},{12,10},{14,12},{16,14},{18,... | collective-permute-start | bytes 5013512 | tf_op jit(solution)/shard_map/ppermute | solution.py:9
  12.0 118.8 %collective-permute-start.1 = (bf16[6,17,64,128]{3,2,1,0:T(8,128)(2,1)}, bf16[6,17,64,128]{3,2,1,0:T(8,128)(2,1)}, u32[]{:S(2)}, u32[]{:S(2)}) collective-permute-start(bf16[6,17,64,128]{3,2,1,0:T(8,128)(2,1)} %param.9), channel_id=1, source_target_pairs={{0,2},{2,4},{4,6},{6,8},{8,10},{10,12},{12,14},{14,16},{16,18},{18... | collective-permute-start | bytes 5013512 | tf_op jit(solution)/shard_map/ppermute | solution.py:9
  12.0 118.8 %collective-permute-start = (bf16[6,17,64,128]{3,2,1,0:T(8,128)(2,1)}, bf16[6,17,64,128]{3,2,1,0:T(8,128)(2,1)}, u32[]{:S(2)}, u32[]{:S(2)}) collective-permute-start(bf16[6,17,64,128]{3,2,1,0:T(8,128)(2,1)} %param.9), channel_id=1, source_target_pairs={{0,4},{2,6},{4,8},{6,10},{8,12},{10,14},{12,16},{14,18},{16,20},{1... | collective-permute-start | bytes 5013512 | tf_op jit(solution)/shard_map/ppermute | solution.py:9
  12.0 118.8 %collective-permute-start.3 = (bf16[6,17,64,128]{3,2,1,0:T(8,128)(2,1)}, bf16[6,17,64,128]{3,2,1,0:T(8,128)(2,1)}, u32[]{:S(2)}, u32[]{:S(2)}) collective-permute-start(bf16[6,17,64,128]{3,2,1,0:T(8,128)(2,1)} %param.9), channel_id=1, source_target_pairs={{0,28},{2,30},{4,0},{6,2},{8,4},{10,6},{12,8},{14,10},{16,12},{18,... | collective-permute-start | bytes 5013512 | tf_op jit(solution)/shard_map/ppermute | solution.py:9
  16.7 54.9 %collective-permute-start.5 = (s32[6]{0:T(128)}, s32[6]{0:T(128)S(1)}, u32[]{:S(2)}, u32[]{:S(2)}) collective-permute-start(s32[6]{0:T(128)} %param.11), channel_id=1, source_target_pairs={{0,2},{2,4},{4,6},{6,8},{8,10},{10,12},{12,14},{14,16},{16,18},{18... | collective-permute-start | bytes 80 | tf_op jit(solution)/shard_map/ppermute | solution.py:9
  71.7 53.1 %collective-permute-start.4 = (s32[6]{0:T(128)}, s32[6]{0:T(128)S(1)}, u32[]{:S(2)}, u32[]{:S(2)}) collective-permute-start(s32[6]{0:T(128)} %param.11), channel_id=1, source_target_pairs={{0,4},{2,6},{4,8},{6,10},{8,12},{10,14},{12,16},{14,18},{16,20},{1... | collective-permute-start | bytes 80 | tf_op jit(solution)/shard_map/ppermute | solution.py:9
  124.8 1.4 collective-permute-start.6
  126.2 3.7 collective-permute-start.7
Sparse Core Ops, SparseCore 0:
  356.4 81.8 reduce-scatter.1
where the time goes:
time: 446 us; the launch traced here: 445 us
  waiting for transfers between devices  142 us (32%)
  other arithmetic  111 us (25%)
  matrix products  93.1 us (21%)
  starting transfers between devices  60.7 us (14%)
  local copies, waits for them, and re-layouts  24.6 us (6%)
  between operations  13.4 us (3%)
    dynamic_update_slice x8, other arithmetic, add_pair(): return lax.dynamic_update_slice_in_dim(totals, window, offset_one, 1)  102 us
    dot_general x17, matrix products, product_at(): jnp.einsum('ikm,ibkn->ibmn', left_operand, right_operand, preferred_eleme...  93.1 us
    reduce_scatter x1, waiting for transfers between devices, local(): lax.psum_scatter(totals.astype(jnp.bfloat16), 'rep', scatter_dimension=0,...  82 us
    ppermute x8, starting transfers between devices, passed_along(): return lax.ppermute(x, axis, [(i, (i + by) % size) for i in range(size)])  60.7 us
    ppermute x8, waiting for transfers between devices, passed_along(): return lax.ppermute(x, axis, [(i, (i + by) % size) for i in range(size)])  60.2 us
    while x1, local copies, waits for them, and re-layouts, local(): totals = lax.fori_loop(0, half_band, add_pair, totals)  11.3 us
  transfers between devices with their start and end apart: 9, of which 5 were waited for; matrix products, arithmetic and copies ran while one was open for 1% of the time, Pallas kernels for 0%

commit v1 on v0

v1 whole, which is shorter than its diff:
```python
import functools

import jax
import jax.numpy as jnp
from jax import lax
from jax.experimental import pallas as pl
from jax.experimental.pallas import tpu as pltpu
from jax.sharding import PartitionSpec as P

RING = ("row", "col")
EVERY = ("row", "col", "rep")
CHUNK_ROWS = 2
EXTRA_ROWS = 2


def band_live(extent, band_width):
    half_band = (band_width - 1) // 2
    distance = jnp.abs(jnp.arange(band_width) - half_band)
    return (distance[None, :] <= extent[:, None]).astype(jnp.bfloat16)


def to_chip_peer(x, ring):
    return lax.ppermute(x, RING, [(g, g ^ 1) for g in range(ring)])


def to_outer_neighbour(x, ring):
    return lax.ppermute(x, RING, [(g, (g + 2 * (g % 2) - 1) % ring) for g in range(ring)])


def to_second_neighbour(x, ring):
    pairs = []
    for g in range(ring):
        owner = g + 1 if g % 2 else g - 1
        pairs.append((2 * g, 2 * ((owner + 2) % ring)))
        pairs.append((2 * g + 1, 2 * ((owner - 2) % ring) + 1))
    return lax.ppermute(x, EVERY, pairs)


def over_rep(x):
    return lax.ppermute(x, "rep", [(0, 1), (1, 0)])


def product_kernel(depth, rows_out, plan, has_partial, *refs):
    refs = list(refs)
    left_ref = refs.pop(0)
    source_refs = [refs.pop(0) for _ in range(plan["sources"])]
    partial_ref = refs.pop(0) if has_partial else None
    out_ref, window, result, row_sem, out_sem = refs
    slots = plan["slots"]
    band = plan["band"]
    block = window.shape[-1]
    pairs = window.shape[0] // 2
    rep = lax.axis_index("rep")
    core = lax.rem(lax.axis_index("col"), 2)

    def row_copy(source, position, slot):
        return pltpu.make_async_copy(
            source.at[position], window.at[pl.ds(slot, band), slot], row_sem.at[slot]
        )

    for rep_value in range(2):
        for core_value in range(2):

            @pl.when((rep == rep_value) & (core == core_value))
            def _(rep_value=rep_value, core_value=core_value):
                for slot, (source, position) in enumerate(plan["where"](rep_value, core_value)):
                    row_copy(source_refs[source], position, slot).start()

    blank = jnp.zeros((depth, block), window.dtype)
    for pair in range(pairs):
        if 2 * pair + 1 < slots:
            window[2 * pair, 2 * pair + 1] = blank
        if 0 <= 2 * pair + 1 - band < slots:
            window[2 * pair + 1, 2 * pair + 1 - band] = blank
        if slots % 2 and slots <= 2 * pair + 1:
            window[2 * pair, slots] = blank
            window[2 * pair + 1, slots] = blank

    waited = 0
    for pair in range(pairs):
        first = max(0, 2 * pair + 1 - band)
        last = min(slots + slots % 2, 2 * pair + 2)
        while waited < min(last, slots):
            row_copy(source_refs[0], 0, waited).wait()
            waited += 1
        span = (last - first) * depth
        left = left_ref[:, first * depth : last * depth]
        right = jnp.concatenate(
            [window[2 * pair + side, first:last].reshape(span, block) for side in range(2)], 1
        )
        total = jnp.dot(left, right, preferred_element_type=jnp.float32).astype(jnp.bfloat16)
        if has_partial:
            total = total.astype(jnp.float32) + partial_ref[pair].astype(jnp.float32)
            total = total.astype(jnp.bfloat16)
            for row in range(rows_out):
                for side in range(2):
                    offset = 2 * pair + side - row
                    if 0 <= offset < 2 * band - 1:
                        result[row, offset] = total[
                            row * block : (row + 1) * block, side * block : (side + 1) * block
                        ]
        else:
            result[pair] = total
    copy = pltpu.make_async_copy(result, out_ref, out_sem)
    copy.start()
    copy.wait()


def half_product(left, sources, where, partial, rows_out, band):
    depth, block = sources[0].shape[2:]
    slots = rows_out + band - 1
    columns = slots + band - 1
    pairs = (columns + 1) // 2
    plan = {"sources": len(sources), "where": where, "slots": slots, "band": band}
    has_partial = partial is not None
    if has_partial:
        out_shape = (rows_out, 2 * band - 1, block, block)
    else:
        out_shape = (pairs, rows_out * block, 2 * block)
    in_specs = [pl.BlockSpec(memory_space=pltpu.VMEM)]
    in_specs += [pl.BlockSpec(memory_space=pl.ANY)] * len(sources)
    operands = [left, *sources]
    if has_partial:
        in_specs.append(pl.BlockSpec(memory_space=pltpu.VMEM))
        operands.append(partial)
    window_slots = slots + slots % 2
    flops = 2 * rows_out * block * depth * slots * band * block
    return pl.pallas_call(
        functools.partial(product_kernel, depth, rows_out, plan, has_partial),
        out_shape=jax.ShapeDtypeStruct(out_shape, jnp.bfloat16),
        in_specs=in_specs,
        out_specs=pl.BlockSpec(memory_space=pl.ANY),
        scratch_shapes=[
            pltpu.VMEM((2 * pairs, window_slots, depth, block), jnp.bfloat16),
            pltpu.VMEM(out_shape, jnp.bfloat16),
            pltpu.SemaphoreType.DMA((slots,)),
            pltpu.SemaphoreType.DMA,
        ],
        compiler_params=pltpu.CompilerParams(vmem_limit_bytes=40 * 2**20),
        cost_estimate=pl.CostEstimate(
            flops=flops, bytes_accessed=12 * 2**20, transcendentals=0
        ),
    )(*operands)


def stacked_left(a_rows):
    rows_out, band, depth, block = a_rows.shape
    slots = rows_out + band - 1
    turned = jnp.transpose(a_rows, (0, 3, 1, 2)).reshape(rows_out, block, band * depth)
    total = (slots + slots % 2) * depth
    lines = [
        jnp.pad(turned[i], ((0, 0), (i * depth, total - (i + band) * depth)))
        for i in range(rows_out)
    ]
    return jnp.concatenate(lines, 0)


def local(a_blocks, b_blocks, a_extent, b_extent):
    rows, band, depth, block = a_blocks.shape
    ring = lax.axis_size("row") * lax.axis_size("col")
    rows_out = rows // lax.axis_size("rep")
    rep = lax.axis_index("rep")
    chunks = rows // CHUNK_ROWS

    b_own = b_blocks * band_live(b_extent, band)[:, :, None, None]
    a_own = a_blocks * band_live(a_extent, band)[:, :, None, None]
    a_keep = lax.dynamic_slice_in_dim(a_own, rows_out * rep, rows_out, 0)
    a_send = lax.dynamic_slice_in_dim(a_own, rows_out * (1 - rep), rows_out, 0)

    def start_for(side, index):
        return jnp.where(side == 0, rows - (index + 1) * CHUNK_ROWS, index * CHUNK_ROWS)

    peer = to_chip_peer(b_own, ring)
    outer = to_outer_neighbour(b_own, ring)
    across = [
        over_rep(lax.dynamic_slice_in_dim(b_own, start_for(1 - rep, i), CHUNK_ROWS, 0))
        for i in range(chunks)
    ]
    across_outer = [to_outer_neighbour(x, ring) for x in across]
    across_peer = [to_chip_peer(x, ring) for x in across]
    a_across = over_rep(a_send)
    extra = to_second_neighbour(
        lax.dynamic_slice_in_dim(outer, start_for(rep, 0), EXTRA_ROWS, 0), ring
    )
    across_extra = to_second_neighbour(across_outer[0], ring)

    def window_rows(rep_value, core_value):
        left, right = ("outer", "peer") if core_value == 0 else ("peer", "outer")
        line = [("extra", i) for i in range(EXTRA_ROWS)] if rep_value == 0 else []
        first = 0 if rep_value == 0 else rows_out - EXTRA_ROWS
        line += [(left, i) for i in range(first, rows)]
        line += [("own", i) for i in range(rows)]
        line += [(right, i) for i in range(rows)]
        if rep_value == 0:
            line = line[: rows_out + band - 1]
        else:
            line += [("extra", i) for i in range(EXTRA_ROWS)]
        return line

    def where_near(rep_value, core_value):
        index = {"own": 0, "peer": 1, "outer": 2, "extra": 3}
        return [(index[kind], i) for kind, i in window_rows(rep_value, core_value)]

    def where_far(rep_value, core_value):
        index = {"own": 0, "peer": chunks, "outer": 2 * chunks}
        found = []
        for kind, i in window_rows(rep_value, core_value):
            if kind == "extra":
                found.append((3 * chunks, i))
            else:
                chunk = i // CHUNK_ROWS
                chunk = chunks - 1 - chunk if rep_value == 0 else chunk
                found.append((index[kind] + chunk, i % CHUNK_ROWS))
        return found

    near = half_product(
        stacked_left(a_keep), [b_own, peer, outer, extra], where_near, None, rows_out, band
    )
    far_sources = [*across, *across_peer, *across_outer, across_extra]
    return half_product(stacked_left(a_across), far_sources, where_far, near, rows_out, band)


def solution(mesh):
    return jax.shard_map(
        local,
        mesh=mesh,
        in_specs=(
            P(("row", "col"), None, "rep", None),
            P(("row", "col"), None, "rep", None),
            P(("row", "col")),
            P(("row", "col")),
        ),
        out_specs=P(("row", "col", "rep"), None, None, None),
        check_vma=False,
    )
```

time: 446 us -> 102 us (0.23)
  the two profiles are of different devices: /device:TPU:0 before, /device:TPU:1 now
where the time goes in v1:
time: 102 us
  waiting for transfers between devices  43.6 us (43%)
  local copies, waits for them, and re-layouts  19.6 us (19%)
  starting transfers between devices  16.6 us (16%)
  Pallas kernels  15.7 us (15%)
  other arithmetic  6.38 us (6%)
    ppermute x4, waiting for transfers between devices, to_outer_neighbour(): lax.ppermute(x, RING, [(g, (g + 2 * (g % 2) - 1) % ring) for g in range(r...  30.8 us
    pallas_call x2, Pallas kernels, half_product(): pl.pallas_call(functools.partial(product_kernel, depth, rows_out, plan, h...  15.7 us
    ppermute x4, waiting for transfers between devices, over_rep(): return lax.ppermute(x, 'rep', [(0, 1), (1, 0)])  12.8 us
    squeeze x6, local copies, waits for them, and re-layouts, stacked_left(): turned[i]  10.4 us
    ppermute x4, starting transfers between devices, to_outer_neighbour(): lax.ppermute(x, RING, [(g, (g + 2 * (g % 2) - 1) % ring) for g in range(r...  5.1 us
    ppermute x4, starting transfers between devices, to_chip_peer(): return lax.ppermute(x, RING, [(g, g ^ 1) for g in range(ring)])  4.41 us
    slice x2, local copies, waits for them, and re-layouts, stacked_left(): turned[i]  4.17 us
    ppermute x4, starting transfers between devices, over_rep(): return lax.ppermute(x, 'rep', [(0, 1), (1, 0)])  3.89 us
  transfers between devices with their start and end apart: 14, of which 5 were waited for; matrix products, arithmetic and copies ran while one was open for 23% of the time, Pallas kernels for 7%

profile of v1, /device:TPU:1, one launch (start us, length us, event | category | flops | bytes accessed | tf_op | source)
XLA Modules:
  0.0 102.0 jit_solution(6942898026001113115)
XLA Ops:
  0.7 1.6 %broadcast_multiply_fusion.refs_1_ = bf16[6,17,64,128]{3,2,1,0:T(8,128)(2,1)S(1)} fusion(bf16[6,17,64,128]{3,2,1,0:T(8,128)(2,1)} %param.5, bf16[6,17]{1,0:T(8,128)(2,1)S(1)} %get-tuple-element.16), kind=kLoop, calls=%fused_computation.16 | loop fusion | flops 835584 | bytes 3342540 | tf_op jit(solution)/shard_map/mul | solution.py:165
  2.4 2.7 %collective-permute-start.12 = (bf16[6,17,64,128]{3,2,1,0:T(8,128)(2,1)S(1)}, bf16[6,17,64,128]{3,2,1,0:T(8,128)(2,1)S(1)}, u32[]{:S(2)}, u32[]{:S(2)}) collective-permute-start(bf16[6,17,64,128]{3,2,1,0:T(8,128)(2,1)S(1)} %broadcast_multiply_fusion.refs_1_), channel_id=1, source_target_pairs={{0,30},{2,4},{4,2},{6,8},{8,6},{10,12},{12,10},{14,16},{16,14},{18... | collective-permute-start | bytes 5013512 | tf_op jit(solution)/shard_map/ppermute | solution.py:27
  5.1 2.9 %collective-permute-start.11 = (bf16[6,17,64,128]{3,2,1,0:T(8,128)(2,1)S(1)}, bf16[6,17,64,128]{3,2,1,0:T(8,128)(2,1)}, u32[]{:S(2)}, u32[]{:S(2)}) collective-permute-start(bf16[6,17,64,128]{3,2,1,0:T(8,128)(2,1)S(1)} %broadcast_multiply_fusion.refs_1_), channel_id=1, source_target_pairs={{0,2},{2,0},{4,6},{6,4},{8,10},{10,8},{12,14},{14,12},{16,18},{18,... | collective-permute-start | bytes 5013512 | tf_op jit(solution)/shard_map/ppermute | solution.py:23
  7.9 1.2 %constant_dynamic-slice_fusion.1 = (bf16[2,17,64,128]{3,2,1,0:T(8,128)(2,1)}, bf16[2,17,64,128]{3,2,1,0:T(8,128)(2,1)}, bf16[2,17,64,128]{3,2,1,0:T(8,128)(2,1)}) fusion(bf16[6,17,64,128]{3,2,1,0:T(8,128)(2,1)S(1)} %broadcast_multiply_fusion.refs_1_, s32[]{:T(128)S(6)} %select_n.23, s32[]{:T(128)S(6)} %select_n.22), kind=kLoop, calls=%fused_computation.21 | loop fusion | bytes 3342344 | tf_op jit(solution)/shard_map/dynamic_slice | solution.py:176
  11.8 1.4 %broadcast_multiply_fusion.1 = bf16[6,17,64,128]{3,2,1,0:T(8,128)(2,1)} fusion(bf16[6,17,64,128]{3,2,1,0:T(8,128)(2,1)S(1)} %copy-done.2, bf16[6,17]{1,0:T(8,128)(2,1)S(1)} %get-tuple-element.17), kind=kLoop, calls=%fused_computation.17 | loop fusion | flops 835584 | bytes 3342540 | tf_op jit(solution)/shard_map/mul | solution.py:166
  13.2 2.7 %dynamic-slice_bitcast_fusion = (bf16[3,128,17,64]{1,3,2,0:T(8,128)(2,1)}, bf16[3,17,64,128]{3,2,1,0:T(8,128)(2,1)}) fusion(bf16[6,17,64,128]{3,2,1,0:T(8,128)(2,1)} %broadcast_multiply_fusion.1, s32[]{:T(128)S(6)} %select_n.24, s32[]{:T(128)S(6)} %select_n.21), kind=kLoop, calls=%fused_computation.15 | loop fusion | bytes 3342344 | tf_op jit(solution)/shard_map/transpose | solution.py:149
  15.9 7.8 %collective-permute-done.1.refs_1_ = bf16[2,17,64,128]{3,2,1,0:T(8,128)(2,1)} collective-permute-done((bf16[2,17,64,128]{3,2,1,0:T(8,128)(2,1)}, bf16[2,17,64,128]{3,2,1,0:T(8,128)(2,1)}, u32[]{:S(2)}, u32[]{:S(2)}) %collective-permute-start.1) | collective-permute-done | bytes 557088 | tf_op jit(solution)/shard_map/ppermute | solution.py:40
  25.0 23.5 %collective-permute-done.12.refs_3_ = bf16[6,17,64,128]{3,2,1,0:T(8,128)(2,1)S(1)} collective-permute-done((bf16[6,17,64,128]{3,2,1,0:T(8,128)(2,1)S(1)}, bf16[6,17,64,128]{3,2,1,0:T(8,128)(2,1)S(1)}, u32[]{:S(2)}, u32[]{:S(2)}) %collective-permute-start.12) | collective-permute-done | bytes 1671200 | tf_op jit(solution)/shard_map/ppermute | solution.py:27
  48.5 1.3 %collective-permute-start.7 = (bf16[2,17,64,128]{3,2,1,0:T(8,128)(2,1)}, bf16[2,17,64,128]{3,2,1,0:T(8,128)(2,1)}, u32[]{:S(2)}, u32[]{:S(2)}) collective-permute-start(bf16[2,17,64,128]{3,2,1,0:T(8,128)(2,1)} %collective-permute-done.1.refs_1_), channel_id=1, source_target_pairs={{0,30},{2,4},{4,2},{6,8},{8,6},{10,12},{12,10},{14,16},{16,14},{18... | collective-permute-start | bytes 1671176 | tf_op jit(solution)/shard_map/ppermute | solution.py:27
  50.7 1.7 %collective-permute-start.13 = (bf16[2,17,64,128]{3,2,1,0:T(8,128)(2,1)}, bf16[2,17,64,128]{3,2,1,0:T(8,128)(2,1)}, u32[]{:S(2)}, u32[]{:S(2)}) collective-permute-start(bf16[2,17,64,128]{3,2,1,0:T(8,128)(2,1)} %constant_dynamic-slice_fusion), channel_id=1, source_target_pairs={{0,2},{1,27},{2,8},{3,1},{4,6},{5,31},{6,12},{7,5},{8,10},{9,3},{1... | collective-permute-start | bytes 1671176 | tf_op jit(solution)/shard_map/ppermute | solution.py:36
  52.4 2.1 %fusion.11 = (bf16[1,128,17,64]{1,3,2,0:T(8,128)(2,1)}, bf16[1,128,17,64]{1,3,2,0:T(8,128)(2,1)}, bf16[1,128,17,64]{1,3,2,0:T(8,128)(2,1)}) fusion(bf16[3,128,17,64]{1,3,2,0:T(8,128)(2,1)} %get-tuple-element.5), kind=kLoop, calls=%fused_computation.25 | loop fusion | bytes 1671168 | tf_op jit(solution)/shard_map/slice | solution.py:152
  54.5 1.9 %copy.14 = bf16[128,1088]{1,0:T(8,128)(2,1)} copy(bf16[128,1088]{0,1:T(8,128)(2,1)} %bitcast.13) | data formatting | bytes 557056 | tf_op jit(solution)/shard_map/squeeze | solution.py:152
  56.4 1.8 %copy.15 = bf16[128,1088]{1,0:T(8,128)(2,1)} copy(bf16[128,1088]{0,1:T(8,128)(2,1)} %bitcast.11) | data formatting | bytes 557056 | tf_op jit(solution)/shard_map/squeeze | solution.py:152
  60.6 4.9 %collective-permute-done = bf16[3,17,64,128]{3,2,1,0:T(8,128)(2,1)} collective-permute-done((bf16[3,17,64,128]{3,2,1,0:T(8,128)(2,1)}, bf16[3,17,64,128]{3,2,1,0:T(8,128)(2,1)}, u32[]{:S(2)}, u32[]{:S(2)}) %collective-permute-start) | collective-permute-done | bytes 835616 | tf_op jit(solution)/shard_map/ppermute | solution.py:40
  68.1 1.5 %collective-permute-start.10 = (bf16[2,17,64,128]{3,2,1,0:T(8,128)(2,1)}, bf16[2,17,64,128]{3,2,1,0:T(8,128)(2,1)}, u32[]{:S(2)}, u32[]{:S(2)}) collective-permute-start(bf16[2,17,64,128]{3,2,1,0:T(8,128)(2,1)} %collective-permute-done.7.refs_7_), channel_id=1, source_target_pairs={{0,2},{1,27},{2,8},{3,1},{4,6},{5,31},{6,12},{7,5},{8,10},{9,3},{1... | collective-permute-start | bytes 1671176 | tf_op jit(solution)/shard_map/ppermute | solution.py:36
  69.6 2.1 %fusion.12 = (bf16[1,128,17,64]{1,3,2,0:T(8,128)(2,1)}, bf16[1,128,17,64]{1,3,2,0:T(8,128)(2,1)}, bf16[1,128,17,64]{1,3,2,0:T(8,128)(2,1)}) fusion(bf16[3,128,17,64]{1,3,2,0:T(8,128)(2,1)} %bitcast), kind=kLoop, calls=%fused_computation.26 | loop fusion | bytes 1671168 | tf_op jit(solution)/shard_map/slice | solution.py:152
  71.7 1.9 %copy.11 = bf16[128,1088]{1,0:T(8,128)(2,1)} copy(bf16[128,1088]{0,1:T(8,128)(2,1)} %bitcast.14) | data formatting | bytes 557056 | tf_op jit(solution)/shard_map/squeeze | solution.py:152
  73.6 1.8 %copy.12 = bf16[128,1088]{1,0:T(8,128)(2,1)} copy(bf16[128,1088]{0,1:T(8,128)(2,1)} %bitcast.12) | data formatting | bytes 557056 | tf_op jit(solution)/shard_map/squeeze | solution.py:152
  75.4 1.9 %copy.13 = bf16[128,1088]{1,0:T(8,128)(2,1)} copy(bf16[128,1088]{0,1:T(8,128)(2,1)} %bitcast.10) | data formatting | bytes 557056 | tf_op jit(solution)/shard_map/squeeze | solution.py:152
  77.3 1.4 %fusion.8.refs_0_ = bf16[384,1280]{1,0:T(8,128)(2,1)S(1)} fusion(bf16[128,1088]{1,0:T(8,128)(2,1)} %copy.13, bf16[128,1088]{1,0:T(8,128)(2,1)} %copy.12, bf16[128,1088]{1,0:T(8,128)(2,1)} %copy.11), kind=kLoop, calls=%fused_computation.12 | loop fusion | flops 6881280 | bytes 1818624 | tf_op jit(solution)/shard_map/concatenate | solution.py:155
  79.0 7.2 %shard_map.46.refs_11_ = bf16[18,384,256]{2,1,0:T(8,128)(2,1)S(1)} custom-call(bf16[384,1280]{1,0:T(8,128)(2,1)S(1)} %fusion.10.refs_0_, bf16[6,17,64,128]{3,2,1,0:T(8,128)(2,1)S(1)} %broadcast_multiply_fusion.refs_1_, bf16[6,17,64,128]{3,2,1,0:T(8,128)(2,1)} %collective-permute-done.11.refs_2_, bf16[6,17,64,128]{3,2,1,0:T(8,128)(2,1)S(1)} %copy-done.1, ...), custom_call_target="tpu_custom_call" | custom-call | flops 2032140288 | bytes 12582912 | tf_op jit(solution)/shard_map/pallas_call | solution.py:128
  86.2 1.3 %collective-permute-done.8.refs_8_ = bf16[2,17,64,128]{3,2,1,0:T(8,128)(2,1)} collective-permute-done((bf16[2,17,64,128]{3,2,1,0:T(8,128)(2,1)}, bf16[2,17,64,128]{3,2,1,0:T(8,128)(2,1)}, u32[]{:S(2)}, u32[]{:S(2)}) %collective-permute-start.8) | collective-permute-done | bytes 557088 | tf_op jit(solution)/shard_map/ppermute | solution.py:27
  87.5 5.9 %collective-permute-done.9.refs_9_ = bf16[2,17,64,128]{3,2,1,0:T(8,128)(2,1)} collective-permute-done((bf16[2,17,64,128]{3,2,1,0:T(8,128)(2,1)}, bf16[2,17,64,128]{3,2,1,0:T(8,128)(2,1)}, u32[]{:S(2)}, u32[]{:S(2)}) %collective-permute-start.9) | collective-permute-done | bytes 557088 | tf_op jit(solution)/shard_map/ppermute | solution.py:27
  93.5 8.5 %shard_map.47 = bf16[3,33,128,128]{3,2,1,0:T(8,128)(2,1)} custom-call(bf16[384,1280]{1,0:T(8,128)(2,1)S(1)} %fusion.8.refs_0_, bf16[2,17,64,128]{3,2,1,0:T(8,128)(2,1)} %collective-permute-done.1.refs_1_, bf16[2,17,64,128]{3,2,1,0:T(8,128)(2,1)} %collective-permute-done.2.refs_2_, bf16[2,17,64,128]{3,2,1,0:T(8,128)(2,1)} %collective-permute-done.3.refs_3_, ...), custom_call_target="tpu_custom_call" | custom-call | flops 2032140288 | bytes 12582912 | tf_op jit(solution)/shard_map/pallas_call | solution.py:128
  (29 shorter events, 10.8 us)
Async XLA Ops:
  2.4 46.1 %collective-permute-start.12 = (bf16[6,17,64,128]{3,2,1,0:T(8,128)(2,1)S(1)}, bf16[6,17,64,128]{3,2,1,0:T(8,128)(2,1)S(1)}, u32[]{:S(2)}, u32[]{:S(2)}) collective-permute-start(bf16[6,17,64,128]{3,2,1,0:T(8,128)(2,1)S(1)} %broadcast_multiply_fusion.refs_1_), channel_id=1, source_target_pairs={{0,30},{2,4},{4,2},{6,8},{8,6},{10,12},{12,10},{14,16},{16,14},{18... | collective-permute-start | bytes 5013512 | tf_op jit(solution)/shard_map/ppermute | solution.py:27
  5.1 62.0 %collective-permute-start.11 = (bf16[6,17,64,128]{3,2,1,0:T(8,128)(2,1)S(1)}, bf16[6,17,64,128]{3,2,1,0:T(8,128)(2,1)}, u32[]{:S(2)}, u32[]{:S(2)}) collective-permute-start(bf16[6,17,64,128]{3,2,1,0:T(8,128)(2,1)S(1)} %broadcast_multiply_fusion.refs_1_), channel_id=1, source_target_pairs={{0,2},{2,0},{4,6},{6,4},{8,10},{10,8},{12,14},{14,12},{16,18},{18,... | collective-permute-start | bytes 5013512 | tf_op jit(solution)/shard_map/ppermute | solution.py:23
  7.9 3.9 %copy-start.2 = (bf16[6,17,64,128]{3,2,1,0:T(8,128)(2,1)S(1)}, bf16[6,17,64,128]{3,2,1,0:T(8,128)(2,1)}, u32[]{:S(2)}) copy-start(bf16[6,17,64,128]{3,2,1,0:T(8,128)(2,1)} %param.4) | copy-start | bytes 5013508
  9.2 14.6 %collective-permute-start.1 = (bf16[2,17,64,128]{3,2,1,0:T(8,128)(2,1)}, bf16[2,17,64,128]{3,2,1,0:T(8,128)(2,1)}, u32[]{:S(2)}, u32[]{:S(2)}) collective-permute-start(bf16[2,17,64,128]{3,2,1,0:T(8,128)(2,1)} %get-tuple-element.9), channel_id=1, source_target_pairs={{0,1},{1,0},{2,3},{3,2},{4,5},{5,4},{6,7},{7,6},{8,9},{9,8},{10,11... | collective-permute-start | bytes 1671176 | tf_op jit(solution)/shard_map/ppermute | solution.py:40
  10.4 40.3 %collective-permute-start.2 = (bf16[2,17,64,128]{3,2,1,0:T(8,128)(2,1)}, bf16[2,17,64,128]{3,2,1,0:T(8,128)(2,1)}, u32[]{:S(2)}, u32[]{:S(2)}) collective-permute-start(bf16[2,17,64,128]{3,2,1,0:T(8,128)(2,1)} %get-tuple-element.8), channel_id=1, source_target_pairs={{0,1},{1,0},{2,3},{3,2},{4,5},{5,4},{6,7},{7,6},{8,9},{9,8},{10,11... | collective-permute-start | bytes 1671176 | tf_op jit(solution)/shard_map/ppermute | solution.py:40
  10.6 40.1 %collective-permute-start.3 = (bf16[2,17,64,128]{3,2,1,0:T(8,128)(2,1)}, bf16[2,17,64,128]{3,2,1,0:T(8,128)(2,1)}, u32[]{:S(2)}, u32[]{:S(2)}) collective-permute-start(bf16[2,17,64,128]{3,2,1,0:T(8,128)(2,1)} %get-tuple-element.7), channel_id=1, source_target_pairs={{0,1},{1,0},{2,3},{3,2},{4,5},{5,4},{6,7},{7,6},{8,9},{9,8},{10,11... | collective-permute-start | bytes 1671176 | tf_op jit(solution)/shard_map/ppermute | solution.py:40
  23.7 41.8 %collective-permute-start = (bf16[3,17,64,128]{3,2,1,0:T(8,128)(2,1)}, bf16[3,17,64,128]{3,2,1,0:T(8,128)(2,1)}, u32[]{:S(2)}, u32[]{:S(2)}) collective-permute-start(bf16[3,17,64,128]{3,2,1,0:T(8,128)(2,1)} %get-tuple-element.6), channel_id=1, source_target_pairs={{0,1},{1,0},{2,3},{3,2},{4,5},{5,4},{6,7},{7,6},{8,9},{9,8},{10,11... | collective-permute-start | bytes 2506760 | tf_op jit(solution)/shard_map/ppermute | solution.py:40
  48.5 9.7 %copy-start = (bf16[6,17,64,128]{3,2,1,0:T(8,128)(2,1)}, bf16[6,17,64,128]{3,2,1,0:T(8,128)(2,1)S(1)}, u32[]{:S(2)}) copy-start(bf16[6,17,64,128]{3,2,1,0:T(8,128)(2,1)S(1)} %collective-permute-done.12.refs_3_) | copy-start | bytes 5013508
  48.5 17.8 %collective-permute-start.7 = (bf16[2,17,64,128]{3,2,1,0:T(8,128)(2,1)}, bf16[2,17,64,128]{3,2,1,0:T(8,128)(2,1)}, u32[]{:S(2)}, u32[]{:S(2)}) collective-permute-start(bf16[2,17,64,128]{3,2,1,0:T(8,128)(2,1)} %collective-permute-done.1.refs_1_), channel_id=1, source_target_pairs={{0,30},{2,4},{4,2},{6,8},{8,6},{10,12},{12,10},{14,16},{16,14},{18... | collective-permute-start | bytes 1671176 | tf_op jit(solution)/shard_map/ppermute | solution.py:27
  50.7 15.6 %collective-permute-start.4 = (bf16[2,17,64,128]{3,2,1,0:T(8,128)(2,1)}, bf16[2,17,64,128]{3,2,1,0:T(8,128)(2,1)}, u32[]{:S(2)}, u32[]{:S(2)}) collective-permute-start(bf16[2,17,64,128]{3,2,1,0:T(8,128)(2,1)} %collective-permute-done.1.refs_1_), channel_id=1, source_target_pairs={{0,2},{2,0},{4,6},{6,4},{8,10},{10,8},{12,14},{14,12},{16,18},{18,... | collective-permute-start | bytes 1671176 | tf_op jit(solution)/shard_map/ppermute | solution.py:23
  50.7 17.4 %collective-permute-start.13 = (bf16[2,17,64,128]{3,2,1,0:T(8,128)(2,1)}, bf16[2,17,64,128]{3,2,1,0:T(8,128)(2,1)}, u32[]{:S(2)}, u32[]{:S(2)}) collective-permute-start(bf16[2,17,64,128]{3,2,1,0:T(8,128)(2,1)} %constant_dynamic-slice_fusion), channel_id=1, source_target_pairs={{0,2},{1,27},{2,8},{3,1},{4,6},{5,31},{6,12},{7,5},{8,10},{9,3},{1... | collective-permute-start | bytes 1671176 | tf_op jit(solution)/shard_map/ppermute | solution.py:36
  65.5 20.7 %collective-permute-start.5 = (bf16[2,17,64,128]{3,2,1,0:T(8,128)(2,1)}, bf16[2,17,64,128]{3,2,1,0:T(8,128)(2,1)S(1)}, u32[]{:S(2)}, u32[]{:S(2)}) collective-permute-start(bf16[2,17,64,128]{3,2,1,0:T(8,128)(2,1)} %collective-permute-done.2.refs_2_), channel_id=1, source_target_pairs={{0,2},{2,0},{4,6},{6,4},{8,10},{10,8},{12,14},{14,12},{16,18},{18,... | collective-permute-start | bytes 1671176 | tf_op jit(solution)/shard_map/ppermute | solution.py:23
  66.3 21.2 %collective-permute-start.8 = (bf16[2,17,64,128]{3,2,1,0:T(8,128)(2,1)}, bf16[2,17,64,128]{3,2,1,0:T(8,128)(2,1)}, u32[]{:S(2)}, u32[]{:S(2)}) collective-permute-start(bf16[2,17,64,128]{3,2,1,0:T(8,128)(2,1)} %collective-permute-done.2.refs_2_), channel_id=1, source_target_pairs={{0,30},{2,4},{4,2},{6,8},{8,6},{10,12},{12,10},{14,16},{16,14},{18... | collective-permute-start | bytes 1671176 | tf_op jit(solution)/shard_map/ppermute | solution.py:27
  66.3 19.9 %collective-permute-start.6 = (bf16[2,17,64,128]{3,2,1,0:T(8,128)(2,1)}, bf16[2,17,64,128]{3,2,1,0:T(8,128)(2,1)}, u32[]{:S(2)}, u32[]{:S(2)}) collective-permute-start(bf16[2,17,64,128]{3,2,1,0:T(8,128)(2,1)} %collective-permute-done.3.refs_3_), channel_id=1, source_target_pairs={{0,2},{2,0},{4,6},{6,4},{8,10},{10,8},{12,14},{14,12},{16,18},{18,... | collective-permute-start | bytes 1671176 | tf_op jit(solution)/shard_map/ppermute | solution.py:23
  67.1 26.4 %collective-permute-start.9 = (bf16[2,17,64,128]{3,2,1,0:T(8,128)(2,1)}, bf16[2,17,64,128]{3,2,1,0:T(8,128)(2,1)}, u32[]{:S(2)}, u32[]{:S(2)}) collective-permute-start(bf16[2,17,64,128]{3,2,1,0:T(8,128)(2,1)} %collective-permute-done.3.refs_3_), channel_id=1, source_target_pairs={{0,30},{2,4},{4,2},{6,8},{8,6},{10,12},{12,10},{14,16},{16,14},{18... | collective-permute-start | bytes 1671176 | tf_op jit(solution)/shard_map/ppermute | solution.py:27
  68.1 25.4 %collective-permute-start.10 = (bf16[2,17,64,128]{3,2,1,0:T(8,128)(2,1)}, bf16[2,17,64,128]{3,2,1,0:T(8,128)(2,1)}, u32[]{:S(2)}, u32[]{:S(2)}) collective-permute-start(bf16[2,17,64,128]{3,2,1,0:T(8,128)(2,1)} %collective-permute-done.7.refs_7_), channel_id=1, source_target_pairs={{0,2},{1,27},{2,8},{3,1},{4,6},{5,31},{6,12},{7,5},{8,10},{9,3},{1... | collective-permute-start | bytes 1671176 | tf_op jit(solution)/shard_map/ppermute | solution.py:36
  77.3 1.7 %copy-start.1 = (bf16[6,17,64,128]{3,2,1,0:T(8,128)(2,1)S(1)}, bf16[6,17,64,128]{3,2,1,0:T(8,128)(2,1)}, u32[]{:S(2)}) copy-start(bf16[6,17,64,128]{3,2,1,0:T(8,128)(2,1)} %copy-done) | copy-start | bytes 5013508

commit v2 on v1

v2 whole, which is shorter than its diff:
```python
import functools

import jax
import jax.numpy as jnp
from jax import lax
from jax.experimental import pallas as pl
from jax.experimental.pallas import tpu as pltpu
from jax.sharding import PartitionSpec as P

RING = ("row", "col")
EVERY = ("row", "col", "rep")
EXTRA_ROWS = 2
REST = 1


def to_chip_peer(x, ring):
    return lax.ppermute(x, RING, [(g, g ^ 1) for g in range(ring)])


def to_outer_neighbour(x, ring):
    return lax.ppermute(x, RING, [(g, (g + 2 * (g % 2) - 1) % ring) for g in range(ring)])


def to_second_neighbour(x, ring):
    pairs = []
    for g in range(ring):
        owner = g + 1 if g % 2 else g - 1
        pairs.append((2 * g, 2 * ((owner + 2) % ring)))
        pairs.append((2 * g + 1, 2 * ((owner - 2) % ring) + 1))
    return lax.ppermute(x, EVERY, pairs)


def over_rep(x):
    return lax.ppermute(x, "rep", [(0, 1), (1, 0)])


def turn_kernel(rows_out, extent_ref, a_ref, out_ref):
    rows, band, depth, block = a_ref.shape
    half_band = (band - 1) // 2
    squares = out_ref.shape[2] // (2 * depth)
    blank = jnp.zeros((depth, block), a_ref.dtype)
    for row in range(rows):
        shift = (row % rows_out) % 2
        extent = extent_ref[row]

        def piece(offset):
            if not 0 <= offset < band:
                return blank
            return jnp.where(abs(offset - half_band) <= extent, a_ref[row, offset], blank)

        for square in range(squares):
            offset = 2 * square - shift
            both = jnp.concatenate([piece(offset), piece(offset + 1)], 0)
            out_ref[row, :, square * 2 * depth : (square + 1) * 2 * depth] = both.T


def turned_left(a_blocks, a_extent, rows_out):
    rows, band, depth, block = a_blocks.shape
    return pl.pallas_call(
        functools.partial(turn_kernel, rows_out),
        out_shape=jax.ShapeDtypeStruct((rows, block, (band + 1) * depth), a_blocks.dtype),
        in_specs=[
            pl.BlockSpec(memory_space=pltpu.SMEM),
            pl.BlockSpec(memory_space=pltpu.VMEM),
        ],
        out_specs=pl.BlockSpec(memory_space=pltpu.VMEM),
        cost_estimate=pl.CostEstimate(
            flops=0, bytes_accessed=8 * a_blocks.size, transcendentals=0
        ),
    )(a_extent, a_blocks)


def product_kernel(plan, *refs):
    refs = list(refs)
    turned_ref = refs.pop(0)
    source_refs = [refs.pop(0) for _ in range(plan["sources"])]
    has_partial = plan["partial"]
    partial_ref = refs.pop(0) if has_partial else None
    out_ref, left, window, result, left_sem, row_sem, out_sem = refs[:7]
    if has_partial:
        partial, partial_sem = refs[7:]
    slots, band, rows_out, depth = plan["slots"], plan["band"], plan["rows_out"], plan["depth"]
    block = window.shape[-1]
    pairs = window.shape[0] // 2
    rep = lax.axis_index("rep")
    core = lax.rem(lax.axis_index("col"), 2)
    first_row = rows_out * rep if plan["own_left"] else 0
    reach = (band + 1) * depth

    def left_copy(row):
        at = (row - row % 2) * depth
        return pltpu.make_async_copy(
            turned_ref.at[first_row + row],
            left.at[pl.ds(row * block, block), pl.ds(at, reach)],
            left_sem.at[row],
        )

    def row_copy(source, position, slot):
        return pltpu.make_async_copy(
            source.at[position], window.at[pl.ds(slot, band), slot], row_sem.at[slot]
        )

    def partial_copy(pair):
        return pltpu.make_async_copy(
            partial_ref.at[pair], partial.at[pair], partial_sem.at[pair]
        )

    def out_copy(pair):
        if has_partial:
            low = max(0, 2 * pair - rows_out + 1)
            high = min(2 * pair - rows_out + 3, 2 * band - 1)
            return pltpu.make_async_copy(
                result.at[:, pl.ds(low, high - low)],
                out_ref.at[:, pl.ds(low, high - low)],
                out_sem.at[pair],
            )
        return pltpu.make_async_copy(result.at[pair], out_ref.at[pair], out_sem.at[pair])

    for row in range(rows_out):
        left_copy(row).start()
    for rep_value in range(2):
        for core_value in range(2):

            @pl.when((rep == rep_value) & (core == core_value))
            def _(rep_value=rep_value, core_value=core_value):
                for slot, (source, position) in enumerate(plan["where"](rep_value, core_value)):
                    row_copy(source_refs[source], position, slot).start()

    if has_partial:
        for pair in range(pairs):
            partial_copy(pair).start()

    width = left.shape[1]
    for row in range(rows_out):
        at = (row - row % 2) * depth
        if at:
            left[row * block : (row + 1) * block, :at] = jnp.zeros((block, at), left.dtype)
        if at + reach < width:
            rest = width - at - reach
            left[row * block : (row + 1) * block, at + reach :] = jnp.zeros(
                (block, rest), left.dtype
            )
    blank = jnp.zeros((depth, block), window.dtype)
    for pair in range(pairs):
        if 2 * pair + 1 < slots:
            window[2 * pair, 2 * pair + 1] = blank
        if 0 <= 2 * pair + 1 - band < slots:
            window[2 * pair + 1, 2 * pair + 1 - band] = blank
        if slots % 2 and slots <= 2 * pair + 1:
            window[2 * pair, slots] = blank
            window[2 * pair + 1, slots] = blank
    for row in range(rows_out):
        left_copy(row).wait()

    waited = 0
    for pair in range(pairs):
        first = max(0, 2 * pair + 1 - band)
        last = min(slots + slots % 2, 2 * pair + 2)
        while waited < min(last, slots):
            row_copy(source_refs[0], 0, waited).wait()
            waited += 1
        span = (last - first) * depth
        right = jnp.concatenate(
            [window[2 * pair + side, first:last].reshape(span, block) for side in range(2)], 1
        )
        total = jnp.dot(
            left[:, first * depth : last * depth], right, preferred_element_type=jnp.float32
        ).astype(jnp.bfloat16)
        if has_partial:
            partial_copy(pair).wait()
            total = total.astype(jnp.float32) + partial[pair].astype(jnp.float32)
            total = total.astype(jnp.bfloat16)
            for row in range(rows_out):
                for side in range(2):
                    offset = 2 * pair + side - row
                    if 0 <= offset < 2 * band - 1:
                        result[row, offset] = total[
                            row * block : (row + 1) * block, side * block : (side + 1) * block
                        ]
        else:
            result[pair] = total
        if pair >= plan["first_out"]:
            out_copy(pair).start()
    for pair in range(plan["first_out"], pairs):
        out_copy(pair).wait()


def half_product(turned, sources, where, partial, rows_out, own_left):
    band, depth, block = sources[0].shape[1:]
    slots = rows_out + band - 1
    columns = slots + band - 1
    pairs = (columns + 1) // 2
    has_partial = partial is not None
    plan = {
        "sources": len(sources),
        "where": where,
        "slots": slots,
        "band": band,
        "rows_out": rows_out,
        "depth": depth,
        "own_left": own_left,
        "partial": has_partial,
        "first_out": (rows_out - 1) // 2 if has_partial else 0,
    }
    operands = [turned, *sources]
    pair_shape = (pairs, rows_out * block, 2 * block)
    if has_partial:
        out_shape = (rows_out, 2 * band - 1, block, block)
        operands.append(partial)
    else:
        out_shape = pair_shape
    window_slots = slots + slots % 2
    scratch = [
        pltpu.VMEM((rows_out * block, window_slots * depth), jnp.bfloat16),
        pltpu.VMEM((2 * pairs, window_slots, depth, block), jnp.bfloat16),
        pltpu.VMEM(out_shape, jnp.bfloat16),
        pltpu.SemaphoreType.DMA((rows_out,)),
        pltpu.SemaphoreType.DMA((slots,)),
        pltpu.SemaphoreType.DMA((pairs,)),
    ]
    if has_partial:
        scratch += [pltpu.VMEM(pair_shape, jnp.bfloat16), pltpu.SemaphoreType.DMA((pairs,))]
    return pl.pallas_call(
        functools.partial(product_kernel, plan),
        out_shape=jax.ShapeDtypeStruct(out_shape, jnp.bfloat16),
        in_specs=[pl.BlockSpec(memory_space=pl.ANY)] * len(operands),
        out_specs=pl.BlockSpec(memory_space=pl.ANY),
        scratch_shapes=scratch,
        compiler_params=pltpu.CompilerParams(vmem_limit_bytes=40 * 2**20),
        cost_estimate=pl.CostEstimate(flops=0, bytes_accessed=0, transcendentals=0),
    )(*operands)


def local(a_blocks, b_blocks, a_extent, b_extent):
    rows, band, depth, block = a_blocks.shape
    half_band = (band - 1) // 2
    ring = lax.axis_size("row") * lax.axis_size("col")
    rows_out = rows // lax.axis_size("rep")
    rep = lax.axis_index("rep")

    distance = jnp.abs(lax.broadcasted_iota(jnp.int32, b_blocks.shape, 1) - half_band)
    live = distance <= b_extent[:, None, None, None]
    b_own = b_blocks * live.astype(b_blocks.dtype)

    starts = ((rows - EXTRA_ROWS, REST, 0), (0, EXTRA_ROWS, rows - REST))
    sizes = (EXTRA_ROWS, rows - EXTRA_ROWS - REST, REST)

    def rows_for(x, side, index):
        start = jnp.where(side == 0, starts[0][index], starts[1][index])
        return lax.dynamic_slice_in_dim(x, start, sizes[index], 0)

    outer = to_outer_neighbour(b_own, ring)
    across = over_rep(b_own)
    peer = to_chip_peer(b_own, ring)
    turned = turned_left(a_blocks, a_extent, rows_out)
    turned_send = lax.dynamic_slice_in_dim(turned, rows_out * (1 - rep), rows_out, 0)
    turned_across = over_rep(turned_send)
    across = lax.optimization_barrier((across, turned_send))[0]
    across_outer = [to_outer_neighbour(rows_for(across, rep, i), ring) for i in range(2)]
    across_peer = to_chip_peer(across, ring)
    extra = to_second_neighbour(rows_for(outer, rep, 0), ring)
    across_outer.append(over_rep(rows_for(outer, 1 - rep, 2)))
    across_extra = to_second_neighbour(across_outer[0], ring)

    def window_rows(rep_value, core_value):
        left, right = ("outer", "peer") if core_value == 0 else ("peer", "outer")
        line = [("extra", i) for i in range(EXTRA_ROWS)] if rep_value == 0 else []
        first = 0 if rep_value == 0 else rows_out - EXTRA_ROWS
        line += [(left, i) for i in range(first, rows)]
        line += [("own", i) for i in range(rows)]
        line += [(right, i) for i in range(rows)]
        if rep_value == 0:
            line = line[: rows_out + band - 1]
        else:
            line += [("extra", i) for i in range(EXTRA_ROWS)]
        return line

    def where_near(rep_value, core_value):
        index = {"own": 0, "peer": 1, "outer": 2, "extra": 3}
        return [(index[kind], i) for kind, i in window_rows(rep_value, core_value)]

    def where_far(rep_value, core_value):
        found = []
        for kind, i in window_rows(rep_value, core_value):
            if kind == "outer":
                spans = zip(starts[rep_value], sizes)
                piece = [low <= i < low + size for low, size in spans].index(True)
                found.append((2 + piece, i - starts[rep_value][piece]))
            else:
                found.append(({"own": 0, "peer": 1, "extra": 5}[kind], i))
        return found

    near = half_product(
        turned, [b_own, peer, outer, extra], where_near, None, rows_out, True
    )
    far_sources = [across, across_peer, *across_outer, across_extra]
    return half_product(turned_across, far_sources, where_far, near, rows_out, False)


def solution(mesh):
    return jax.shard_map(
        local,
        mesh=mesh,
        in_specs=(
            P(("row", "col"), None, "rep", None),
            P(("row", "col"), None, "rep", None),
            P(("row", "col")),
            P(("row", "col")),
        ),
        out_specs=P(("row", "col", "rep"), None, None, None),
        check_vma=False,
    )
```

time: 102 us -> 98.1 us (0.962)
  the two profiles are of different devices: /device:TPU:1 before, /device:TPU:0 now
where the time goes in v2:
time: 98.1 us; the launch traced here: 97.7 us
  waiting for transfers between devices  39.5 us (40%)
  Pallas kernels  31 us (32%)
  starting transfers between devices  16.3 us (17%)
  local copies, waits for them, and re-layouts  9.18 us (9%)
  other arithmetic  1.65 us (2%)
    pallas_call x2, Pallas kernels, half_product(): pl.pallas_call(functools.partial(product_kernel, plan), out_shape=jax.Sha...  27.8 us
    ppermute x3, waiting for transfers between devices, over_rep(): return lax.ppermute(x, 'rep', [(0, 1), (1, 0)])  27.5 us
    ppermute x3, starting transfers between devices, to_outer_neighbour(): lax.ppermute(x, RING, [(g, (g + 2 * (g % 2) - 1) % ring) for g in range(r...  9.08 us
    dynamic_slice x4, local copies, waits for them, and re-layouts, rows_for(): return lax.dynamic_slice_in_dim(x, start, sizes[index], 0)  6.99 us
    ppermute x3, starting transfers between devices, over_rep(): return lax.ppermute(x, 'rep', [(0, 1), (1, 0)])  6.77 us
    ppermute x2, waiting for transfers between devices, to_second_neighbour(): return lax.ppermute(x, EVERY, pairs)  6.14 us
    ppermute x3, waiting for transfers between devices, to_outer_neighbour(): lax.ppermute(x, RING, [(g, (g + 2 * (g % 2) - 1) % ring) for g in range(r...  5.85 us
    pallas_call x1, Pallas kernels, turned_left(): pl.pallas_call(functools.partial(turn_kernel, rows_out), out_shape=jax.Sh...  3.18 us
  transfers between devices with their start and end apart: 10, of which 3 were waited for; matrix products, arithmetic and copies ran while one was open for 9% of the time, Pallas kernels for 17%

profile of v2, /device:TPU:0, one launch (start us, length us, event | category | flops | bytes accessed | tf_op | source)
XLA Modules:
  0.0 97.7 jit_solution(14750801615097355988)
XLA Ops:
  0.0 1.6 %compare_select_fusion.refs_1_ = bf16[6,17,64,128]{3,2,1,0:T(8,128)(2,1)S(1)} fusion(bf16[6,17,64,128]{3,2,1,0:T(8,128)(2,1)} %param.5, s32[6]{0:T(128)} %param.7, s32[17]{0:T(128)S(1)} %add_abs_fusion), kind=kLoop, calls=%fused_computation | loop fusion | flops 1671168 | bytes 3342428 | tf_op jit(solution)/shard_map/mul | solution.py:243
  1.7 3.0 %collective-permute-start.1 = (bf16[6,17,64,128]{3,2,1,0:T(8,128)(2,1)S(1)}, bf16[6,17,64,128]{3,2,1,0:T(8,128)(2,1)}, u32[]{:S(2)}, u32[]{:S(2)}) collective-permute-start(bf16[6,17,64,128]{3,2,1,0:T(8,128)(2,1)S(1)} %compare_select_fusion.refs_1_), channel_id=1, source_target_pairs={{0,1},{1,0},{2,3},{3,2},{4,5},{5,4},{6,7},{7,6},{8,9},{9,8},{10,11... | collective-permute-start | bytes 5013512 | tf_op jit(solution)/shard_map/ppermute | solution.py:34
  4.7 3.7 %collective-permute-start.5 = (bf16[6,17,64,128]{3,2,1,0:T(8,128)(2,1)S(1)}, bf16[6,17,64,128]{3,2,1,0:T(8,128)(2,1)}, u32[]{:S(2)}, u32[]{:S(2)}) collective-permute-start(bf16[6,17,64,128]{3,2,1,0:T(8,128)(2,1)S(1)} %compare_select_fusion.refs_1_), channel_id=1, source_target_pairs={{0,30},{2,4},{4,2},{6,8},{8,6},{10,12},{12,10},{14,16},{16,14},{18... | collective-permute-start | bytes 5013512 | tf_op jit(solution)/shard_map/ppermute | solution.py:21
  8.4 0.0 collective-permute-start.8
  8.4 3.2 %shard_map.46.refs_0_ = bf16[6,128,1152]{2,1,0:T(8,128)(2,1)} custom-call(s32[6]{0:T(128)} %extent_ref.1, bf16[6,17,64,128]{3,2,1,0:T(8,128)(2,1)} %a_ref.1), custom_call_target="tpu_custom_call" | custom-call | bytes 6684672 | tf_op jit(solution)/shard_map/pallas_call | solution.py:59
  11.6 2.2 %constant_dynamic-slice_fusion.4 = bf16[3,128,1152]{2,1,0:T(8,128)(2,1)} fusion(bf16[6,128,1152]{2,1,0:T(8,128)(2,1)} %shard_map.46.refs_0_, s32[]{:T(128)S(6)} %select_n.18), kind=kLoop, calls=%fused_computation.5 | loop fusion | bytes 1769476 | tf_op jit(solution)/shard_map/dynamic_slice | solution.py:256
  13.8 27.5 %collective-permute-done.1.refs_1_ = bf16[6,17,64,128]{3,2,1,0:T(8,128)(2,1)} collective-permute-done((bf16[6,17,64,128]{3,2,1,0:T(8,128)(2,1)S(1)}, bf16[6,17,64,128]{3,2,1,0:T(8,128)(2,1)}, u32[]{:S(2)}, u32[]{:S(2)}) %collective-permute-start.1) | collective-permute-done | bytes 1671200 | tf_op jit(solution)/shard_map/ppermute | solution.py:34
  41.3 0.0 collective-permute-start.2
  41.3 1.9 %constant_dynamic-slice_fusion.3 = bf16[2,17,64,128]{3,2,1,0:T(8,128)(2,1)} fusion(bf16[6,17,64,128]{3,2,1,0:T(8,128)(2,1)} %collective-permute-done.1.refs_1_, s32[]{:T(128)S(6)} %select_n.19), kind=kLoop, calls=%fused_computation.4 | loop fusion | bytes 1114116 | tf_op jit(solution)/shard_map/dynamic_slice | solution.py:250
  43.2 4.9 %collective-permute-start.3 = (bf16[2,17,64,128]{3,2,1,0:T(8,128)(2,1)}, bf16[2,17,64,128]{3,2,1,0:T(8,128)(2,1)}, u32[]{:S(2)}, u32[]{:S(2)}) collective-permute-start(bf16[2,17,64,128]{3,2,1,0:T(8,128)(2,1)} %constant_dynamic-slice_fusion.3), channel_id=1, source_target_pairs={{0,30},{2,4},{4,2},{6,8},{8,6},{10,12},{12,10},{14,16},{16,14},{18... | collective-permute-start | bytes 1671176 | tf_op jit(solution)/shard_map/ppermute | solution.py:21
  48.1 1.5 %collective-permute-start = (bf16[3,128,1152]{2,1,0:T(8,128)(2,1)}, bf16[3,128,1152]{2,1,0:T(8,128)(2,1)}, u32[]{:S(2)}, u32[]{:S(2)}) collective-permute-start(bf16[3,128,1152]{2,1,0:T(8,128)(2,1)} %constant_dynamic-slice_fusion.4), channel_id=1, source_target_pairs={{0,1},{1,0},{2,3},{3,2},{4,5},{5,4},{6,7},{7,6},{8,9},{9,8},{10,11... | collective-permute-start | bytes 2654216 | tf_op jit(solution)/shard_map/ppermute | solution.py:34
  49.6 2.0 %constant_dynamic-slice_fusion = bf16[2,17,64,128]{3,2,1,0:T(8,128)(2,1)} fusion(bf16[6,17,64,128]{3,2,1,0:T(8,128)(2,1)} %collective-permute-done.5.refs_3_, s32[]{:T(128)S(6)} %select_n.19), kind=kLoop, calls=%fused_computation.1 | loop fusion | bytes 1114116 | tf_op jit(solution)/shard_map/dynamic_slice | solution.py:250
  51.6 2.1 %constant_dynamic-slice_fusion.2 = bf16[3,17,64,128]{3,2,1,0:T(8,128)(2,1)} fusion(bf16[6,17,64,128]{3,2,1,0:T(8,128)(2,1)} %collective-permute-done.1.refs_1_, s32[]{:T(128)S(6)} %select_n.20), kind=kLoop, calls=%fused_computation.3 | loop fusion | bytes 1671172 | tf_op jit(solution)/shard_map/dynamic_slice | solution.py:250
  53.7 0.0 collective-permute-done.8.refs_2_
  53.7 0.4 collective-permute-start.4
  54.2 5.8 %collective-permute-done.3.refs_3_ = bf16[2,17,64,128]{3,2,1,0:T(8,128)(2,1)} collective-permute-done((bf16[2,17,64,128]{3,2,1,0:T(8,128)(2,1)}, bf16[2,17,64,128]{3,2,1,0:T(8,128)(2,1)}, u32[]{:S(2)}, u32[]{:S(2)}) %collective-permute-start.3) | collective-permute-done | bytes 557088 | tf_op jit(solution)/shard_map/ppermute | solution.py:21
  60.0 0.4 collective-permute-start.7
  60.4 1.0 constant_dynamic-slice_fusion.1
  61.4 6.1 %collective-permute-done.9.refs_4_ = bf16[2,17,64,128]{3,2,1,0:T(8,128)(2,1)} collective-permute-done((bf16[2,17,64,128]{3,2,1,0:T(8,128)(2,1)}, bf16[2,17,64,128]{3,2,1,0:T(8,128)(2,1)}, u32[]{:S(2)}, u32[]{:S(2)}) %collective-permute-start.9) | collective-permute-done | bytes 557088 | tf_op jit(solution)/shard_map/ppermute | solution.py:30
  67.5 2.3 %collective-permute-start.6 = (bf16[1,17,64,128]{3,2,1,0:T(8,128)(2,1)S(1)}, bf16[1,17,64,128]{3,2,1,0:T(8,128)(2,1)S(1)}, u32[]{:S(2)}, u32[]{:S(2)}) collective-permute-start(bf16[1,17,64,128]{3,2,1,0:T(8,128)(2,1)S(1)} %constant_dynamic-slice_fusion.1), channel_id=1, source_target_pairs={{0,1},{1,0},{2,3},{3,2},{4,5},{5,4},{6,7},{7,6},{8,9},{9,8},{10,11... | collective-permute-start | bytes 835592 | tf_op jit(solution)/shard_map/ppermute | solution.py:34
  69.8 13.6 %shard_map.47.refs_7_ = bf16[18,384,256]{2,1,0:T(8,128)(2,1)S(1)} custom-call(bf16[6,128,1152]{2,1,0:T(8,128)(2,1)S(1)} %copy-done, bf16[6,17,64,128]{3,2,1,0:T(8,128)(2,1)S(1)} %compare_select_fusion.refs_1_, bf16[6,17,64,128]{3,2,1,0:T(8,128)(2,1)} %collective-permute-done.8.refs_2_, bf16[6,17,64,128]{3,2,1,0:T(8,128)(2,1)} %collective-permute-done.5.refs_3_, ...), custom_call_target="tpu_custom_call" | custom-call | tf_op jit(solution)/shard_map/pallas_call | solution.py:223
  83.5 0.0 collective-permute-done.refs_0_
  83.5 0.0 collective-permute-done.6.refs_5_
  83.5 14.2 %shard_map.48 = bf16[3,33,128,128]{3,2,1,0:T(8,128)(2,1)} custom-call(bf16[3,128,1152]{2,1,0:T(8,128)(2,1)} %collective-permute-done.refs_0_, bf16[6,17,64,128]{3,2,1,0:T(8,128)(2,1)} %collective-permute-done.1.refs_1_, bf16[6,17,64,128]{3,2,1,0:T(8,128)(2,1)} %collective-permute-done.2.refs_2_, bf16[2,17,64,128]{3,2,1,0:T(8,128)(2,1)} %collective-permute-done.3.refs_3_, ...), custom_call_target="tpu_custom_call" | custom-call | tf_op jit(solution)/shard_map/pallas_call | solution.py:223
  (8 shorter events, 0.0 us)
Async XLA Ops:
  1.7 39.6 %collective-permute-start.1 = (bf16[6,17,64,128]{3,2,1,0:T(8,128)(2,1)S(1)}, bf16[6,17,64,128]{3,2,1,0:T(8,128)(2,1)}, u32[]{:S(2)}, u32[]{:S(2)}) collective-permute-start(bf16[6,17,64,128]{3,2,1,0:T(8,128)(2,1)S(1)} %compare_select_fusion.refs_1_), channel_id=1, source_target_pairs={{0,1},{1,0},{2,3},{3,2},{4,5},{5,4},{6,7},{7,6},{8,9},{9,8},{10,11... | collective-permute-start | bytes 5013512 | tf_op jit(solution)/shard_map/ppermute | solution.py:34
  4.7 44.9 %collective-permute-start.5 = (bf16[6,17,64,128]{3,2,1,0:T(8,128)(2,1)S(1)}, bf16[6,17,64,128]{3,2,1,0:T(8,128)(2,1)}, u32[]{:S(2)}, u32[]{:S(2)}) collective-permute-start(bf16[6,17,64,128]{3,2,1,0:T(8,128)(2,1)S(1)} %compare_select_fusion.refs_1_), channel_id=1, source_target_pairs={{0,30},{2,4},{4,2},{6,8},{8,6},{10,12},{12,10},{14,16},{16,14},{18... | collective-permute-start | bytes 5013512 | tf_op jit(solution)/shard_map/ppermute | solution.py:21
  8.4 45.3 %collective-permute-start.8 = (bf16[6,17,64,128]{3,2,1,0:T(8,128)(2,1)S(1)}, bf16[6,17,64,128]{3,2,1,0:T(8,128)(2,1)}, u32[]{:S(2)}, u32[]{:S(2)}) collective-permute-start(bf16[6,17,64,128]{3,2,1,0:T(8,128)(2,1)S(1)} %compare_select_fusion.refs_1_), channel_id=1, source_target_pairs={{0,2},{2,0},{4,6},{6,4},{8,10},{10,8},{12,14},{14,12},{16,18},{18,... | collective-permute-start | bytes 5013512 | tf_op jit(solution)/shard_map/ppermute | solution.py:17
  41.3 42.2 %collective-permute-start.2 = (bf16[6,17,64,128]{3,2,1,0:T(8,128)(2,1)}, bf16[6,17,64,128]{3,2,1,0:T(8,128)(2,1)}, u32[]{:S(2)}, u32[]{:S(2)}) collective-permute-start(bf16[6,17,64,128]{3,2,1,0:T(8,128)(2,1)} %collective-permute-done.1.refs_1_), channel_id=1, source_target_pairs={{0,2},{2,0},{4,6},{6,4},{8,10},{10,8},{12,14},{14,12},{16,18},{18,... | collective-permute-start | bytes 5013512 | tf_op jit(solution)/shard_map/ppermute | solution.py:17
  43.2 16.8 %collective-permute-start.3 = (bf16[2,17,64,128]{3,2,1,0:T(8,128)(2,1)}, bf16[2,17,64,128]{3,2,1,0:T(8,128)(2,1)}, u32[]{:S(2)}, u32[]{:S(2)}) collective-permute-start(bf16[2,17,64,128]{3,2,1,0:T(8,128)(2,1)} %constant_dynamic-slice_fusion.3), channel_id=1, source_target_pairs={{0,30},{2,4},{4,2},{6,8},{8,6},{10,12},{12,10},{14,16},{16,14},{18... | collective-permute-start | bytes 1671176 | tf_op jit(solution)/shard_map/ppermute | solution.py:21
  48.1 35.4 %collective-permute-start = (bf16[3,128,1152]{2,1,0:T(8,128)(2,1)}, bf16[3,128,1152]{2,1,0:T(8,128)(2,1)}, u32[]{:S(2)}, u32[]{:S(2)}) collective-permute-start(bf16[3,128,1152]{2,1,0:T(8,128)(2,1)} %constant_dynamic-slice_fusion.4), channel_id=1, source_target_pairs={{0,1},{1,0},{2,3},{3,2},{4,5},{5,4},{6,7},{7,6},{8,9},{9,8},{10,11... | collective-permute-start | bytes 2654216 | tf_op jit(solution)/shard_map/ppermute | solution.py:34
  49.6 20.2 %copy-start = (bf16[6,128,1152]{2,1,0:T(8,128)(2,1)S(1)}, bf16[6,128,1152]{2,1,0:T(8,128)(2,1)}, u32[]{:S(2)}) copy-start(bf16[6,128,1152]{2,1,0:T(8,128)(2,1)} %shard_map.46.refs_0_) | copy-start | bytes 5308420
  51.6 15.9 %collective-permute-start.9 = (bf16[2,17,64,128]{3,2,1,0:T(8,128)(2,1)}, bf16[2,17,64,128]{3,2,1,0:T(8,128)(2,1)}, u32[]{:S(2)}, u32[]{:S(2)}) collective-permute-start(bf16[2,17,64,128]{3,2,1,0:T(8,128)(2,1)} %constant_dynamic-slice_fusion), channel_id=1, source_target_pairs={{0,2},{1,27},{2,8},{3,1},{4,6},{5,31},{6,12},{7,5},{8,10},{9,3},{1... | collective-permute-start | bytes 1671176 | tf_op jit(solution)/shard_map/ppermute | solution.py:30
  53.7 29.8 %collective-permute-start.4 = (bf16[3,17,64,128]{3,2,1,0:T(8,128)(2,1)}, bf16[3,17,64,128]{3,2,1,0:T(8,128)(2,1)}, u32[]{:S(2)}, u32[]{:S(2)}) collective-permute-start(bf16[3,17,64,128]{3,2,1,0:T(8,128)(2,1)} %constant_dynamic-slice_fusion.2), channel_id=1, source_target_pairs={{0,30},{2,4},{4,2},{6,8},{8,6},{10,12},{12,10},{14,16},{16,14},{18... | collective-permute-start | bytes 2506760 | tf_op jit(solution)/shard_map/ppermute | solution.py:21
  60.0 23.5 %collective-permute-start.7 = (bf16[2,17,64,128]{3,2,1,0:T(8,128)(2,1)}, bf16[2,17,64,128]{3,2,1,0:T(8,128)(2,1)}, u32[]{:S(2)}, u32[]{:S(2)}) collective-permute-start(bf16[2,17,64,128]{3,2,1,0:T(8,128)(2,1)} %collective-permute-done.3.refs_3_), channel_id=1, source_target_pairs={{0,2},{1,27},{2,8},{3,1},{4,6},{5,31},{6,12},{7,5},{8,10},{9,3},{1... | collective-permute-start | bytes 1671176 | tf_op jit(solution)/shard_map/ppermute | solution.py:30
  67.5 15.9 %collective-permute-start.6 = (bf16[1,17,64,128]{3,2,1,0:T(8,128)(2,1)S(1)}, bf16[1,17,64,128]{3,2,1,0:T(8,128)(2,1)S(1)}, u32[]{:S(2)}, u32[]{:S(2)}) collective-permute-start(bf16[1,17,64,128]{3,2,1,0:T(8,128)(2,1)S(1)} %constant_dynamic-slice_fusion.1), channel_id=1, source_target_pairs={{0,1},{1,0},{2,3},{3,2},{4,5},{5,4},{6,7},{7,6},{8,9},{9,8},{10,11... | collective-permute-start | bytes 835592 | tf_op jit(solution)/shard_map/ppermute | solution.py:34

commit v3 on v2

v3 whole, which is shorter than its diff:
```python
import functools

import jax
import jax.numpy as jnp
from jax import lax
from jax.experimental import pallas as pl
from jax.experimental.pallas import tpu as pltpu
from jax.sharding import PartitionSpec as P

RING = ("row", "col")
EVERY = ("row", "col", "rep")
EXTRA_ROWS = 2
REST = 1
VMEM_LIMIT = 24 * 2**20


def to_chip_peer(x, ring):
    return lax.ppermute(x, RING, [(g, g ^ 1) for g in range(ring)])


def to_outer_neighbour(x, ring):
    return lax.ppermute(x, RING, [(g, (g + 2 * (g % 2) - 1) % ring) for g in range(ring)])


def to_second_neighbour(x, ring):
    pairs = []
    for g in range(ring):
        owner = g + 1 if g % 2 else g - 1
        pairs.append((2 * g, 2 * ((owner + 2) % ring)))
        pairs.append((2 * g + 1, 2 * ((owner - 2) % ring) + 1))
    return lax.ppermute(x, EVERY, pairs)


def over_rep(x):
    return lax.ppermute(x, "rep", [(0, 1), (1, 0)])


def turn_kernel(rows_out, extent_ref, a_ref, out_ref):
    rows, band, depth, block = a_ref.shape
    half_band = (band - 1) // 2
    squares = out_ref.shape[2] // (2 * depth)
    blank = jnp.zeros((depth, block), a_ref.dtype)
    for row in range(rows):
        shift = first_slot(row // rows_out, row % rows_out) % 2
        extent = extent_ref[row]

        def piece(offset):
            if not 0 <= offset < band:
                return blank
            return jnp.where(abs(offset - half_band) <= extent, a_ref[row, offset], blank)

        for square in range(squares):
            offset = 2 * square - shift
            both = jnp.concatenate([piece(offset), piece(offset + 1)], 0)
            out_ref[row, :, square * 2 * depth : (square + 1) * 2 * depth] = both.T


def turned_left(a_blocks, a_extent, rows_out):
    rows, band, depth, block = a_blocks.shape
    return pl.pallas_call(
        functools.partial(turn_kernel, rows_out),
        out_shape=jax.ShapeDtypeStruct((rows, block, (band + 1) * depth), a_blocks.dtype),
        in_specs=[
            pl.BlockSpec(memory_space=pltpu.SMEM),
            pl.BlockSpec(memory_space=pltpu.VMEM),
        ],
        out_specs=pl.BlockSpec(memory_space=pltpu.VMEM),
        cost_estimate=pl.CostEstimate(
            flops=0, bytes_accessed=8 * a_blocks.size, transcendentals=0
        ),
    )(a_extent, a_blocks)


def first_slot(rep_value, row):
    return row + rep_value


def product_kernel(plan, *refs):
    refs = list(refs)
    turned_ref = refs.pop(0)
    source_refs = [refs.pop(0) for _ in range(plan["sources"])]
    partial_ref = refs.pop(0) if plan["partial"] else None
    out_ref, left, window, left_sem, row_sem = refs[:5]
    final = plan["final"]
    if final:
        result, out_sem = refs[5:]
    band, rows_out = plan["band"], plan["rows_out"]
    columns, slots, depth, block = window.shape
    pairs = columns // 2
    reach = (band + 1) * depth
    width = slots * depth
    rep = lax.axis_index("rep")
    core = lax.rem(lax.axis_index("col"), 2)
    first_row = rows_out * rep if plan["own_left"] else 0

    def left_copy(row, at):
        return pltpu.make_async_copy(
            turned_ref.at[first_row + row],
            left.at[pl.ds(row * block, block), pl.ds(at, reach)],
            left_sem.at[row],
        )

    def row_copy(source, position, slot, index):
        return pltpu.make_async_copy(
            source.at[position], window.at[pl.ds(slot, band), slot], row_sem.at[index]
        )

    def out_copy(half, row):
        low = half * (band - 1)
        count = band - 1 if half == 0 else band
        return pltpu.make_async_copy(
            result.at[row, pl.ds(first_slot(rep, row) + low, count)],
            out_ref.at[row, pl.ds(low, count)],
            out_sem.at[half, row],
        )

    def place_left(rep_value):
        for row in range(rows_out):
            at = first_slot(rep_value, row) // 2 * 2 * depth
            left_copy(row, at).start()
            lines = slice(row * block, (row + 1) * block)
            if at:
                left[lines, :at] = jnp.zeros((block, at), left.dtype)
            if at + reach < width:
                left[lines, at + reach :] = jnp.zeros((block, width - at - reach), left.dtype)

    def place_rows(listed):
        for index, (slot, source, position) in enumerate(listed):
            row_copy(source_refs[source], position, slot, index).start()
        blank = jnp.zeros((depth, block), window.dtype)
        taken = {slot for slot, _, _ in listed}
        for pair in range(pairs):
            if 2 * pair + 1 in taken:
                window[2 * pair, 2 * pair + 1] = blank
            if 2 * pair + 1 - band in taken:
                window[2 * pair + 1, 2 * pair + 1 - band] = blank

    def multiply(ranges, some_pairs):
        for pair in some_pairs:
            total = None
            for low, high in ranges:
                first, last = max(low, 2 * pair + 1 - band), min(high, 2 * pair + 2)
                if first >= last:
                    continue
                span = (last - first) * depth
                right = jnp.concatenate(
                    [
                        window[2 * pair + side, first:last].reshape(span, block)
                        for side in range(2)
                    ],
                    1,
                )
                term = jnp.dot(
                    left[:, first * depth : last * depth],
                    right,
                    preferred_element_type=jnp.float32,
                )
                total = term if total is None else total + term
            if partial_ref is not None:
                before = partial_ref[pair].astype(jnp.float32)
                total = before if total is None else total + before
            if not final:
                out_ref[pair] = total.astype(out_ref.dtype)
                continue
            total = total.astype(result.dtype)
            for row in range(rows_out):
                for side in range(2):
                    result[row, 2 * pair + side] = total[
                        row * block : (row + 1) * block, side * block : (side + 1) * block
                    ]

    for rep_value in range(2):

        @pl.when(rep == rep_value)
        def _(rep_value=rep_value):
            place_left(rep_value)

        for core_value in range(2):

            @pl.when((rep == rep_value) & (core == core_value))
            def _(rep_value=rep_value, core_value=core_value):
                place_rows(plan["where"](rep_value, core_value))

    for row in range(rows_out):
        left_copy(row, 0).wait()
    for index in range(plan["taken"]):
        row_copy(source_refs[0], 0, 0, index).wait()

    parts = [range(pairs)]
    if final:
        middle = (band - 1 + rows_out) // 2 + 1
        parts = [range(middle), range(middle, pairs)]
    for half, part in enumerate(parts):
        if plan["taken"] == slots:
            multiply([(0, slots)], part)
        else:
            for rep_value in range(2):
                for core_value in range(2):

                    @pl.when((rep == rep_value) & (core == core_value))
                    def _(rep_value=rep_value, core_value=core_value, part=part):
                        taken = sorted(slot for slot, _, _ in plan["where"](rep_value, core_value))
                        lows = [slot for slot in taken if slot - 1 not in taken]
                        highs = [slot + 1 for slot in taken if slot + 1 not in taken]
                        multiply(list(zip(lows, highs)), part)

        if final:
            for row in range(rows_out):
                out_copy(half, row).start()
    if final:
        for half in range(2):
            for row in range(rows_out):
                out_copy(half, row).wait()


def partial_product(turned, sources, where, partial, rows_out, own_left, kind):
    band, depth, block = sources[0].shape[1:]
    slots = rows_out + band
    columns = slots + band - 1
    taken = len(where(0, 0))
    final = kind is None
    plan = {
        "sources": len(sources),
        "where": where,
        "taken": taken,
        "band": band,
        "rows_out": rows_out,
        "own_left": own_left,
        "partial": partial is not None,
        "final": final,
    }
    operands = [turned, *sources]
    in_specs = [pl.BlockSpec(memory_space=pl.ANY)] * len(operands)
    if partial is not None:
        operands.append(partial)
        in_specs.append(pl.BlockSpec(memory_space=pltpu.VMEM))
    scratch = [
        pltpu.VMEM((rows_out * block, slots * depth), jnp.bfloat16),
        pltpu.VMEM((columns, slots, depth, block), jnp.bfloat16),
        pltpu.SemaphoreType.DMA((rows_out,)),
        pltpu.SemaphoreType.DMA((taken,)),
    ]
    if final:
        out_shape = jax.ShapeDtypeStruct((rows_out, 2 * band - 1, block, block), jnp.bfloat16)
        out_spec = pl.BlockSpec(memory_space=pl.ANY)
        scratch += [
            pltpu.VMEM((rows_out, columns, block, block), jnp.bfloat16),
            pltpu.SemaphoreType.DMA((2, rows_out)),
        ]
    else:
        out_shape = pltpu.VMEM((columns // 2, rows_out * block, 2 * block), kind)
        out_spec = pl.BlockSpec(memory_space=pltpu.VMEM)
    return pl.pallas_call(
        functools.partial(product_kernel, plan),
        out_shape=out_shape,
        in_specs=in_specs,
        out_specs=out_spec,
        scratch_shapes=scratch,
        compiler_params=pltpu.CompilerParams(vmem_limit_bytes=VMEM_LIMIT),
        cost_estimate=pl.CostEstimate(flops=0, bytes_accessed=0, transcendentals=0),
    )(*operands)


def local(a_blocks, b_blocks, a_extent, b_extent):
    rows, band, depth, block = a_blocks.shape
    half_band = (band - 1) // 2
    ring = lax.axis_size("row") * lax.axis_size("col")
    rows_out = rows // lax.axis_size("rep")
    rep = lax.axis_index("rep")

    distance = jnp.abs(lax.broadcasted_iota(jnp.int32, b_blocks.shape, 1) - half_band)
    live = distance <= b_extent[:, None, None, None]
    b_own = b_blocks * live.astype(b_blocks.dtype)

    starts = ((rows - EXTRA_ROWS, REST, 0), (0, EXTRA_ROWS, rows - REST))
    sizes = (EXTRA_ROWS, rows - EXTRA_ROWS - REST, REST)

    def rows_for(x, side, index):
        start = jnp.where(side == 0, starts[0][index], starts[1][index])
        return lax.dynamic_slice_in_dim(x, start, sizes[index], 0)

    outer = to_outer_neighbour(b_own, ring)
    across = over_rep(b_own)
    peer = to_chip_peer(b_own, ring)
    turned = turned_left(a_blocks, a_extent, rows_out)
    turned_send = lax.dynamic_slice_in_dim(turned, rows_out * (1 - rep), rows_out, 0)
    turned_across = over_rep(turned_send)
    across = lax.optimization_barrier((across, turned_send))[0]
    across_outer = [to_outer_neighbour(rows_for(across, rep, i), ring) for i in range(2)]
    across_peer = to_chip_peer(across, ring)
    extra = to_second_neighbour(rows_for(outer, rep, 0), ring)
    across_outer.append(over_rep(rows_for(outer, 1 - rep, 2)))
    across_extra = to_second_neighbour(across_outer[0], ring)

    def window_rows(rep_value, core_value):
        sides = ("outer", "peer") if core_value == 0 else ("peer", "outer")
        line = [(kind, i) for kind in (sides[0], "own", sides[1]) for i in range(rows)]
        extra_line = [("extra", i) for i in range(EXTRA_ROWS)]
        return extra_line + line if rep_value == 0 else line + extra_line

    def where_of(index):
        def where(rep_value, core_value):
            found = []
            for slot, (kind, i) in enumerate(window_rows(rep_value, core_value)):
                if kind not in index:
                    continue
                source = index[kind]
                if isinstance(source, tuple):
                    spans = zip(starts[rep_value], sizes)
                    piece = [low <= i < low + size for low, size in spans].index(True)
                    found.append((slot, source[piece], i - starts[rep_value][piece]))
                else:
                    found.append((slot, source, i))
            return found

        return where

    total = partial_product(
        turned,
        [b_own, peer, outer, extra],
        where_of({"own": 0, "peer": 1, "outer": 2, "extra": 3}),
        None,
        rows_out,
        True,
        jnp.bfloat16,
    )
    total = partial_product(
        turned_across,
        [across, across_peer],
        where_of({"own": 0, "peer": 1}),
        total,
        rows_out,
        False,
        jnp.float32,
    )
    return partial_product(
        turned_across,
        [*across_outer, across_extra],
        where_of({"outer": (0, 1, 2), "extra": 3}),
        total,
        rows_out,
        False,
        None,
    )


def solution(mesh):
    return jax.shard_map(
        local,
        mesh=mesh,
        in_specs=(
            P(("row", "col"), None, "rep", None),
            P(("row", "col"), None, "rep", None),
            P(("row", "col")),
            P(("row", "col")),
        ),
        out_specs=P(("row", "col", "rep"), None, None, None),
        check_vma=False,
    )
```

time: 98.1 us -> 84.3 us (0.86)
  Pallas kernels: 31 us -> 17 us
    pallas_call x2 -> x3, Pallas kernels: 27.8 us -> 13.8 us  [partial_product(): pl.pallas_call(functools.partial(product_kernel, plan), out_shape=out_sha...]
  transfers between devices with their start and end apart: 10 -> 10, of which waited for: 3 -> 3; matrix products, arithmetic and copies ran while one was open for 9% -> 11% of each run, Pallas kernels for 17% -> 15%
where the time goes in v3:
time: 84.3 us; the launch traced here: 83.8 us
  waiting for transfers between devices  39.5 us (47%)
  Pallas kernels  17 us (20%)
  starting transfers between devices  16.3 us (19%)
  local copies, waits for them, and re-layouts  9.18 us (11%)
  other arithmetic  1.65 us (2%)
    ppermute x3, waiting for transfers between devices, over_rep(): return lax.ppermute(x, 'rep', [(0, 1), (1, 0)])  27.5 us
    pallas_call x3, Pallas kernels, partial_product(): pl.pallas_call(functools.partial(product_kernel, plan), out_shape=out_sha...  13.8 us
    ppermute x3, starting transfers between devices, to_outer_neighbour(): lax.ppermute(x, RING, [(g, (g + 2 * (g % 2) - 1) % ring) for g in range(r...  9.08 us
    dynamic_slice x4, local copies, waits for them, and re-layouts, rows_for(): return lax.dynamic_slice_in_dim(x, start, sizes[index], 0)  6.99 us
    ppermute x3, starting transfers between devices, over_rep(): return lax.ppermute(x, 'rep', [(0, 1), (1, 0)])  6.77 us
    ppermute x2, waiting for transfers between devices, to_second_neighbour(): return lax.ppermute(x, EVERY, pairs)  6.14 us
    ppermute x3, waiting for transfers between devices, to_outer_neighbour(): lax.ppermute(x, RING, [(g, (g + 2 * (g % 2) - 1) % ring) for g in range(r...  5.85 us
    pallas_call x1, Pallas kernels, turned_left(): pl.pallas_call(functools.partial(turn_kernel, rows_out), out_shape=jax.Sh...  3.18 us
  transfers between devices with their start and end apart: 10, of which 3 were waited for; matrix products, arithmetic and copies ran while one was open for 11% of the time, Pallas kernels for 15%

profile of v3, /device:TPU:0, one launch (start us, length us, event | category | flops | bytes accessed | tf_op | source)
XLA Modules:
  0.0 83.8 jit_solution(15012415372916236634)
XLA Ops:
  0.0 1.6 %compare_select_fusion.refs_1_ = bf16[6,17,64,128]{3,2,1,0:T(8,128)(2,1)S(1)} fusion(bf16[6,17,64,128]{3,2,1,0:T(8,128)(2,1)} %param.5, s32[6]{0:T(128)} %param.7, s32[17]{0:T(128)S(1)} %add_abs_fusion), kind=kLoop, calls=%fused_computation | loop fusion | flops 1671168 | bytes 3342428 | tf_op jit(solution)/shard_map/mul | solution.py:273
  1.7 3.0 %collective-permute-start.1 = (bf16[6,17,64,128]{3,2,1,0:T(8,128)(2,1)S(1)}, bf16[6,17,64,128]{3,2,1,0:T(8,128)(2,1)}, u32[]{:S(2)}, u32[]{:S(2)}) collective-permute-start(bf16[6,17,64,128]{3,2,1,0:T(8,128)(2,1)S(1)} %compare_select_fusion.refs_1_), channel_id=1, source_target_pairs={{0,1},{1,0},{2,3},{3,2},{4,5},{5,4},{6,7},{7,6},{8,9},{9,8},{10,11... | collective-permute-start | bytes 5013512 | tf_op jit(solution)/shard_map/ppermute | solution.py:35
  4.7 3.7 %collective-permute-start.4 = (bf16[6,17,64,128]{3,2,1,0:T(8,128)(2,1)S(1)}, bf16[6,17,64,128]{3,2,1,0:T(8,128)(2,1)}, u32[]{:S(2)}, u32[]{:S(2)}) collective-permute-start(bf16[6,17,64,128]{3,2,1,0:T(8,128)(2,1)S(1)} %compare_select_fusion.refs_1_), channel_id=1, source_target_pairs={{0,30},{2,4},{4,2},{6,8},{8,6},{10,12},{12,10},{14,16},{16,14},{18... | collective-permute-start | bytes 5013512 | tf_op jit(solution)/shard_map/ppermute | solution.py:22
  8.4 0.0 collective-permute-start.8
  8.4 3.2 %shard_map.46.refs_0_ = bf16[6,128,1152]{2,1,0:T(8,128)(2,1)} custom-call(s32[6]{0:T(128)} %extent_ref.1, bf16[6,17,64,128]{3,2,1,0:T(8,128)(2,1)} %a_ref.1), custom_call_target="tpu_custom_call" | custom-call | bytes 6684672 | tf_op jit(solution)/shard_map/pallas_call | solution.py:60
  11.6 2.2 %constant_dynamic-slice_fusion.4 = bf16[3,128,1152]{2,1,0:T(8,128)(2,1)} fusion(bf16[6,128,1152]{2,1,0:T(8,128)(2,1)} %shard_map.46.refs_0_, s32[]{:T(128)S(6)} %select_n.18), kind=kLoop, calls=%fused_computation.5 | loop fusion | bytes 1769476 | tf_op jit(solution)/shard_map/dynamic_slice | solution.py:286
  13.8 27.5 %collective-permute-done.1.refs_1_ = bf16[6,17,64,128]{3,2,1,0:T(8,128)(2,1)} collective-permute-done((bf16[6,17,64,128]{3,2,1,0:T(8,128)(2,1)S(1)}, bf16[6,17,64,128]{3,2,1,0:T(8,128)(2,1)}, u32[]{:S(2)}, u32[]{:S(2)}) %collective-permute-start.1) | collective-permute-done | bytes 1671200 | tf_op jit(solution)/shard_map/ppermute | solution.py:35
  41.3 0.0 collective-permute-start.7
  41.3 1.9 %constant_dynamic-slice_fusion.3 = bf16[2,17,64,128]{3,2,1,0:T(8,128)(2,1)} fusion(bf16[6,17,64,128]{3,2,1,0:T(8,128)(2,1)} %collective-permute-done.1.refs_1_, s32[]{:T(128)S(6)} %select_n.19), kind=kLoop, calls=%fused_computation.4 | loop fusion | bytes 1114116 | tf_op jit(solution)/shard_map/dynamic_slice | solution.py:280
  43.2 4.9 %collective-permute-start.2 = (bf16[2,17,64,128]{3,2,1,0:T(8,128)(2,1)}, bf16[2,17,64,128]{3,2,1,0:T(8,128)(2,1)}, u32[]{:S(2)}, u32[]{:S(2)}) collective-permute-start(bf16[2,17,64,128]{3,2,1,0:T(8,128)(2,1)} %constant_dynamic-slice_fusion.3), channel_id=1, source_target_pairs={{0,30},{2,4},{4,2},{6,8},{8,6},{10,12},{12,10},{14,16},{16,14},{18... | collective-permute-start | bytes 1671176 | tf_op jit(solution)/shard_map/ppermute | solution.py:22
  48.1 1.5 %collective-permute-start = (bf16[3,128,1152]{2,1,0:T(8,128)(2,1)}, bf16[3,128,1152]{2,1,0:T(8,128)(2,1)}, u32[]{:S(2)}, u32[]{:S(2)}) collective-permute-start(bf16[3,128,1152]{2,1,0:T(8,128)(2,1)} %constant_dynamic-slice_fusion.4), channel_id=1, source_target_pairs={{0,1},{1,0},{2,3},{3,2},{4,5},{5,4},{6,7},{7,6},{8,9},{9,8},{10,11... | collective-permute-start | bytes 2654216 | tf_op jit(solution)/shard_map/ppermute | solution.py:35
  49.6 0.0 collective-permute-done.4.refs_3_
  49.6 2.0 %constant_dynamic-slice_fusion = bf16[2,17,64,128]{3,2,1,0:T(8,128)(2,1)} fusion(bf16[6,17,64,128]{3,2,1,0:T(8,128)(2,1)} %collective-permute-done.4.refs_3_, s32[]{:T(128)S(6)} %select_n.19), kind=kLoop, calls=%fused_computation.1 | loop fusion | bytes 1114116 | tf_op jit(solution)/shard_map/dynamic_slice | solution.py:280
  51.6 0.0 collective-permute-start.9
  51.6 2.1 %constant_dynamic-slice_fusion.2 = bf16[3,17,64,128]{3,2,1,0:T(8,128)(2,1)} fusion(bf16[6,17,64,128]{3,2,1,0:T(8,128)(2,1)} %collective-permute-done.1.refs_1_, s32[]{:T(128)S(6)} %select_n.20), kind=kLoop, calls=%fused_computation.3 | loop fusion | bytes 1671172 | tf_op jit(solution)/shard_map/dynamic_slice | solution.py:280
  53.7 0.4 collective-permute-start.3
  54.2 5.8 %collective-permute-done.2.refs_1_ = bf16[2,17,64,128]{3,2,1,0:T(8,128)(2,1)} collective-permute-done((bf16[2,17,64,128]{3,2,1,0:T(8,128)(2,1)}, bf16[2,17,64,128]{3,2,1,0:T(8,128)(2,1)}, u32[]{:S(2)}, u32[]{:S(2)}) %collective-permute-start.2) | collective-permute-done | bytes 557088 | tf_op jit(solution)/shard_map/ppermute | solution.py:22
  60.0 0.4 collective-permute-start.6
  60.4 1.0 %constant_dynamic-slice_fusion.1 = bf16[1,17,64,128]{3,2,1,0:T(8,128)(2,1)S(1)} fusion(bf16[6,17,64,128]{3,2,1,0:T(8,128)(2,1)} %collective-permute-done.4.refs_3_, s32[]{:T(128)S(6)} %select_n.21), kind=kLoop, calls=%fused_computation.2 | loop fusion | bytes 557060 | tf_op jit(solution)/shard_map/dynamic_slice | solution.py:280
  61.4 6.1 %collective-permute-done.9.refs_4_ = bf16[2,17,64,128]{3,2,1,0:T(8,128)(2,1)} collective-permute-done((bf16[2,17,64,128]{3,2,1,0:T(8,128)(2,1)}, bf16[2,17,64,128]{3,2,1,0:T(8,128)(2,1)}, u32[]{:S(2)}, u32[]{:S(2)}) %collective-permute-start.9) | collective-permute-done | bytes 557088 | tf_op jit(solution)/shard_map/ppermute | solution.py:31
  67.5 2.3 %collective-permute-start.5 = (bf16[1,17,64,128]{3,2,1,0:T(8,128)(2,1)S(1)}, bf16[1,17,64,128]{3,2,1,0:T(8,128)(2,1)S(1)}, u32[]{:S(2)}, u32[]{:S(2)}) collective-permute-start(bf16[1,17,64,128]{3,2,1,0:T(8,128)(2,1)S(1)} %constant_dynamic-slice_fusion.1), channel_id=1, source_target_pairs={{0,1},{1,0},{2,3},{3,2},{4,5},{5,4},{6,7},{7,6},{8,9},{9,8},{10,11... | collective-permute-start | bytes 835592 | tf_op jit(solution)/shard_map/ppermute | solution.py:35
  69.8 5.1 %shard_map.47.refs_3_ = bf16[18,384,256]{2,1,0:T(8,128)(2,1)S(1)} custom-call(bf16[6,128,1152]{2,1,0:T(8,128)(2,1)S(1)} %copy-done, bf16[6,17,64,128]{3,2,1,0:T(8,128)(2,1)S(1)} %compare_select_fusion.refs_1_, bf16[6,17,64,128]{3,2,1,0:T(8,128)(2,1)} %collective-permute-done.8.refs_2_, bf16[6,17,64,128]{3,2,1,0:T(8,128)(2,1)} %collective-permute-done.4.refs_3_, ...), custom_call_target="tpu_custom_call" | custom-call | tf_op jit(solution)/shard_map/pallas_call | solution.py:253
  74.9 4.1 %shard_map.48.refs_5_ = f32[18,384,256]{2,1,0:T(8,128)S(1)} custom-call(bf16[3,128,1152]{2,1,0:T(8,128)(2,1)} %collective-permute-done.refs_0_, bf16[6,17,64,128]{3,2,1,0:T(8,128)(2,1)} %collective-permute-done.1.refs_1_, bf16[6,17,64,128]{3,2,1,0:T(8,128)(2,1)} %collective-permute-done.7.refs_2_, bf16[18,384,256]{2,1,0:T(8,128)(2,1)S(1)} %shard_map.47.refs_3_), custom_call_target="tpu_custom_call" | custom-call | tf_op jit(solution)/shard_map/pallas_call | solution.py:253
  79.0 4.7 %shard_map.49 = bf16[3,33,128,128]{3,2,1,0:T(8,128)(2,1)} custom-call(bf16[3,128,1152]{2,1,0:T(8,128)(2,1)} %collective-permute-done.refs_0_, bf16[2,17,64,128]{3,2,1,0:T(8,128)(2,1)} %collective-permute-done.2.refs_1_, bf16[3,17,64,128]{3,2,1,0:T(8,128)(2,1)} %collective-permute-done.3.refs_2_, bf16[1,17,64,128]{3,2,1,0:T(8,128)(2,1)S(1)} %collective-permute-done.5.refs_3_, ...), custom_call_target="tpu_custom_call" | custom-call | tf_op jit(solution)/shard_map/pallas_call | solution.py:253
  (9 shorter events, 0.0 us)
Async XLA Ops:
  1.7 39.6 %collective-permute-start.1 = (bf16[6,17,64,128]{3,2,1,0:T(8,128)(2,1)S(1)}, bf16[6,17,64,128]{3,2,1,0:T(8,128)(2,1)}, u32[]{:S(2)}, u32[]{:S(2)}) collective-permute-start(bf16[6,17,64,128]{3,2,1,0:T(8,128)(2,1)S(1)} %compare_select_fusion.refs_1_), channel_id=1, source_target_pairs={{0,1},{1,0},{2,3},{3,2},{4,5},{5,4},{6,7},{7,6},{8,9},{9,8},{10,11... | collective-permute-start | bytes 5013512 | tf_op jit(solution)/shard_map/ppermute | solution.py:35
  4.7 44.9 %collective-permute-start.4 = (bf16[6,17,64,128]{3,2,1,0:T(8,128)(2,1)S(1)}, bf16[6,17,64,128]{3,2,1,0:T(8,128)(2,1)}, u32[]{:S(2)}, u32[]{:S(2)}) collective-permute-start(bf16[6,17,64,128]{3,2,1,0:T(8,128)(2,1)S(1)} %compare_select_fusion.refs_1_), channel_id=1, source_target_pairs={{0,30},{2,4},{4,2},{6,8},{8,6},{10,12},{12,10},{14,16},{16,14},{18... | collective-permute-start | bytes 5013512 | tf_op jit(solution)/shard_map/ppermute | solution.py:22
  8.4 45.3 %collective-permute-start.8 = (bf16[6,17,64,128]{3,2,1,0:T(8,128)(2,1)S(1)}, bf16[6,17,64,128]{3,2,1,0:T(8,128)(2,1)}, u32[]{:S(2)}, u32[]{:S(2)}) collective-permute-start(bf16[6,17,64,128]{3,2,1,0:T(8,128)(2,1)S(1)} %compare_select_fusion.refs_1_), channel_id=1, source_target_pairs={{0,2},{2,0},{4,6},{6,4},{8,10},{10,8},{12,14},{14,12},{16,18},{18,... | collective-permute-start | bytes 5013512 | tf_op jit(solution)/shard_map/ppermute | solution.py:18
  41.3 33.6 %collective-permute-start.7 = (bf16[6,17,64,128]{3,2,1,0:T(8,128)(2,1)}, bf16[6,17,64,128]{3,2,1,0:T(8,128)(2,1)}, u32[]{:S(2)}, u32[]{:S(2)}) collective-permute-start(bf16[6,17,64,128]{3,2,1,0:T(8,128)(2,1)} %collective-permute-done.1.refs_1_), channel_id=1, source_target_pairs={{0,2},{2,0},{4,6},{6,4},{8,10},{10,8},{12,14},{14,12},{16,18},{18,... | collective-permute-start | bytes 5013512 | tf_op jit(solution)/shard_map/ppermute | solution.py:18
  43.2 16.8 %collective-permute-start.2 = (bf16[2,17,64,128]{3,2,1,0:T(8,128)(2,1)}, bf16[2,17,64,128]{3,2,1,0:T(8,128)(2,1)}, u32[]{:S(2)}, u32[]{:S(2)}) collective-permute-start(bf16[2,17,64,128]{3,2,1,0:T(8,128)(2,1)} %constant_dynamic-slice_fusion.3), channel_id=1, source_target_pairs={{0,30},{2,4},{4,2},{6,8},{8,6},{10,12},{12,10},{14,16},{16,14},{18... | collective-permute-start | bytes 1671176 | tf_op jit(solution)/shard_map/ppermute | solution.py:22
  48.1 26.8 %collective-permute-start = (bf16[3,128,1152]{2,1,0:T(8,128)(2,1)}, bf16[3,128,1152]{2,1,0:T(8,128)(2,1)}, u32[]{:S(2)}, u32[]{:S(2)}) collective-permute-start(bf16[3,128,1152]{2,1,0:T(8,128)(2,1)} %constant_dynamic-slice_fusion.4), channel_id=1, source_target_pairs={{0,1},{1,0},{2,3},{3,2},{4,5},{5,4},{6,7},{7,6},{8,9},{9,8},{10,11... | collective-permute-start | bytes 2654216 | tf_op jit(solution)/shard_map/ppermute | solution.py:35
  49.6 20.2 %copy-start = (bf16[6,128,1152]{2,1,0:T(8,128)(2,1)S(1)}, bf16[6,128,1152]{2,1,0:T(8,128)(2,1)}, u32[]{:S(2)}) copy-start(bf16[6,128,1152]{2,1,0:T(8,128)(2,1)} %shard_map.46.refs_0_) | copy-start | bytes 5308420
  51.6 15.9 %collective-permute-start.9 = (bf16[2,17,64,128]{3,2,1,0:T(8,128)(2,1)}, bf16[2,17,64,128]{3,2,1,0:T(8,128)(2,1)}, u32[]{:S(2)}, u32[]{:S(2)}) collective-permute-start(bf16[2,17,64,128]{3,2,1,0:T(8,128)(2,1)} %constant_dynamic-slice_fusion), channel_id=1, source_target_pairs={{0,2},{1,27},{2,8},{3,1},{4,6},{5,31},{6,12},{7,5},{8,10},{9,3},{1... | collective-permute-start | bytes 1671176 | tf_op jit(solution)/shard_map/ppermute | solution.py:31
  53.7 25.3 %collective-permute-start.3 = (bf16[3,17,64,128]{3,2,1,0:T(8,128)(2,1)}, bf16[3,17,64,128]{3,2,1,0:T(8,128)(2,1)}, u32[]{:S(2)}, u32[]{:S(2)}) collective-permute-start(bf16[3,17,64,128]{3,2,1,0:T(8,128)(2,1)} %constant_dynamic-slice_fusion.2), channel_id=1, source_target_pairs={{0,30},{2,4},{4,2},{6,8},{8,6},{10,12},{12,10},{14,16},{16,14},{18... | collective-permute-start | bytes 2506760 | tf_op jit(solution)/shard_map/ppermute | solution.py:22
  60.0 19.0 %collective-permute-start.6 = (bf16[2,17,64,128]{3,2,1,0:T(8,128)(2,1)}, bf16[2,17,64,128]{3,2,1,0:T(8,128)(2,1)}, u32[]{:S(2)}, u32[]{:S(2)}) collective-permute-start(bf16[2,17,64,128]{3,2,1,0:T(8,128)(2,1)} %collective-permute-done.2.refs_1_), channel_id=1, source_target_pairs={{0,2},{1,27},{2,8},{3,1},{4,6},{5,31},{6,12},{7,5},{8,10},{9,3},{1... | collective-permute-start | bytes 1671176 | tf_op jit(solution)/shard_map/ppermute | solution.py:31
  67.5 11.4 %collective-permute-start.5 = (bf16[1,17,64,128]{3,2,1,0:T(8,128)(2,1)S(1)}, bf16[1,17,64,128]{3,2,1,0:T(8,128)(2,1)S(1)}, u32[]{:S(2)}, u32[]{:S(2)}) collective-permute-start(bf16[1,17,64,128]{3,2,1,0:T(8,128)(2,1)S(1)} %constant_dynamic-slice_fusion.1), channel_id=1, source_target_pairs={{0,1},{1,0},{2,3},{3,2},{4,5},{5,4},{6,7},{7,6},{8,9},{9,8},{10,11... | collective-permute-start | bytes 835592 | tf_op jit(solution)/shard_map/ppermute | solution.py:35

commit v4 on v3

--- a/solution.py
+++ b/solution.py
@@ -35,12 +35,14 @@
     return lax.ppermute(x, "rep", [(0, 1), (1, 0)])
 
 
-def turn_kernel(rows_out, extent_ref, a_ref, out_ref):
+def turn_kernel(rows_out, extent_ref, a_ref, keep_ref, send_ref):
     rows, band, depth, block = a_ref.shape
     half_band = (band - 1) // 2
-    squares = out_ref.shape[2] // (2 * depth)
+    squares = keep_ref.shape[2] // (2 * depth)
     blank = jnp.zeros((depth, block), a_ref.dtype)
-    for row in range(rows):
+    rep = lax.axis_index("rep")
+
+    def turn(row, into_ref):
         shift = first_slot(row // rows_out, row % rows_out) % 2
         extent = extent_ref[row]
 
@@ -52,23 +54,63 @@
         for square in range(squares):
             offset = 2 * square - shift
             both = jnp.concatenate([piece(offset), piece(offset + 1)], 0)
-            out_ref[row, :, square * 2 * depth : (square + 1) * 2 * depth] = both.T
+            into_ref[row % rows_out, :, square * 2 * depth : (square + 1) * 2 * depth] = both.T
+
+    for rep_value in range(rows // rows_out):
+
+        @pl.when(rep == rep_value)
+        def _(rep_value=rep_value):
+            for row in range(rows):
+                turn(row, keep_ref if row // rows_out == rep_value else send_ref)
 
 
 def turned_left(a_blocks, a_extent, rows_out):
     rows, band, depth, block = a_blocks.shape
+    shape = jax.ShapeDtypeStruct((rows_out, block, (band + 1) * depth), a_blocks.dtype)
     return pl.pallas_call(
         functools.partial(turn_kernel, rows_out),
-        out_shape=jax.ShapeDtypeStruct((rows, block, (band + 1) * depth), a_blocks.dtype),
+        out_shape=(shape, shape),
         in_specs=[
             pl.BlockSpec(memory_space=pltpu.SMEM),
             pl.BlockSpec(memory_space=pltpu.VMEM),
         ],
-        out_specs=pl.BlockSpec(memory_space=pltpu.VMEM),
-        cost_estimate=pl.CostEstimate(
-            flops=0, bytes_accessed=8 * a_blocks.size, transcendentals=0
-        ),
+        out_specs=(pl.BlockSpec(memory_space=pltpu.VMEM),) * 2,
+        compiler_params=pltpu.CompilerParams(vmem_limit_bytes=8 * 2**20),
+        cost_estimate=pl.CostEstimate(flops=0, bytes_accessed=0, transcendentals=0),
     )(a_extent, a_blocks)
+
+
+def pick_kernel(spans, x_ref, *refs):
+    out_refs, sem = refs[:-1], refs[-1]
+    rep = lax.axis_index("rep")
+
+    def copies():
+        return [
+            pltpu.make_async_copy(
+                x_ref.at[pl.ds(jnp.where(rep == 0, low, high), out_ref.shape[0])],
+                out_ref,
+                sem.at[i],
+            )
+            for i, ((low, high), out_ref) in enumerate(zip(spans, out_refs))
+        ]
+
+    for copy in copies():
+        copy.start()
+    for copy in copies():
+        copy.wait()
+
+
+def picked(x, spans, sizes):
+    shapes = [jax.ShapeDtypeStruct((size, *x.shape[1:]), x.dtype) for size in sizes]
+    return pl.pallas_call(
+        functools.partial(pick_kernel, spans),
+        out_shape=shapes,
+        in_specs=[pl.BlockSpec(memory_space=pl.ANY)],
+        out_specs=[pl.BlockSpec(memory_space=pl.ANY)] * len(sizes),
+        scratch_shapes=[pltpu.SemaphoreType.DMA((len(sizes),))],
+        compiler_params=pltpu.CompilerParams(vmem_limit_bytes=2**20),
+        cost_estimate=pl.CostEstimate(flops=0, bytes_accessed=0, transcendentals=0),
+    )(x)
 
 
 def first_slot(rep_value, row):
@@ -77,6 +119,7 @@
 
 def product_kernel(plan, *refs):
     refs = list(refs)
+    extent_ref = refs.pop(0)
     turned_ref = refs.pop(0)
     source_refs = [refs.pop(0) for _ in range(plan["sources"])]
     partial_ref = refs.pop(0) if plan["partial"] else None
@@ -87,15 +130,15 @@
     band, rows_out = plan["band"], plan["rows_out"]
     columns, slots, depth, block = window.shape
     pairs = columns // 2
+    half_band = (band - 1) // 2
     reach = (band + 1) * depth
     width = slots * depth
     rep = lax.axis_index("rep")
     core = lax.rem(lax.axis_index("col"), 2)
-    first_row = rows_out * rep if plan["own_left"] else 0
 
     def left_copy(row, at):
         return pltpu.make_async_copy(
-            turned_ref.at[first_row + row],
+            turned_ref.at[row],
             left.at[pl.ds(row * block, block), pl.ds(at, reach)],
             left_sem.at[row],
         )
@@ -181,10 +224,36 @@
             def _(rep_value=rep_value, core_value=core_value):
                 place_rows(plan["where"](rep_value, core_value))
 
+    def blank_absent(slot):
+        row_count = extent_ref.shape[0]
+        rows = 2 * rows_out
+        group = lax.axis_index("row") * lax.axis_size("col") + lax.axis_index("col")
+        place = group * rows + slot - half_band + rep * (half_band - rows)
+        extent = extent_ref[lax.rem(place + row_count, row_count)]
+        blank = jnp.zeros((depth, block), window.dtype)
+
+        def clear(offset, carry):
+            window[slot + offset, slot] = blank
+            window[slot + band - 1 - offset, slot] = blank
+            return carry
+
+        lax.fori_loop(0, half_band - extent, clear, 0)
+
     for row in range(rows_out):
         left_copy(row, 0).wait()
     for index in range(plan["taken"]):
         row_copy(source_refs[0], 0, 0, index).wait()
+    if plan["taken"] == slots:
+        for slot in range(slots):
+            blank_absent(slot)
+    else:
+        for rep_value in range(2):
+            for core_value in range(2):
+
+                @pl.when((rep == rep_value) & (core == core_value))
+                def _(rep_value=rep_value, core_value=core_value):
+                    for slot, _, _ in plan["where"](rep_value, core_value):
+                        blank_absent(slot)
 
     parts = [range(pairs)]
     if final:
@@ -213,7 +282,7 @@
                 out_copy(half, row).wait()
 
 
-def partial_product(turned, sources, where, partial, rows_out, own_left, kind):
+def partial_product(extents, turned, sources, where, partial, rows_out, kind):
     band, depth, block = sources[0].shape[1:]
     slots = rows_out + band
     columns = slots + band - 1
@@ -225,12 +294,12 @@
         "taken": taken,
         "band": band,
         "rows_out": rows_out,
-        "own_left": own_left,
         "partial": partial is not None,
         "final": final,
     }
-    operands = [turned, *sources]
-    in_specs = [pl.BlockSpec(memory_space=pl.ANY)] * len(operands)
+    operands = [extents, turned, *sources]
+    in_specs = [pl.BlockSpec(memory_space=pltpu.SMEM)]
+    in_specs += [pl.BlockSpec(memory_space=pl.ANY)] * (1 + len(sources))
     if partial is not None:
         operands.append(partial)
         in_specs.append(pl.BlockSpec(memory_space=pltpu.VMEM))
@@ -263,33 +332,27 @@
 
 def local(a_blocks, b_blocks, a_extent, b_extent):
     rows, band, depth, block = a_blocks.shape
-    half_band = (band - 1) // 2
     ring = lax.axis_size("row") * lax.axis_size("col")
     rows_out = rows // lax.axis_size("rep")
-    rep = lax.axis_index("rep")
-
-    distance = jnp.abs(lax.broadcasted_iota(jnp.int32, b_blocks.shape, 1) - half_band)
-    live = distance <= b_extent[:, None, None, None]
-    b_own = b_blocks * live.astype(b_blocks.dtype)
 
     starts = ((rows - EXTRA_ROWS, REST, 0), (0, EXTRA_ROWS, rows - REST))
     sizes = (EXTRA_ROWS, rows - EXTRA_ROWS - REST, REST)
-
-    def rows_for(x, side, index):
-        start = jnp.where(side == 0, starts[0][index], starts[1][index])
-        return lax.dynamic_slice_in_dim(x, start, sizes[index], 0)
-
-    outer = to_outer_neighbour(b_own, ring)
-    across = over_rep(b_own)
-    peer = to_chip_peer(b_own, ring)
-    turned = turned_left(a_blocks, a_extent, rows_out)
-    turned_send = lax.dynamic_slice_in_dim(turned, rows_out * (1 - rep), rows_out, 0)
+    spans = list(zip(*starts))
+
+    outer = to_outer_neighbour(b_blocks, ring)
+    across = over_rep(b_blocks)
+    peer = to_chip_peer(b_blocks, ring)
+    extents = lax.all_gather(b_extent, RING, tiled=True)
+    turned, turned_send = turned_left(a_blocks, a_extent, rows_out)
     turned_across = over_rep(turned_send)
-    across = lax.optimization_barrier((across, turned_send))[0]
-    across_outer = [to_outer_neighbour(rows_for(across, rep, i), ring) for i in range(2)]
+    across, extents = lax.optimization_barrier((across, turned_send, extents))[::2]
+    across_outer = [
+        to_outer_neighbour(x, ring) for x in picked(across, spans[:2], sizes[:2])
+    ]
     across_peer = to_chip_peer(across, ring)
-    extra = to_second_neighbour(rows_for(outer, rep, 0), ring)
-    across_outer.append(over_rep(rows_for(outer, 1 - rep, 2)))
+    extra, rest = picked(outer, [spans[0], spans[2][::-1]], [sizes[0], sizes[2]])
+    extra = to_second_neighbour(extra, ring)
+    across_outer.append(over_rep(rest))
     across_extra = to_second_neighbour(across_outer[0], ring)
 
     def window_rows(rep_value, core_value):
@@ -316,30 +379,30 @@
         return where
 
     total = partial_product(
+        extents,
         turned,
-        [b_own, peer, outer, extra],
+        [b_blocks, peer, outer, extra],
         where_of({"own": 0, "peer": 1, "outer": 2, "extra": 3}),
         None,
         rows_out,
-        True,
         jnp.bfloat16,
     )
     total = partial_product(
+        extents,
         turned_across,
         [across, across_peer],
         where_of({"own": 0, "peer": 1}),
         total,
         rows_out,
-        False,
         jnp.float32,
     )
     return partial_product(
+        extents,
         turned_across,
         [*across_outer, across_extra],
         where_of({"outer": (0, 1, 2), "extra": 3}),
         total,
         rows_out,
-        False,
         None,
     )
 

time: 84.3 us -> 87.3 us (1.036)
  blocking collectives: 0 us -> 36.3 us
  waiting for transfers between devices: 39.5 us -> 8.19 us
  starting transfers between devices: 16.3 us -> 21.4 us
  local copies, waits for them, and re-layouts: 9.18 us -> 4.78 us
  Pallas kernels: 17 us -> 14.8 us
  other arithmetic: 1.65 us -> 0 us
    optimization_barrier x0 -> x1, blocking collectives: none -> 36.3 us  [local(): lax.optimization_barrier((across, turned_send, extents))[::2]]
    ppermute x3, waiting for transfers between devices: 27.5 us -> 0.01 us  [over_rep(): return lax.ppermute(x, 'rep', [(0, 1), (1, 0)])]
    dynamic_slice x5 -> x0, local copies, waits for them, and re-layouts: 9.18 us -> none  [the longest x4 6.99 us: rows_for(): return lax.dynamic_slice_in_dim(x, start, sizes[index], 0)]
    unnamed x2 -> x19, local copies, waits for them, and re-layouts: 0.01 us -> 4.78 us
    ppermute x2, waiting for transfers between devices: 6.14 us -> 1.9 us  [to_second_neighbour(): return lax.ppermute(x, EVERY, pairs)]
    ppermute x2, starting transfers between devices: 0.42 us -> 3.85 us  [to_second_neighbour(): return lax.ppermute(x, EVERY, pairs)]
    ppermute x3, starting transfers between devices: 6.77 us -> 8.85 us  [over_rep(): return lax.ppermute(x, 'rep', [(0, 1), (1, 0)])]
    pallas_call x1 -> x3, Pallas kernels: 3.18 us -> 1.43 us  [the longest x1 1.07 us: turned_left(): pl.pallas_call(functools.partial(turn_kernel, rows_out), out_shape=(shape...]
  transfers between devices with their start and end apart: 10 -> 10, of which waited for: 3 -> 2; matrix products, arithmetic and copies ran while one was open for 11% -> 1% of each run, Pallas kernels for 15% -> 12%
where the time goes in v4:
time: 87.3 us; the launch traced here: 86.4 us
  blocking collectives  36.3 us (42%)
  starting transfers between devices  21.4 us (25%)
  Pallas kernels  14.8 us (17%)
  waiting for transfers between devices  8.19 us (9%)
  local copies, waits for them, and re-layouts  4.78 us (5%)
  between operations  0.92 us (1%)
    optimization_barrier x1, blocking collectives, local(): lax.optimization_barrier((across, turned_send, extents))[::2]  36.3 us
    pallas_call x3, Pallas kernels, partial_product(): pl.pallas_call(functools.partial(product_kernel, plan), out_shape=out_sha...  13.4 us
    ppermute x3, starting transfers between devices, over_rep(): return lax.ppermute(x, 'rep', [(0, 1), (1, 0)])  8.85 us
    ppermute x3, starting transfers between devices, to_outer_neighbour(): lax.ppermute(x, RING, [(g, (g + 2 * (g % 2) - 1) % ring) for g in range(r...  8.6 us
    ppermute x3, waiting for transfers between devices, to_outer_neighbour(): lax.ppermute(x, RING, [(g, (g + 2 * (g % 2) - 1) % ring) for g in range(r...  6.28 us
    unnamed x19, local copies, waits for them, and re-layouts  4.78 us
    ppermute x2, starting transfers between devices, to_second_neighbour(): return lax.ppermute(x, EVERY, pairs)  3.85 us
    ppermute x2, waiting for transfers between devices, to_second_neighbour(): return lax.ppermute(x, EVERY, pairs)  1.9 us
  transfers between devices with their start and end apart: 10, of which 2 were waited for; matrix products, arithmetic and copies ran while one was open for 1% of the time, Pallas kernels for 12%

profile of v4, /device:TPU:0, one launch (start us, length us, event | category | flops | bytes accessed | tf_op | source)
XLA Modules:
  0.0 86.4 jit_solution(9118574855834801397)
XLA Ops:
  0.0 2.9 %collective-permute-start = (bf16[6,17,64,128]{3,2,1,0:T(8,128)(2,1)}, bf16[6,17,64,128]{3,2,1,0:T(8,128)(2,1)S(1)}, u32[]{:S(2)}, u32[]{:S(2)}) collective-permute-start(bf16[6,17,64,128]{3,2,1,0:T(8,128)(2,1)} %refs_2_.1), channel_id=1, source_target_pairs={{0,1},{1,0},{2,3},{3,2},{4,5},{5,4},{6,7},{7,6},{8,9},{9,8},{10,11... | collective-permute-start | bytes 5013512 | tf_op jit(solution)/shard_map/ppermute | solution.py:35
  2.9 3.7 %collective-permute-start.4 = (bf16[6,17,64,128]{3,2,1,0:T(8,128)(2,1)}, bf16[6,17,64,128]{3,2,1,0:T(8,128)(2,1)S(1)}, u32[]{:S(2)}, u32[]{:S(2)}) collective-permute-start(bf16[6,17,64,128]{3,2,1,0:T(8,128)(2,1)} %refs_2_.1), channel_id=1, source_target_pairs={{0,30},{2,4},{4,2},{6,8},{8,6},{10,12},{12,10},{14,16},{16,14},{18... | collective-permute-start | bytes 5013512 | tf_op jit(solution)/shard_map/ppermute | solution.py:22
  6.7 1.4 %copy-done.1 = bf16[6,17,64,128]{3,2,1,0:T(8,128)(2,1)S(1)} copy-done((bf16[6,17,64,128]{3,2,1,0:T(8,128)(2,1)S(1)}, bf16[6,17,64,128]{3,2,1,0:T(8,128)(2,1)}, u32[]{:S(2)}) %copy-start.1) | copy-done | bytes 1671192
  8.1 0.7 copy-done.4
  8.8 1.1 %shard_map.46 = (bf16[3,128,1152]{2,1,0:T(8,128)(2,1)S(1)}, bf16[3,128,1152]{2,1,0:T(8,128)(2,1)S(1)}) custom-call(s32[6]{0:T(128)S(1)} %copy-done.4, bf16[6,17,64,128]{3,2,1,0:T(8,128)(2,1)S(1)} %copy-done.1), custom_call_target="tpu_custom_call" | custom-call | tf_op jit(solution)/shard_map/pallas_call | solution.py:70
  9.9 0.9 %copy-done.2 = bf16[3,128,1152]{2,1,0:T(8,128)(2,1)} copy-done((bf16[3,128,1152]{2,1,0:T(8,128)(2,1)}, bf16[3,128,1152]{2,1,0:T(8,128)(2,1)S(1)}, u32[]{:S(2)}) %copy-start.2) | copy-done | bytes 884760
  10.8 0.9 %copy-done.5 = bf16[3,128,1152]{2,1,0:T(8,128)(2,1)} copy-done((bf16[3,128,1152]{2,1,0:T(8,128)(2,1)}, bf16[3,128,1152]{2,1,0:T(8,128)(2,1)S(1)}, u32[]{:S(2)}) %copy-start.5) | copy-done | bytes 884760
  11.7 0.6 dynamic-slice
  12.9 0.2 dynamic-update-slice
  13.2 36.3 %all-reduce.refs_0_ = s32[96]{0:T(128)S(1)} all-reduce(s32[96]{0:T(128)S(1)} %dynamic-update-slice), channel_id=1, replica_groups=mesh['row'=4,'col'=4,'rep'=2] {'row','col'}, use_global_device_ids=true, to_apply=%add | all-reduce | flops 96 | bytes 768 | tf_op jit(solution)/shard_map/optimization_barrier | solution.py:348
  49.5 0.1 collective-permute-start.7
  49.6 0.2 shard_map.47
  49.8 0.1 collective-permute-start.2
  49.9 0.6 collective-permute-start.1
  50.5 0.1 shard_map.48
  50.7 0.3 collective-permute-start.9
  50.9 4.8 %collective-permute-start.3 = (bf16[3,17,64,128]{3,2,1,0:T(8,128)(2,1)S(1)}, bf16[3,17,64,128]{3,2,1,0:T(8,128)(2,1)S(1)}, u32[]{:S(2)}, u32[]{:S(2)}) collective-permute-start(bf16[3,17,64,128]{3,2,1,0:T(8,128)(2,1)S(1)} %get-tuple-element.17), channel_id=1, source_target_pairs={{0,30},{2,4},{4,2},{6,8},{8,6},{10,12},{12,10},{14,16},{16,14},{18... | collective-permute-start | bytes 2506760 | tf_op jit(solution)/shard_map/ppermute | solution.py:22
  55.7 6.3 %collective-permute-done.2.refs_2_ = bf16[2,17,64,128]{3,2,1,0:T(8,128)(2,1)S(1)} collective-permute-done((bf16[2,17,64,128]{3,2,1,0:T(8,128)(2,1)S(1)}, bf16[2,17,64,128]{3,2,1,0:T(8,128)(2,1)S(1)}, u32[]{:S(2)}, u32[]{:S(2)}) %collective-permute-start.2) | collective-permute-done | bytes 557088 | tf_op jit(solution)/shard_map/ppermute | solution.py:22
  62.0 3.6 %collective-permute-start.6 = (bf16[2,17,64,128]{3,2,1,0:T(8,128)(2,1)S(1)}, bf16[2,17,64,128]{3,2,1,0:T(8,128)(2,1)S(1)}, u32[]{:S(2)}, u32[]{:S(2)}) collective-permute-start(bf16[2,17,64,128]{3,2,1,0:T(8,128)(2,1)S(1)} %collective-permute-done.2.refs_2_), channel_id=1, source_target_pairs={{0,2},{1,27},{2,8},{3,1},{4,6},{5,31},{6,12},{7,5},{8,10},{9,3},{1... | collective-permute-start | bytes 1671176 | tf_op jit(solution)/shard_map/ppermute | solution.py:31
  65.6 1.9 %collective-permute-done.9.refs_5_ = bf16[2,17,64,128]{3,2,1,0:T(8,128)(2,1)S(1)} collective-permute-done((bf16[2,17,64,128]{3,2,1,0:T(8,128)(2,1)S(1)}, bf16[2,17,64,128]{3,2,1,0:T(8,128)(2,1)S(1)}, u32[]{:S(2)}, u32[]{:S(2)}) %collective-permute-start.9) | collective-permute-done | bytes 557088 | tf_op jit(solution)/shard_map/ppermute | solution.py:31
  67.5 5.3 %collective-permute-start.5 = (bf16[1,17,64,128]{3,2,1,0:T(8,128)(2,1)S(1)}, bf16[1,17,64,128]{3,2,1,0:T(8,128)(2,1)S(1)}, u32[]{:S(2)}, u32[]{:S(2)}) collective-permute-start(bf16[1,17,64,128]{3,2,1,0:T(8,128)(2,1)S(1)} %get-tuple-element.18), channel_id=1, source_target_pairs={{0,1},{1,0},{2,3},{3,2},{4,5},{5,4},{6,7},{7,6},{8,9},{9,8},{10,11... | collective-permute-start | bytes 835592 | tf_op jit(solution)/shard_map/ppermute | solution.py:35
  72.8 5.8 %shard_map.49.refs_4_ = bf16[18,384,256]{2,1,0:T(8,128)(2,1)S(1)} custom-call(s32[96]{0:T(128)S(1)} %all-reduce.refs_0_, bf16[3,128,1152]{2,1,0:T(8,128)(2,1)S(1)} %copy-done.3, bf16[6,17,64,128]{3,2,1,0:T(8,128)(2,1)S(1)} %copy-done, bf16[6,17,64,128]{3,2,1,0:T(8,128)(2,1)} %collective-permute-done.8.refs_3_, ...), custom_call_target="tpu_custom_call" | custom-call | tf_op jit(solution)/shard_map/pallas_call | solution.py:322
  78.7 3.4 %shard_map.50.refs_6_ = f32[18,384,256]{2,1,0:T(8,128)S(1)} custom-call(s32[96]{0:T(128)S(1)} %all-reduce.refs_0_, bf16[3,128,1152]{2,1,0:T(8,128)(2,1)S(1)} %collective-permute-done.1.refs_1_, bf16[6,17,64,128]{3,2,1,0:T(8,128)(2,1)S(1)} %collective-permute-done.x_ref.refs_2_, bf16[6,17,64,128]{3,2,1,0:T(8,128)(2,1)S(1)} %collective-permute-done.7.refs_3_, ...), custom_call_target="tpu_custom_call" | custom-call | tf_op jit(solution)/shard_map/pallas_call | solution.py:322
  82.1 4.2 %shard_map.51 = bf16[3,33,128,128]{3,2,1,0:T(8,128)(2,1)} custom-call(s32[96]{0:T(128)S(1)} %all-reduce.refs_0_, bf16[3,128,1152]{2,1,0:T(8,128)(2,1)S(1)} %collective-permute-done.1.refs_1_, bf16[2,17,64,128]{3,2,1,0:T(8,128)(2,1)S(1)} %collective-permute-done.2.refs_2_, bf16[3,17,64,128]{3,2,1,0:T(8,128)(2,1)S(1)} %collective-permute-done.3.refs_3_, ...), custom_call_target="tpu_custom_call" | custom-call | tf_op jit(solution)/shard_map/pallas_call | solution.py:322
  (22 shorter events, 0.0 us)
Async XLA Ops:
  0.0 11.7 %copy-start.7 = (u32[32]{0:T(128)S(1)}, u32[32]{0:T(128)}, u32[]{:S(2)}) copy-start(u32[32]{0:T(128)} %constant.6) | copy-start | bytes 388
  0.0 12.9 %copy-start.6 = (s32[6]{0:T(128)S(1)}, s32[6]{0:T(128)}, u32[]{:S(2)}) copy-start(s32[6]{0:T(128)} %param.7) | copy-start | bytes 76
  0.0 49.5 %collective-permute-start = (bf16[6,17,64,128]{3,2,1,0:T(8,128)(2,1)}, bf16[6,17,64,128]{3,2,1,0:T(8,128)(2,1)S(1)}, u32[]{:S(2)}, u32[]{:S(2)}) collective-permute-start(bf16[6,17,64,128]{3,2,1,0:T(8,128)(2,1)} %refs_2_.1), channel_id=1, source_target_pairs={{0,1},{1,0},{2,3},{3,2},{4,5},{5,4},{6,7},{7,6},{8,9},{9,8},{10,11... | collective-permute-start | bytes 5013512 | tf_op jit(solution)/shard_map/ppermute | solution.py:35
  2.9 47.6 %collective-permute-start.4 = (bf16[6,17,64,128]{3,2,1,0:T(8,128)(2,1)}, bf16[6,17,64,128]{3,2,1,0:T(8,128)(2,1)S(1)}, u32[]{:S(2)}, u32[]{:S(2)}) collective-permute-start(bf16[6,17,64,128]{3,2,1,0:T(8,128)(2,1)} %refs_2_.1), channel_id=1, source_target_pairs={{0,30},{2,4},{4,2},{6,8},{8,6},{10,12},{12,10},{14,16},{16,14},{18... | collective-permute-start | bytes 5013512 | tf_op jit(solution)/shard_map/ppermute | solution.py:22
  6.7 44.2 %collective-permute-start.8 = (bf16[6,17,64,128]{3,2,1,0:T(8,128)(2,1)}, bf16[6,17,64,128]{3,2,1,0:T(8,128)(2,1)}, u32[]{:S(2)}, u32[]{:S(2)}) collective-permute-start(bf16[6,17,64,128]{3,2,1,0:T(8,128)(2,1)} %refs_2_.1), channel_id=1, source_target_pairs={{0,2},{2,0},{4,6},{6,4},{8,10},{10,8},{12,14},{14,12},{16,18},{18,... | collective-permute-start | bytes 5013512 | tf_op jit(solution)/shard_map/ppermute | solution.py:18
  6.7 1.4 %copy-start.1 = (bf16[6,17,64,128]{3,2,1,0:T(8,128)(2,1)S(1)}, bf16[6,17,64,128]{3,2,1,0:T(8,128)(2,1)}, u32[]{:S(2)}) copy-start(bf16[6,17,64,128]{3,2,1,0:T(8,128)(2,1)} %a_ref.1) | copy-start | bytes 5013508
  8.1 0.7 copy-start.4
  9.8 0.9 %copy-start.2 = (bf16[3,128,1152]{2,1,0:T(8,128)(2,1)}, bf16[3,128,1152]{2,1,0:T(8,128)(2,1)S(1)}, u32[]{:S(2)}) copy-start(bf16[3,128,1152]{2,1,0:T(8,128)(2,1)S(1)} %get-tuple-element.19.refs_1_) | copy-start | bytes 2654212
  10.8 0.9 %copy-start.5 = (bf16[3,128,1152]{2,1,0:T(8,128)(2,1)}, bf16[3,128,1152]{2,1,0:T(8,128)(2,1)S(1)}, u32[]{:S(2)}) copy-start(bf16[3,128,1152]{2,1,0:T(8,128)(2,1)S(1)} %get-tuple-element.13) | copy-start | bytes 2654212
  49.5 23.3 %copy-start = (bf16[6,17,64,128]{3,2,1,0:T(8,128)(2,1)S(1)}, bf16[6,17,64,128]{3,2,1,0:T(8,128)(2,1)}, u32[]{:S(2)}) copy-start(bf16[6,17,64,128]{3,2,1,0:T(8,128)(2,1)} %refs_2_.1) | copy-start | bytes 5013508
  49.5 23.3 %copy-start.3 = (bf16[3,128,1152]{2,1,0:T(8,128)(2,1)S(1)}, bf16[3,128,1152]{2,1,0:T(8,128)(2,1)}, u32[]{:S(2)}) copy-start(bf16[3,128,1152]{2,1,0:T(8,128)(2,1)} %copy-done.2) | copy-start | bytes 2654212
  49.5 29.1 %collective-permute-start.7 = (bf16[6,17,64,128]{3,2,1,0:T(8,128)(2,1)S(1)}, bf16[6,17,64,128]{3,2,1,0:T(8,128)(2,1)S(1)}, u32[]{:S(2)}, u32[]{:S(2)}) collective-permute-start(bf16[6,17,64,128]{3,2,1,0:T(8,128)(2,1)S(1)} %collective-permute-done.x_ref.refs_2_), channel_id=1, source_target_pairs={{0,2},{2,0},{4,6},{6,4},{8,10},{10,8},{12,14},{14,12},{16,18},{18,... | collective-permute-start | bytes 5013512 | tf_op jit(solution)/shard_map/ppermute | solution.py:18
  49.8 12.2 %collective-permute-start.2 = (bf16[2,17,64,128]{3,2,1,0:T(8,128)(2,1)S(1)}, bf16[2,17,64,128]{3,2,1,0:T(8,128)(2,1)S(1)}, u32[]{:S(2)}, u32[]{:S(2)}) collective-permute-start(bf16[2,17,64,128]{3,2,1,0:T(8,128)(2,1)S(1)} %get-tuple-element.16), channel_id=1, source_target_pairs={{0,30},{2,4},{4,2},{6,8},{8,6},{10,12},{12,10},{14,16},{16,14},{18... | collective-permute-start | bytes 1671176 | tf_op jit(solution)/shard_map/ppermute | solution.py:22
  49.9 28.7 %collective-permute-start.1 = (bf16[3,128,1152]{2,1,0:T(8,128)(2,1)}, bf16[3,128,1152]{2,1,0:T(8,128)(2,1)S(1)}, u32[]{:S(2)}, u32[]{:S(2)}) collective-permute-start(bf16[3,128,1152]{2,1,0:T(8,128)(2,1)} %copy-done.5), channel_id=1, source_target_pairs={{0,1},{1,0},{2,3},{3,2},{4,5},{5,4},{6,7},{7,6},{8,9},{9,8},{10,11... | collective-permute-start | bytes 2654216 | tf_op jit(solution)/shard_map/ppermute | solution.py:35
  50.7 16.8 %collective-permute-start.9 = (bf16[2,17,64,128]{3,2,1,0:T(8,128)(2,1)S(1)}, bf16[2,17,64,128]{3,2,1,0:T(8,128)(2,1)S(1)}, u32[]{:S(2)}, u32[]{:S(2)}) collective-permute-start(bf16[2,17,64,128]{3,2,1,0:T(8,128)(2,1)S(1)} %get-tuple-element.20), channel_id=1, source_target_pairs={{0,2},{1,27},{2,8},{3,1},{4,6},{5,31},{6,12},{7,5},{8,10},{9,3},{1... | collective-permute-start | bytes 1671176 | tf_op jit(solution)/shard_map/ppermute | solution.py:31
  50.9 31.1 %collective-permute-start.3 = (bf16[3,17,64,128]{3,2,1,0:T(8,128)(2,1)S(1)}, bf16[3,17,64,128]{3,2,1,0:T(8,128)(2,1)S(1)}, u32[]{:S(2)}, u32[]{:S(2)}) collective-permute-start(bf16[3,17,64,128]{3,2,1,0:T(8,128)(2,1)S(1)} %get-tuple-element.17), channel_id=1, source_target_pairs={{0,30},{2,4},{4,2},{6,8},{8,6},{10,12},{12,10},{14,16},{16,14},{18... | collective-permute-start | bytes 2506760 | tf_op jit(solution)/shard_map/ppermute | solution.py:22
  62.0 20.1 %collective-permute-start.6 = (bf16[2,17,64,128]{3,2,1,0:T(8,128)(2,1)S(1)}, bf16[2,17,64,128]{3,2,1,0:T(8,128)(2,1)S(1)}, u32[]{:S(2)}, u32[]{:S(2)}) collective-permute-start(bf16[2,17,64,128]{3,2,1,0:T(8,128)(2,1)S(1)} %collective-permute-done.2.refs_2_), channel_id=1, source_target_pairs={{0,2},{1,27},{2,8},{3,1},{4,6},{5,31},{6,12},{7,5},{8,10},{9,3},{1... | collective-permute-start | bytes 1671176 | tf_op jit(solution)/shard_map/ppermute | solution.py:31
  67.5 14.5 %collective-permute-start.5 = (bf16[1,17,64,128]{3,2,1,0:T(8,128)(2,1)S(1)}, bf16[1,17,64,128]{3,2,1,0:T(8,128)(2,1)S(1)}, u32[]{:S(2)}, u32[]{:S(2)}) collective-permute-start(bf16[1,17,64,128]{3,2,1,0:T(8,128)(2,1)S(1)} %get-tuple-element.18), channel_id=1, source_target_pairs={{0,1},{1,0},{2,3},{3,2},{4,5},{5,4},{6,7},{7,6},{8,9},{9,8},{10,11... | collective-permute-start | bytes 835592 | tf_op jit(solution)/shard_map/ppermute | solution.py:35

commit v5 on v4

--- a/solution.py
+++ b/solution.py
@@ -80,37 +80,60 @@
     )(a_extent, a_blocks)
 
 
-def pick_kernel(spans, x_ref, *refs):
-    out_refs, sem = refs[:-1], refs[-1]
+def clear_absent(ref, at, extent, band):
+    half_band = (band - 1) // 2
+
+    def clear(offset, carry):
+        for b in (offset, band - 1 - offset):
+            ref[at(b)] = jnp.zeros(ref.shape[-2:], ref.dtype)
+        return carry
+
+    lax.fori_loop(0, half_band - extent, clear, 0)
+
+
+def pick_kernel(spans, masks, *refs):
+    refs = list(refs)
+    extent_ref = refs.pop(0) if masks else None
+    x_ref, out_refs, sem = refs[0], refs[1:-1], refs[-1]
     rep = lax.axis_index("rep")
+    starts = [jnp.where(rep == 0, low, high) for low, high in spans]
 
     def copies():
         return [
-            pltpu.make_async_copy(
-                x_ref.at[pl.ds(jnp.where(rep == 0, low, high), out_ref.shape[0])],
-                out_ref,
-                sem.at[i],
-            )
-            for i, ((low, high), out_ref) in enumerate(zip(spans, out_refs))
+            pltpu.make_async_copy(x_ref.at[pl.ds(start, out_ref.shape[0])], out_ref, sem.at[i])
+            for i, (start, out_ref) in enumerate(zip(starts, out_refs))
         ]
 
     for copy in copies():
         copy.start()
     for copy in copies():
         copy.wait()
-
-
-def picked(x, spans, sizes):
+    if masks:
+        for start, out_ref in zip(starts, out_refs):
+            for row in range(out_ref.shape[0]):
+                clear_absent(
+                    out_ref, lambda b, row=row: (row, b), extent_ref[start + row], out_ref.shape[1]
+                )
+
+
+def picked(x, spans, sizes, extents=None):
+    masks = extents is not None
     shapes = [jax.ShapeDtypeStruct((size, *x.shape[1:]), x.dtype) for size in sizes]
+    out_space = pltpu.VMEM if masks else pl.ANY
+    in_specs = [pl.BlockSpec(memory_space=pltpu.SMEM)] if masks else []
     return pl.pallas_call(
-        functools.partial(pick_kernel, spans),
+        functools.partial(pick_kernel, spans, masks),
         out_shape=shapes,
-        in_specs=[pl.BlockSpec(memory_space=pl.ANY)],
-        out_specs=[pl.BlockSpec(memory_space=pl.ANY)] * len(sizes),
+        in_specs=in_specs + [pl.BlockSpec(memory_space=pl.ANY)],
+        out_specs=[pl.BlockSpec(memory_space=out_space)] * len(sizes),
         scratch_shapes=[pltpu.SemaphoreType.DMA((len(sizes),))],
-        compiler_params=pltpu.CompilerParams(vmem_limit_bytes=2**20),
+        compiler_params=pltpu.CompilerParams(vmem_limit_bytes=(4 if masks else 1) * 2**20),
         cost_estimate=pl.CostEstimate(flops=0, bytes_accessed=0, transcendentals=0),
-    )(x)
+    )(*([extents] if masks else []), x)
+
+
+def after(x, *others):
+    return lax.optimization_barrier((x, *others))[0]
 
 
 def first_slot(rep_value, row):
@@ -119,7 +142,7 @@
 
 def product_kernel(plan, *refs):
     refs = list(refs)
-    extent_ref = refs.pop(0)
+    extent_ref = refs.pop(0) if plan["masked_source"] is not None else None
     turned_ref = refs.pop(0)
     source_refs = [refs.pop(0) for _ in range(plan["sources"])]
     partial_ref = refs.pop(0) if plan["partial"] else None
@@ -130,7 +153,6 @@
     band, rows_out = plan["band"], plan["rows_out"]
     columns, slots, depth, block = window.shape
     pairs = columns // 2
-    half_band = (band - 1) // 2
     reach = (band + 1) * depth
     width = slots * depth
     rep = lax.axis_index("rep")
@@ -224,36 +246,24 @@
             def _(rep_value=rep_value, core_value=core_value):
                 place_rows(plan["where"](rep_value, core_value))
 
-    def blank_absent(slot):
-        row_count = extent_ref.shape[0]
-        rows = 2 * rows_out
-        group = lax.axis_index("row") * lax.axis_size("col") + lax.axis_index("col")
-        place = group * rows + slot - half_band + rep * (half_band - rows)
-        extent = extent_ref[lax.rem(place + row_count, row_count)]
-        blank = jnp.zeros((depth, block), window.dtype)
-
-        def clear(offset, carry):
-            window[slot + offset, slot] = blank
-            window[slot + band - 1 - offset, slot] = blank
-            return carry
-
-        lax.fori_loop(0, half_band - extent, clear, 0)
-
     for row in range(rows_out):
         left_copy(row, 0).wait()
     for index in range(plan["taken"]):
         row_copy(source_refs[0], 0, 0, index).wait()
-    if plan["taken"] == slots:
-        for slot in range(slots):
-            blank_absent(slot)
-    else:
+    if extent_ref is not None:
         for rep_value in range(2):
             for core_value in range(2):
 
                 @pl.when((rep == rep_value) & (core == core_value))
                 def _(rep_value=rep_value, core_value=core_value):
-                    for slot, _, _ in plan["where"](rep_value, core_value):
-                        blank_absent(slot)
+                    for slot, source, position in plan["where"](rep_value, core_value):
+                        if source == plan["masked_source"]:
+                            clear_absent(
+                                window,
+                                lambda b, slot=slot: (slot + b, slot),
+                                extent_ref[position],
+                                band,
+                            )
 
     parts = [range(pairs)]
     if final:
@@ -282,7 +292,7 @@
                 out_copy(half, row).wait()
 
 
-def partial_product(extents, turned, sources, where, partial, rows_out, kind):
+def partial_product(turned, sources, where, partial, rows_out, kind, masked=None):
     band, depth, block = sources[0].shape[1:]
     slots = rows_out + band
     columns = slots + band - 1
@@ -296,10 +306,13 @@
         "rows_out": rows_out,
         "partial": partial is not None,
         "final": final,
+        "masked_source": None if masked is None else masked[0],
     }
-    operands = [extents, turned, *sources]
-    in_specs = [pl.BlockSpec(memory_space=pltpu.SMEM)]
-    in_specs += [pl.BlockSpec(memory_space=pl.ANY)] * (1 + len(sources))
+    operands = [turned, *sources]
+    in_specs = [pl.BlockSpec(memory_space=pl.ANY)] * len(operands)
+    if masked is not None:
+        operands.insert(0, masked[1])
+        in_specs.insert(0, pl.BlockSpec(memory_space=pltpu.SMEM))
     if partial is not None:
         operands.append(partial)
         in_specs.append(pl.BlockSpec(memory_space=pltpu.VMEM))
@@ -339,21 +352,27 @@
     sizes = (EXTRA_ROWS, rows - EXTRA_ROWS - REST, REST)
     spans = list(zip(*starts))
 
+    half_band = (band - 1) // 2
+    distance = jnp.abs(lax.broadcasted_iota(jnp.int32, b_blocks.shape, 1) - half_band)
+    live = distance <= b_extent[:, None, None, None]
+
     outer = to_outer_neighbour(b_blocks, ring)
+    outer_extent = to_outer_neighbour(b_extent, ring)
+    b_own = b_blocks * live.astype(b_blocks.dtype)
     across = over_rep(b_blocks)
-    peer = to_chip_peer(b_blocks, ring)
-    extents = lax.all_gather(b_extent, RING, tiled=True)
+    peer = to_chip_peer(b_own, ring)
     turned, turned_send = turned_left(a_blocks, a_extent, rows_out)
     turned_across = over_rep(turned_send)
-    across, extents = lax.optimization_barrier((across, turned_send, extents))[::2]
-    across_outer = [
-        to_outer_neighbour(x, ring) for x in picked(across, spans[:2], sizes[:2])
-    ]
-    across_peer = to_chip_peer(across, ring)
-    extra, rest = picked(outer, [spans[0], spans[2][::-1]], [sizes[0], sizes[2]])
+    across = after(across, turned_send, outer_extent)
+    *onward, across = picked(across, [*spans[:2], (0, 0)], [*sizes[:2], rows], b_extent)
+    across_outer = [to_outer_neighbour(x, ring) for x in onward]
+    extra, rest = picked(
+        outer, [spans[0], spans[2][::-1]], [sizes[0], sizes[2]], outer_extent
+    )
     extra = to_second_neighbour(extra, ring)
     across_outer.append(over_rep(rest))
     across_extra = to_second_neighbour(across_outer[0], ring)
+    across_peer = to_chip_peer(across, ring)
 
     def window_rows(rep_value, core_value):
         sides = ("outer", "peer") if core_value == 0 else ("peer", "outer")
@@ -379,16 +398,15 @@
         return where
 
     total = partial_product(
-        extents,
         turned,
-        [b_blocks, peer, outer, extra],
+        [b_own, peer, outer, extra],
         where_of({"own": 0, "peer": 1, "outer": 2, "extra": 3}),
         None,
         rows_out,
         jnp.bfloat16,
+        (2, outer_extent),
     )
     total = partial_product(
-        extents,
         turned_across,
         [across, across_peer],
         where_of({"own": 0, "peer": 1}),
@@ -397,7 +415,6 @@
         jnp.float32,
     )
     return partial_product(
-        extents,
         turned_across,
         [*across_outer, across_extra],
         where_of({"outer": (0, 1, 2), "extra": 3}),

time: 87.3 us -> 80.5 us (0.922)
  waiting for transfers between devices: 8.19 us -> 47.6 us
  blocking collectives: 36.3 us -> 0 us
  local copies, waits for them, and re-layouts: 4.78 us -> 0.01 us
  starting transfers between devices: 21.4 us -> 17.4 us
  other arithmetic: 0 us -> 1.78 us
  Pallas kernels: 14.8 us -> 13.3 us
    optimization_barrier x1 -> x0, blocking collectives: 36.3 us -> none  [local(): lax.optimization_barrier((across, turned_send, extents))[::2]]
    ppermute x3 -> x4, waiting for transfers between devices: 6.28 us -> 29 us  [to_outer_neighbour(): lax.ppermute(x, RING, [(g, (g + 2 * (g % 2) - 1) % ring) for g in range(r...]
    ppermute x3, waiting for transfers between devices: 0.01 us -> 12.7 us  [over_rep(): return lax.ppermute(x, 'rep', [(0, 1), (1, 0)])]
    ppermute x3, starting transfers between devices: 8.85 us -> 3.64 us  [over_rep(): return lax.ppermute(x, 'rep', [(0, 1), (1, 0)])]
    unnamed x19 -> x6, local copies, waits for them, and re-layouts: 4.78 us -> 0.01 us
    ppermute x2, waiting for transfers between devices: 1.9 us -> 5.93 us  [to_second_neighbour(): return lax.ppermute(x, EVERY, pairs)]
    pallas_call x3, Pallas kernels: 13.4 us -> 9.96 us  [partial_product(): pl.pallas_call(functools.partial(product_kernel, plan), out_shape=out_sha...]
    ppermute x2, starting transfers between devices: 0.07 us -> 2.42 us  [to_chip_peer(): return lax.ppermute(x, RING, [(g, g ^ 1) for g in range(ring)])]
  transfers between devices with their start and end apart: 10 -> 11, of which waited for: 2 -> 6; matrix products, arithmetic and copies ran while one was open for 1% -> 2% of each run, Pallas kernels for 12% -> 13%
where the time goes in v5:
time: 80.5 us
  waiting for transfers between devices  47.6 us (59%)
  starting transfers between devices  17.4 us (22%)
  Pallas kernels  13.3 us (17%)
  other arithmetic  1.78 us (2%)
    ppermute x4, waiting for transfers between devices, to_outer_neighbour(): lax.ppermute(x, RING, [(g, (g + 2 * (g % 2) - 1) % ring) for g in range(r...  29 us
    ppermute x3, waiting for transfers between devices, over_rep(): return lax.ppermute(x, 'rep', [(0, 1), (1, 0)])  12.7 us
    pallas_call x3, Pallas kernels, partial_product(): pl.pallas_call(functools.partial(product_kernel, plan), out_shape=out_sha...  9.96 us
    ppermute x4, starting transfers between devices, to_outer_neighbour(): lax.ppermute(x, RING, [(g, (g + 2 * (g % 2) - 1) % ring) for g in range(r...  9.46 us
    ppermute x2, waiting for transfers between devices, to_second_neighbour(): return lax.ppermute(x, EVERY, pairs)  5.93 us
    ppermute x3, starting transfers between devices, over_rep(): return lax.ppermute(x, 'rep', [(0, 1), (1, 0)])  3.64 us
    ppermute x2, starting transfers between devices, to_chip_peer(): return lax.ppermute(x, RING, [(g, g ^ 1) for g in range(ring)])  2.42 us
    pallas_call x2, Pallas kernels, picked(): pl.pallas_call(functools.partial(pick_kernel, spans, masks), out_shape=sh...  2.27 us
  transfers between devices with their start and end apart: 11, of which 6 were waited for; matrix products, arithmetic and copies ran while one was open for 2% of the time, Pallas kernels for 13%

profile of v5, /device:TPU:0, one launch (start us, length us, event | category | flops | bytes accessed | tf_op | source)
XLA Modules:
  0.0 80.5 jit_solution(16124824916596292811)
XLA Ops:
  0.0 2.9 %collective-permute-start.1 = (bf16[6,17,64,128]{3,2,1,0:T(8,128)(2,1)}, bf16[6,17,64,128]{3,2,1,0:T(8,128)(2,1)S(1)}, u32[]{:S(2)}, u32[]{:S(2)}) collective-permute-start(bf16[6,17,64,128]{3,2,1,0:T(8,128)(2,1)} %param.5), channel_id=1, source_target_pairs={{0,1},{1,0},{2,3},{3,2},{4,5},{5,4},{6,7},{7,6},{8,9},{9,8},{10,11... | collective-permute-start | bytes 5013512 | tf_op jit(solution)/shard_map/ppermute | solution.py:35
  2.9 3.7 %collective-permute-start.5 = (bf16[6,17,64,128]{3,2,1,0:T(8,128)(2,1)}, bf16[6,17,64,128]{3,2,1,0:T(8,128)(2,1)S(1)}, u32[]{:S(2)}, u32[]{:S(2)}) collective-permute-start(bf16[6,17,64,128]{3,2,1,0:T(8,128)(2,1)} %param.5), channel_id=1, source_target_pairs={{0,30},{2,4},{4,2},{6,8},{8,6},{10,12},{12,10},{14,16},{16,14},{18... | collective-permute-start | bytes 5013512 | tf_op jit(solution)/shard_map/ppermute | solution.py:22
  6.7 1.8 %compare_select_fusion.refs_2_ = bf16[6,17,64,128]{3,2,1,0:T(8,128)(2,1)S(1)} fusion(bf16[6,17,64,128]{3,2,1,0:T(8,128)(2,1)} %param.5, s32[6]{0:T(128)} %refs_0_.1, s32[17]{0:T(128)S(1)} %add_abs_fusion), kind=kLoop, calls=%fused_computation | loop fusion | flops 1671168 | bytes 3342428 | tf_op jit(solution)/shard_map/mul | solution.py:361
  8.5 0.1 collective-permute-start.9
  8.5 1.0 %collective-permute-start.2 = (s32[6]{0:T(128)S(1)}, s32[6]{0:T(128)S(1)}, u32[]{:S(2)}, u32[]{:S(2)}) collective-permute-start(s32[6]{0:T(128)S(1)} %copy-done.1), channel_id=1, source_target_pairs={{0,30},{2,4},{4,2},{6,8},{8,6},{10,12},{12,10},{14,16},{16,14},{18... | collective-permute-start | bytes 80 | tf_op jit(solution)/shard_map/ppermute | solution.py:22
  9.5 1.1 %shard_map.46 = (bf16[3,128,1152]{2,1,0:T(8,128)(2,1)S(1)}, bf16[3,128,1152]{2,1,0:T(8,128)(2,1)S(1)}) custom-call(s32[6]{0:T(128)S(1)} %copy-done.2, bf16[6,17,64,128]{3,2,1,0:T(8,128)(2,1)S(1)} %copy-done), custom_call_target="tpu_custom_call" | custom-call | tf_op jit(solution)/shard_map/pallas_call | solution.py:70
  10.6 16.3 %collective-permute-done.2.refs_0_ = s32[6]{0:T(128)S(1)} collective-permute-done((s32[6]{0:T(128)S(1)}, s32[6]{0:T(128)S(1)}, u32[]{:S(2)}, u32[]{:S(2)}) %collective-permute-start.2) | collective-permute-done | bytes 56 | tf_op jit(solution)/shard_map/ppermute | solution.py:22
  26.9 12.7 %collective-permute-done.1.refs_1_ = bf16[6,17,64,128]{3,2,1,0:T(8,128)(2,1)S(1)} collective-permute-done((bf16[6,17,64,128]{3,2,1,0:T(8,128)(2,1)}, bf16[6,17,64,128]{3,2,1,0:T(8,128)(2,1)S(1)}, u32[]{:S(2)}, u32[]{:S(2)}) %collective-permute-start.1) | collective-permute-done | bytes 1671200 | tf_op jit(solution)/shard_map/ppermute | solution.py:35
  39.6 1.5 %shard_map.47 = (bf16[2,17,64,128]{3,2,1,0:T(8,128)(2,1)S(1)}, bf16[3,17,64,128]{3,2,1,0:T(8,128)(2,1)S(1)}, bf16[6,17,64,128]{3,2,1,0:T(8,128)(2,1)S(1)}) custom-call(s32[6]{0:T(128)S(1)} %copy-done.1, bf16[6,17,64,128]{3,2,1,0:T(8,128)(2,1)S(1)} %collective-permute-done.1.refs_1_), custom_call_target="tpu_custom_call" | custom-call | tf_op jit(solution)/shard_map/pallas_call | solution.py:124
  41.1 2.4 %collective-permute-start.8 = (bf16[6,17,64,128]{3,2,1,0:T(8,128)(2,1)S(1)}, bf16[6,17,64,128]{3,2,1,0:T(8,128)(2,1)S(1)}, u32[]{:S(2)}, u32[]{:S(2)}) collective-permute-start(bf16[6,17,64,128]{3,2,1,0:T(8,128)(2,1)S(1)} %get-tuple-element.18.refs_1_), channel_id=1, source_target_pairs={{0,2},{2,0},{4,6},{6,4},{8,10},{10,8},{12,14},{14,12},{16,18},{18,... | collective-permute-start | bytes 5013512 | tf_op jit(solution)/shard_map/ppermute | solution.py:18
  43.5 4.7 %collective-permute-start.3 = (bf16[2,17,64,128]{3,2,1,0:T(8,128)(2,1)S(1)}, bf16[2,17,64,128]{3,2,1,0:T(8,128)(2,1)S(1)}, u32[]{:S(2)}, u32[]{:S(2)}) collective-permute-start(bf16[2,17,64,128]{3,2,1,0:T(8,128)(2,1)S(1)} %get-tuple-element.15), channel_id=1, source_target_pairs={{0,30},{2,4},{4,2},{6,8},{8,6},{10,12},{12,10},{14,16},{16,14},{18... | collective-permute-start | bytes 1671176 | tf_op jit(solution)/shard_map/ppermute | solution.py:22
  48.2 0.5 collective-permute-start
  48.7 0.8 shard_map.48
  49.5 0.1 collective-permute-start.10
  49.6 0.1 collective-permute-start.4
  49.7 10.7 %collective-permute-done.3.refs_1_ = bf16[2,17,64,128]{3,2,1,0:T(8,128)(2,1)S(1)} collective-permute-done((bf16[2,17,64,128]{3,2,1,0:T(8,128)(2,1)S(1)}, bf16[2,17,64,128]{3,2,1,0:T(8,128)(2,1)S(1)}, u32[]{:S(2)}, u32[]{:S(2)}) %collective-permute-start.3) | collective-permute-done | bytes 557088 | tf_op jit(solution)/shard_map/ppermute | solution.py:22
  60.4 1.8 %collective-permute-start.7 = (bf16[2,17,64,128]{3,2,1,0:T(8,128)(2,1)S(1)}, bf16[2,17,64,128]{3,2,1,0:T(8,128)(2,1)S(1)}, u32[]{:S(2)}, u32[]{:S(2)}) collective-permute-start(bf16[2,17,64,128]{3,2,1,0:T(8,128)(2,1)S(1)} %collective-permute-done.3.refs_1_), channel_id=1, source_target_pairs={{0,2},{1,27},{2,8},{3,1},{4,6},{5,31},{6,12},{7,5},{8,10},{9,3},{1... | collective-permute-start | bytes 1671176 | tf_op jit(solution)/shard_map/ppermute | solution.py:31
  62.2 4.2 %collective-permute-done.10.refs_5_ = bf16[2,17,64,128]{3,2,1,0:T(8,128)(2,1)S(1)} collective-permute-done((bf16[2,17,64,128]{3,2,1,0:T(8,128)(2,1)S(1)}, bf16[2,17,64,128]{3,2,1,0:T(8,128)(2,1)S(1)}, u32[]{:S(2)}, u32[]{:S(2)}) %collective-permute-start.10) | collective-permute-done | bytes 557088 | tf_op jit(solution)/shard_map/ppermute | solution.py:31
  66.4 0.2 collective-permute-start.6
  66.6 4.3 %shard_map.49.refs_3_ = bf16[18,384,256]{2,1,0:T(8,128)(2,1)S(1)} custom-call(s32[6]{0:T(128)S(1)} %collective-permute-done.2.refs_0_, bf16[3,128,1152]{2,1,0:T(8,128)(2,1)S(1)} %get-tuple-element.19.refs_1_, bf16[6,17,64,128]{3,2,1,0:T(8,128)(2,1)S(1)} %compare_select_fusion.refs_2_, bf16[6,17,64,128]{3,2,1,0:T(8,128)(2,1)S(1)} %collective-permute-done.9.refs_3_, ...), custom_call_target="tpu_custom_call" | custom-call | tf_op jit(solution)/shard_map/pallas_call | solution.py:335
  70.9 2.5 %shard_map.50.refs_5_ = f32[18,384,256]{2,1,0:T(8,128)S(1)} custom-call(bf16[3,128,1152]{2,1,0:T(8,128)(2,1)S(1)} %collective-permute-done.refs_0_, bf16[6,17,64,128]{3,2,1,0:T(8,128)(2,1)S(1)} %get-tuple-element.18.refs_1_, bf16[6,17,64,128]{3,2,1,0:T(8,128)(2,1)S(1)} %collective-permute-done.8.refs_2_, bf16[18,384,256]{2,1,0:T(8,128)(2,1)S(1)} %shard_map.49.refs_3_), custom_call_target="tpu_custom_call" | custom-call | tf_op jit(solution)/shard_map/pallas_call | solution.py:335
  73.4 2.0 %collective-permute-done.4.refs_2_ = bf16[3,17,64,128]{3,2,1,0:T(8,128)(2,1)S(1)} collective-permute-done((bf16[3,17,64,128]{3,2,1,0:T(8,128)(2,1)S(1)}, bf16[3,17,64,128]{3,2,1,0:T(8,128)(2,1)S(1)}, u32[]{:S(2)}, u32[]{:S(2)}) %collective-permute-start.4) | collective-permute-done | bytes 835616 | tf_op jit(solution)/shard_map/ppermute | solution.py:22
  75.3 1.8 %collective-permute-done.7.refs_4_ = bf16[2,17,64,128]{3,2,1,0:T(8,128)(2,1)S(1)} collective-permute-done((bf16[2,17,64,128]{3,2,1,0:T(8,128)(2,1)S(1)}, bf16[2,17,64,128]{3,2,1,0:T(8,128)(2,1)S(1)}, u32[]{:S(2)}, u32[]{:S(2)}) %collective-permute-start.7) | collective-permute-done | bytes 557088 | tf_op jit(solution)/shard_map/ppermute | solution.py:31
  77.1 3.2 %shard_map.51 = bf16[3,33,128,128]{3,2,1,0:T(8,128)(2,1)} custom-call(bf16[3,128,1152]{2,1,0:T(8,128)(2,1)S(1)} %collective-permute-done.refs_0_, bf16[2,17,64,128]{3,2,1,0:T(8,128)(2,1)S(1)} %collective-permute-done.3.refs_1_, bf16[3,17,64,128]{3,2,1,0:T(8,128)(2,1)S(1)} %collective-permute-done.4.refs_2_, ...), custom_call_target="tpu_custom_call" | custom-call | tf_op jit(solution)/shard_map/pallas_call | solution.py:335
  (12 shorter events, 0.0 us)
Async XLA Ops:
  0.0 39.6 %collective-permute-start.1 = (bf16[6,17,64,128]{3,2,1,0:T(8,128)(2,1)}, bf16[6,17,64,128]{3,2,1,0:T(8,128)(2,1)S(1)}, u32[]{:S(2)}, u32[]{:S(2)}) collective-permute-start(bf16[6,17,64,128]{3,2,1,0:T(8,128)(2,1)} %param.5), channel_id=1, source_target_pairs={{0,1},{1,0},{2,3},{3,2},{4,5},{5,4},{6,7},{7,6},{8,9},{9,8},{10,11... | collective-permute-start | bytes 5013512 | tf_op jit(solution)/shard_map/ppermute | solution.py:35
  2.9 45.8 %collective-permute-start.5 = (bf16[6,17,64,128]{3,2,1,0:T(8,128)(2,1)}, bf16[6,17,64,128]{3,2,1,0:T(8,128)(2,1)S(1)}, u32[]{:S(2)}, u32[]{:S(2)}) collective-permute-start(bf16[6,17,64,128]{3,2,1,0:T(8,128)(2,1)} %param.5), channel_id=1, source_target_pairs={{0,30},{2,4},{4,2},{6,8},{8,6},{10,12},{12,10},{14,16},{16,14},{18... | collective-permute-start | bytes 5013512 | tf_op jit(solution)/shard_map/ppermute | solution.py:22
  6.7 1.9 %copy-start.1 = (s32[6]{0:T(128)S(1)}, s32[6]{0:T(128)}, u32[]{:S(2)}) copy-start(s32[6]{0:T(128)} %refs_0_.1) | copy-start | bytes 76
  6.7 2.8 %copy-start = (bf16[6,17,64,128]{3,2,1,0:T(8,128)(2,1)S(1)}, bf16[6,17,64,128]{3,2,1,0:T(8,128)(2,1)}, u32[]{:S(2)}) copy-start(bf16[6,17,64,128]{3,2,1,0:T(8,128)(2,1)} %a_ref.1) | copy-start | bytes 5013508
  6.7 2.8 %copy-start.2 = (s32[6]{0:T(128)S(1)}, s32[6]{0:T(128)}, u32[]{:S(2)}) copy-start(s32[6]{0:T(128)} %extent_ref.1) | copy-start | bytes 76
  8.5 41.2 %collective-permute-start.9 = (bf16[6,17,64,128]{3,2,1,0:T(8,128)(2,1)S(1)}, bf16[6,17,64,128]{3,2,1,0:T(8,128)(2,1)S(1)}, u32[]{:S(2)}, u32[]{:S(2)}) collective-permute-start(bf16[6,17,64,128]{3,2,1,0:T(8,128)(2,1)S(1)} %compare_select_fusion.refs_2_), channel_id=1, source_target_pairs={{0,2},{2,0},{4,6},{6,4},{8,10},{10,8},{12,14},{14,12},{16,18},{18,... | collective-permute-start | bytes 5013512 | tf_op jit(solution)/shard_map/ppermute | solution.py:18
  8.5 18.4 %collective-permute-start.2 = (s32[6]{0:T(128)S(1)}, s32[6]{0:T(128)S(1)}, u32[]{:S(2)}, u32[]{:S(2)}) collective-permute-start(s32[6]{0:T(128)S(1)} %copy-done.1), channel_id=1, source_target_pairs={{0,30},{2,4},{4,2},{6,8},{8,6},{10,12},{12,10},{14,16},{16,14},{18... | collective-permute-start | bytes 80 | tf_op jit(solution)/shard_map/ppermute | solution.py:22
  41.1 29.7 %collective-permute-start.8 = (bf16[6,17,64,128]{3,2,1,0:T(8,128)(2,1)S(1)}, bf16[6,17,64,128]{3,2,1,0:T(8,128)(2,1)S(1)}, u32[]{:S(2)}, u32[]{:S(2)}) collective-permute-start(bf16[6,17,64,128]{3,2,1,0:T(8,128)(2,1)S(1)} %get-tuple-element.18.refs_1_), channel_id=1, source_target_pairs={{0,2},{2,0},{4,6},{6,4},{8,10},{10,8},{12,14},{14,12},{16,18},{18,... | collective-permute-start | bytes 5013512 | tf_op jit(solution)/shard_map/ppermute | solution.py:18
  43.5 16.9 %collective-permute-start.3 = (bf16[2,17,64,128]{3,2,1,0:T(8,128)(2,1)S(1)}, bf16[2,17,64,128]{3,2,1,0:T(8,128)(2,1)S(1)}, u32[]{:S(2)}, u32[]{:S(2)}) collective-permute-start(bf16[2,17,64,128]{3,2,1,0:T(8,128)(2,1)S(1)} %get-tuple-element.15), channel_id=1, source_target_pairs={{0,30},{2,4},{4,2},{6,8},{8,6},{10,12},{12,10},{14,16},{16,14},{18... | collective-permute-start | bytes 1671176 | tf_op jit(solution)/shard_map/ppermute | solution.py:22
  48.2 22.6 %collective-permute-start = (bf16[3,128,1152]{2,1,0:T(8,128)(2,1)S(1)}, bf16[3,128,1152]{2,1,0:T(8,128)(2,1)S(1)}, u32[]{:S(2)}, u32[]{:S(2)}) collective-permute-start(bf16[3,128,1152]{2,1,0:T(8,128)(2,1)S(1)} %get-tuple-element.13), channel_id=1, source_target_pairs={{0,1},{1,0},{2,3},{3,2},{4,5},{5,4},{6,7},{7,6},{8,9},{9,8},{10,11... | collective-permute-start | bytes 2654216 | tf_op jit(solution)/shard_map/ppermute | solution.py:35
  49.5 16.8 %collective-permute-start.10 = (bf16[2,17,64,128]{3,2,1,0:T(8,128)(2,1)S(1)}, bf16[2,17,64,128]{3,2,1,0:T(8,128)(2,1)S(1)}, u32[]{:S(2)}, u32[]{:S(2)}) collective-permute-start(bf16[2,17,64,128]{3,2,1,0:T(8,128)(2,1)S(1)} %get-tuple-element.20), channel_id=1, source_target_pairs={{0,2},{1,27},{2,8},{3,1},{4,6},{5,31},{6,12},{7,5},{8,10},{9,3},{1... | collective-permute-start | bytes 1671176 | tf_op jit(solution)/shard_map/ppermute | solution.py:31
  49.6 25.7 %collective-permute-start.4 = (bf16[3,17,64,128]{3,2,1,0:T(8,128)(2,1)S(1)}, bf16[3,17,64,128]{3,2,1,0:T(8,128)(2,1)S(1)}, u32[]{:S(2)}, u32[]{:S(2)}) collective-permute-start(bf16[3,17,64,128]{3,2,1,0:T(8,128)(2,1)S(1)} %get-tuple-element.16), channel_id=1, source_target_pairs={{0,30},{2,4},{4,2},{6,8},{8,6},{10,12},{12,10},{14,16},{16,14},{18... | collective-permute-start | bytes 2506760 | tf_op jit(solution)/shard_map/ppermute | solution.py:22
  60.4 16.7 %collective-permute-start.7 = (bf16[2,17,64,128]{3,2,1,0:T(8,128)(2,1)S(1)}, bf16[2,17,64,128]{3,2,1,0:T(8,128)(2,1)S(1)}, u32[]{:S(2)}, u32[]{:S(2)}) collective-permute-start(bf16[2,17,64,128]{3,2,1,0:T(8,128)(2,1)S(1)} %collective-permute-done.3.refs_1_), channel_id=1, source_target_pairs={{0,2},{1,27},{2,8},{3,1},{4,6},{5,31},{6,12},{7,5},{8,10},{9,3},{1... | collective-permute-start | bytes 1671176 | tf_op jit(solution)/shard_map/ppermute | solution.py:31
  66.4 7.0 %collective-permute-start.6 = (bf16[1,17,64,128]{3,2,1,0:T(8,128)(2,1)S(1)}, bf16[1,17,64,128]{3,2,1,0:T(8,128)(2,1)S(1)}, u32[]{:S(2)}, u32[]{:S(2)}) collective-permute-start(bf16[1,17,64,128]{3,2,1,0:T(8,128)(2,1)S(1)} %get-tuple-element.17), channel_id=1, source_target_pairs={{0,1},{1,0},{2,3},{3,2},{4,5},{5,4},{6,7},{7,6},{8,9},{9,8},{10,11... | collective-permute-start | bytes 835592 | tf_op jit(solution)/shard_map/ppermute | solution.py:35

commit v6 on v5

--- a/solution.py
+++ b/solution.py
@@ -142,7 +142,6 @@
 
 def product_kernel(plan, *refs):
     refs = list(refs)
-    extent_ref = refs.pop(0) if plan["masked_source"] is not None else None
     turned_ref = refs.pop(0)
     source_refs = [refs.pop(0) for _ in range(plan["sources"])]
     partial_ref = refs.pop(0) if plan["partial"] else None
@@ -250,21 +249,6 @@
         left_copy(row, 0).wait()
     for index in range(plan["taken"]):
         row_copy(source_refs[0], 0, 0, index).wait()
-    if extent_ref is not None:
-        for rep_value in range(2):
-            for core_value in range(2):
-
-                @pl.when((rep == rep_value) & (core == core_value))
-                def _(rep_value=rep_value, core_value=core_value):
-                    for slot, source, position in plan["where"](rep_value, core_value):
-                        if source == plan["masked_source"]:
-                            clear_absent(
-                                window,
-                                lambda b, slot=slot: (slot + b, slot),
-                                extent_ref[position],
-                                band,
-                            )
-
     parts = [range(pairs)]
     if final:
         middle = (band - 1 + rows_out) // 2 + 1
@@ -292,7 +276,7 @@
                 out_copy(half, row).wait()
 
 
-def partial_product(turned, sources, where, partial, rows_out, kind, masked=None):
+def partial_product(turned, sources, where, partial, rows_out, kind):
     band, depth, block = sources[0].shape[1:]
     slots = rows_out + band
     columns = slots + band - 1
@@ -306,13 +290,9 @@
         "rows_out": rows_out,
         "partial": partial is not None,
         "final": final,
-        "masked_source": None if masked is None else masked[0],
     }
     operands = [turned, *sources]
     in_specs = [pl.BlockSpec(memory_space=pl.ANY)] * len(operands)
-    if masked is not None:
-        operands.insert(0, masked[1])
-        in_specs.insert(0, pl.BlockSpec(memory_space=pltpu.SMEM))
     if partial is not None:
         operands.append(partial)
         in_specs.append(pl.BlockSpec(memory_space=pltpu.VMEM))
@@ -356,19 +336,16 @@
     distance = jnp.abs(lax.broadcasted_iota(jnp.int32, b_blocks.shape, 1) - half_band)
     live = distance <= b_extent[:, None, None, None]
 
-    outer = to_outer_neighbour(b_blocks, ring)
-    outer_extent = to_outer_neighbour(b_extent, ring)
     b_own = b_blocks * live.astype(b_blocks.dtype)
+    outer = to_outer_neighbour(b_own, ring)
     across = over_rep(b_blocks)
     peer = to_chip_peer(b_own, ring)
     turned, turned_send = turned_left(a_blocks, a_extent, rows_out)
     turned_across = over_rep(turned_send)
-    across = after(across, turned_send, outer_extent)
+    across = after(across, turned_send)
     *onward, across = picked(across, [*spans[:2], (0, 0)], [*sizes[:2], rows], b_extent)
     across_outer = [to_outer_neighbour(x, ring) for x in onward]
-    extra, rest = picked(
-        outer, [spans[0], spans[2][::-1]], [sizes[0], sizes[2]], outer_extent
-    )
+    extra, rest = picked(outer, [spans[0], spans[2][::-1]], [sizes[0], sizes[2]])
     extra = to_second_neighbour(extra, ring)
     across_outer.append(over_rep(rest))
     across_extra = to_second_neighbour(across_outer[0], ring)
@@ -404,7 +381,6 @@
         None,
         rows_out,
         jnp.bfloat16,
-        (2, outer_extent),
     )
     total = partial_product(
         turned_across,

time: 80.5 us -> 78.3 us (0.973)
  starting transfers between devices: 17.4 us -> 15.4 us
  Pallas kernels: 13.3 us -> 11.9 us
  waiting for transfers between devices: 47.6 us -> 48.8 us
    ppermute x3, waiting for transfers between devices: 12.7 us -> 30.6 us  [over_rep(): return lax.ppermute(x, 'rep', [(0, 1), (1, 0)])]
    ppermute x4 -> x3, waiting for transfers between devices: 29 us -> 12.9 us  [to_outer_neighbour(): lax.ppermute(x, RING, [(g, (g + 2 * (g % 2) - 1) % ring) for g in range(r...]
    ppermute x2, starting transfers between devices: 2.42 us -> 0.07 us  [to_chip_peer(): return lax.ppermute(x, RING, [(g, g ^ 1) for g in range(ring)])]
    ppermute x4 -> x3, starting transfers between devices: 9.46 us -> 9.17 us  [to_outer_neighbour(): lax.ppermute(x, RING, [(g, (g + 2 * (g % 2) - 1) % ring) for g in range(r...]
  transfers between devices with their start and end apart: 11 -> 10, of which waited for: 6 -> 6; matrix products, arithmetic and copies ran while one was open for 2% -> 2% of each run, Pallas kernels for 13% -> 11%
where the time goes in v6:
time: 78.3 us; the launch traced here: 78.1 us
  waiting for transfers between devices  48.8 us (62%)
  starting transfers between devices  15.4 us (20%)
  Pallas kernels  11.9 us (15%)
  other arithmetic  1.77 us (2%)
    ppermute x3, waiting for transfers between devices, over_rep(): return lax.ppermute(x, 'rep', [(0, 1), (1, 0)])  30.6 us
    ppermute x3, waiting for transfers between devices, to_outer_neighbour(): lax.ppermute(x, RING, [(g, (g + 2 * (g % 2) - 1) % ring) for g in range(r...  12.9 us
    pallas_call x3, Pallas kernels, partial_product(): pl.pallas_call(functools.partial(product_kernel, plan), out_shape=out_sha...  9.18 us
    ppermute x3, starting transfers between devices, to_outer_neighbour(): lax.ppermute(x, RING, [(g, (g + 2 * (g % 2) - 1) % ring) for g in range(r...  9.17 us
    ppermute x2, waiting for transfers between devices, to_second_neighbour(): return lax.ppermute(x, EVERY, pairs)  5.33 us
    ppermute x3, starting transfers between devices, over_rep(): return lax.ppermute(x, 'rep', [(0, 1), (1, 0)])  4.39 us
    mul x1, other arithmetic, local(): b_own = b_blocks * live.astype(b_blocks.dtype)  1.77 us
    ppermute x2, starting transfers between devices, to_second_neighbour(): return lax.ppermute(x, EVERY, pairs)  1.74 us
  transfers between devices with their start and end apart: 10, of which 6 were waited for; matrix products, arithmetic and copies ran while one was open for 2% of the time, Pallas kernels for 11%

profile of v6, /device:TPU:0, one launch (start us, length us, event | category | flops | bytes accessed | tf_op | source)
XLA Modules:
  0.0 78.1 jit_solution(17714678027951698793)
XLA Ops:
  0.0 2.9 %collective-permute-start.1 = (bf16[6,17,64,128]{3,2,1,0:T(8,128)(2,1)}, bf16[6,17,64,128]{3,2,1,0:T(8,128)(2,1)S(1)}, u32[]{:S(2)}, u32[]{:S(2)}) collective-permute-start(bf16[6,17,64,128]{3,2,1,0:T(8,128)(2,1)} %param.5), channel_id=1, source_target_pairs={{0,1},{1,0},{2,3},{3,2},{4,5},{5,4},{6,7},{7,6},{8,9},{9,8},{10,11... | collective-permute-start | bytes 5013512 | tf_op jit(solution)/shard_map/ppermute | solution.py:35
  2.9 1.8 %compare_select_fusion.refs_1_ = bf16[6,17,64,128]{3,2,1,0:T(8,128)(2,1)S(1)} fusion(bf16[6,17,64,128]{3,2,1,0:T(8,128)(2,1)} %param.5, s32[6]{0:T(128)} %refs_0_.1, s32[17]{0:T(128)S(1)} %add_abs_fusion), kind=kLoop, calls=%fused_computation | loop fusion | flops 1671168 | bytes 3342428 | tf_op jit(solution)/shard_map/mul | solution.py:339
  4.7 0.0 copy-start.1
  4.7 3.8 %collective-permute-start.4 = (bf16[6,17,64,128]{3,2,1,0:T(8,128)(2,1)S(1)}, bf16[6,17,64,128]{3,2,1,0:T(8,128)(2,1)S(1)}, u32[]{:S(2)}, u32[]{:S(2)}) collective-permute-start(bf16[6,17,64,128]{3,2,1,0:T(8,128)(2,1)S(1)} %compare_select_fusion.refs_1_), channel_id=1, source_target_pairs={{0,30},{2,4},{4,2},{6,8},{8,6},{10,12},{12,10},{14,16},{16,14},{18... | collective-permute-start | bytes 5013512 | tf_op jit(solution)/shard_map/ppermute | solution.py:22
  8.5 0.0 collective-permute-start.8
  8.5 1.1 %shard_map.46 = (bf16[3,128,1152]{2,1,0:T(8,128)(2,1)S(1)}, bf16[3,128,1152]{2,1,0:T(8,128)(2,1)S(1)}) custom-call(s32[6]{0:T(128)S(1)} %copy-done.2, bf16[6,17,64,128]{3,2,1,0:T(8,128)(2,1)S(1)} %copy-done), custom_call_target="tpu_custom_call" | custom-call | tf_op jit(solution)/shard_map/pallas_call | solution.py:70
  9.6 30.0 %collective-permute-done.1.refs_1_ = bf16[6,17,64,128]{3,2,1,0:T(8,128)(2,1)S(1)} collective-permute-done((bf16[6,17,64,128]{3,2,1,0:T(8,128)(2,1)}, bf16[6,17,64,128]{3,2,1,0:T(8,128)(2,1)S(1)}, u32[]{:S(2)}, u32[]{:S(2)}) %collective-permute-start.1) | collective-permute-done | bytes 1671200 | tf_op jit(solution)/shard_map/ppermute | solution.py:35
  39.7 1.5 %shard_map.47 = (bf16[2,17,64,128]{3,2,1,0:T(8,128)(2,1)S(1)}, bf16[3,17,64,128]{3,2,1,0:T(8,128)(2,1)S(1)}, bf16[6,17,64,128]{3,2,1,0:T(8,128)(2,1)S(1)}) custom-call(s32[6]{0:T(128)S(1)} %copy-done.1, bf16[6,17,64,128]{3,2,1,0:T(8,128)(2,1)S(1)} %collective-permute-done.1.refs_1_), custom_call_target="tpu_custom_call" | custom-call | tf_op jit(solution)/shard_map/pallas_call | solution.py:124
  41.2 0.1 collective-permute-start.7
  41.2 4.8 %collective-permute-start.2 = (bf16[2,17,64,128]{3,2,1,0:T(8,128)(2,1)S(1)}, bf16[2,17,64,128]{3,2,1,0:T(8,128)(2,1)S(1)}, u32[]{:S(2)}, u32[]{:S(2)}) collective-permute-start(bf16[2,17,64,128]{3,2,1,0:T(8,128)(2,1)S(1)} %get-tuple-element.15), channel_id=1, source_target_pairs={{0,30},{2,4},{4,2},{6,8},{8,6},{10,12},{12,10},{14,16},{16,14},{18... | collective-permute-start | bytes 1671176 | tf_op jit(solution)/shard_map/ppermute | solution.py:22
  46.1 1.5 %collective-permute-start = (bf16[3,128,1152]{2,1,0:T(8,128)(2,1)S(1)}, bf16[3,128,1152]{2,1,0:T(8,128)(2,1)S(1)}, u32[]{:S(2)}, u32[]{:S(2)}) collective-permute-start(bf16[3,128,1152]{2,1,0:T(8,128)(2,1)S(1)} %get-tuple-element.13), channel_id=1, source_target_pairs={{0,1},{1,0},{2,3},{3,2},{4,5},{5,4},{6,7},{7,6},{8,9},{9,8},{10,11... | collective-permute-start | bytes 2654216 | tf_op jit(solution)/shard_map/ppermute | solution.py:35
  47.5 0.0 collective-permute-done.4.refs_0_.refs_3_
  47.5 0.1 shard_map.48
  47.7 0.1 collective-permute-start.9
  47.7 0.6 collective-permute-start.3
  48.3 10.4 %collective-permute-done.2.refs_1_ = bf16[2,17,64,128]{3,2,1,0:T(8,128)(2,1)S(1)} collective-permute-done((bf16[2,17,64,128]{3,2,1,0:T(8,128)(2,1)S(1)}, bf16[2,17,64,128]{3,2,1,0:T(8,128)(2,1)S(1)}, u32[]{:S(2)}, u32[]{:S(2)}) %collective-permute-start.2) | collective-permute-done | bytes 557088 | tf_op jit(solution)/shard_map/ppermute | solution.py:22
  58.7 1.7 %collective-permute-start.6 = (bf16[2,17,64,128]{3,2,1,0:T(8,128)(2,1)S(1)}, bf16[2,17,64,128]{3,2,1,0:T(8,128)(2,1)S(1)}, u32[]{:S(2)}, u32[]{:S(2)}) collective-permute-start(bf16[2,17,64,128]{3,2,1,0:T(8,128)(2,1)S(1)} %collective-permute-done.2.refs_1_), channel_id=1, source_target_pairs={{0,2},{1,27},{2,8},{3,1},{4,6},{5,31},{6,12},{7,5},{8,10},{9,3},{1... | collective-permute-start | bytes 1671176 | tf_op jit(solution)/shard_map/ppermute | solution.py:31
  60.3 4.2 %collective-permute-done.9.refs_4_ = bf16[2,17,64,128]{3,2,1,0:T(8,128)(2,1)S(1)} collective-permute-done((bf16[2,17,64,128]{3,2,1,0:T(8,128)(2,1)S(1)}, bf16[2,17,64,128]{3,2,1,0:T(8,128)(2,1)S(1)}, u32[]{:S(2)}, u32[]{:S(2)}) %collective-permute-start.9) | collective-permute-done | bytes 557088 | tf_op jit(solution)/shard_map/ppermute | solution.py:31
  64.5 3.5 %shard_map.49.refs_3_ = bf16[18,384,256]{2,1,0:T(8,128)(2,1)S(1)} custom-call(bf16[3,128,1152]{2,1,0:T(8,128)(2,1)S(1)} %get-tuple-element.19.refs_0_, bf16[6,17,64,128]{3,2,1,0:T(8,128)(2,1)S(1)} %compare_select_fusion.refs_1_, bf16[6,17,64,128]{3,2,1,0:T(8,128)(2,1)S(1)} %collective-permute-done.8.refs_2_, ...), custom_call_target="tpu_custom_call" | custom-call | tf_op jit(solution)/shard_map/pallas_call | solution.py:315
  68.0 2.5 %shard_map.50.refs_5_ = f32[18,384,256]{2,1,0:T(8,128)S(1)} custom-call(bf16[3,128,1152]{2,1,0:T(8,128)(2,1)S(1)} %collective-permute-done.refs_0_, bf16[6,17,64,128]{3,2,1,0:T(8,128)(2,1)S(1)} %get-tuple-element.18.refs_1_, bf16[6,17,64,128]{3,2,1,0:T(8,128)(2,1)S(1)} %collective-permute-done.7.refs_2_, bf16[18,384,256]{2,1,0:T(8,128)(2,1)S(1)} %shard_map.49.refs_3_), custom_call_target="tpu_custom_call" | custom-call | tf_op jit(solution)/shard_map/pallas_call | solution.py:315
  70.5 0.5 collective-permute-done.5.refs_3_
  71.1 2.5 %collective-permute-done.3.refs_2_ = bf16[3,17,64,128]{3,2,1,0:T(8,128)(2,1)S(1)} collective-permute-done((bf16[3,17,64,128]{3,2,1,0:T(8,128)(2,1)S(1)}, bf16[3,17,64,128]{3,2,1,0:T(8,128)(2,1)S(1)}, u32[]{:S(2)}, u32[]{:S(2)}) %collective-permute-start.3) | collective-permute-done | bytes 835616 | tf_op jit(solution)/shard_map/ppermute | solution.py:22
  73.6 1.2 %collective-permute-done.6.refs_4_ = bf16[2,17,64,128]{3,2,1,0:T(8,128)(2,1)S(1)} collective-permute-done((bf16[2,17,64,128]{3,2,1,0:T(8,128)(2,1)S(1)}, bf16[2,17,64,128]{3,2,1,0:T(8,128)(2,1)S(1)}, u32[]{:S(2)}, u32[]{:S(2)}) %collective-permute-start.6) | collective-permute-done | bytes 557088 | tf_op jit(solution)/shard_map/ppermute | solution.py:31
  74.8 3.2 %shard_map.51 = bf16[3,33,128,128]{3,2,1,0:T(8,128)(2,1)} custom-call(bf16[3,128,1152]{2,1,0:T(8,128)(2,1)S(1)} %collective-permute-done.refs_0_, bf16[2,17,64,128]{3,2,1,0:T(8,128)(2,1)S(1)} %collective-permute-done.2.refs_1_, bf16[3,17,64,128]{3,2,1,0:T(8,128)(2,1)S(1)} %collective-permute-done.3.refs_2_, ...), custom_call_target="tpu_custom_call" | custom-call | tf_op jit(solution)/shard_map/pallas_call | solution.py:315
  (10 shorter events, 0.0 us)
Async XLA Ops:
  0.0 39.6 %collective-permute-start.1 = (bf16[6,17,64,128]{3,2,1,0:T(8,128)(2,1)}, bf16[6,17,64,128]{3,2,1,0:T(8,128)(2,1)S(1)}, u32[]{:S(2)}, u32[]{:S(2)}) collective-permute-start(bf16[6,17,64,128]{3,2,1,0:T(8,128)(2,1)} %param.5), channel_id=1, source_target_pairs={{0,1},{1,0},{2,3},{3,2},{4,5},{5,4},{6,7},{7,6},{8,9},{9,8},{10,11... | collective-permute-start | bytes 5013512 | tf_op jit(solution)/shard_map/ppermute | solution.py:35
  2.9 5.6 %copy-start = (bf16[6,17,64,128]{3,2,1,0:T(8,128)(2,1)S(1)}, bf16[6,17,64,128]{3,2,1,0:T(8,128)(2,1)}, u32[]{:S(2)}) copy-start(bf16[6,17,64,128]{3,2,1,0:T(8,128)(2,1)} %a_ref.1) | copy-start | bytes 5013508
  2.9 5.6 %copy-start.2 = (s32[6]{0:T(128)S(1)}, s32[6]{0:T(128)}, u32[]{:S(2)}) copy-start(s32[6]{0:T(128)} %extent_ref.1) | copy-start | bytes 76
  4.7 34.9 %copy-start.1 = (s32[6]{0:T(128)S(1)}, s32[6]{0:T(128)}, u32[]{:S(2)}) copy-start(s32[6]{0:T(128)} %refs_0_.1) | copy-start | bytes 76
  4.7 42.8 %collective-permute-start.4 = (bf16[6,17,64,128]{3,2,1,0:T(8,128)(2,1)S(1)}, bf16[6,17,64,128]{3,2,1,0:T(8,128)(2,1)S(1)}, u32[]{:S(2)}, u32[]{:S(2)}) collective-permute-start(bf16[6,17,64,128]{3,2,1,0:T(8,128)(2,1)S(1)} %compare_select_fusion.refs_1_), channel_id=1, source_target_pairs={{0,30},{2,4},{4,2},{6,8},{8,6},{10,12},{12,10},{14,16},{16,14},{18... | collective-permute-start | bytes 5013512 | tf_op jit(solution)/shard_map/ppermute | solution.py:22
  8.5 39.2 %collective-permute-start.8 = (bf16[6,17,64,128]{3,2,1,0:T(8,128)(2,1)S(1)}, bf16[6,17,64,128]{3,2,1,0:T(8,128)(2,1)S(1)}, u32[]{:S(2)}, u32[]{:S(2)}) collective-permute-start(bf16[6,17,64,128]{3,2,1,0:T(8,128)(2,1)S(1)} %compare_select_fusion.refs_1_), channel_id=1, source_target_pairs={{0,2},{2,0},{4,6},{6,4},{8,10},{10,8},{12,14},{14,12},{16,18},{18,... | collective-permute-start | bytes 5013512 | tf_op jit(solution)/shard_map/ppermute | solution.py:18
  41.2 26.8 %collective-permute-start.7 = (bf16[6,17,64,128]{3,2,1,0:T(8,128)(2,1)S(1)}, bf16[6,17,64,128]{3,2,1,0:T(8,128)(2,1)S(1)}, u32[]{:S(2)}, u32[]{:S(2)}) collective-permute-start(bf16[6,17,64,128]{3,2,1,0:T(8,128)(2,1)S(1)} %get-tuple-element.18.refs_1_), channel_id=1, source_target_pairs={{0,2},{2,0},{4,6},{6,4},{8,10},{10,8},{12,14},{14,12},{16,18},{18,... | collective-permute-start | bytes 5013512 | tf_op jit(solution)/shard_map/ppermute | solution.py:18
  41.2 17.4 %collective-permute-start.2 = (bf16[2,17,64,128]{3,2,1,0:T(8,128)(2,1)S(1)}, bf16[2,17,64,128]{3,2,1,0:T(8,128)(2,1)S(1)}, u32[]{:S(2)}, u32[]{:S(2)}) collective-permute-start(bf16[2,17,64,128]{3,2,1,0:T(8,128)(2,1)S(1)} %get-tuple-element.15), channel_id=1, source_target_pairs={{0,30},{2,4},{4,2},{6,8},{8,6},{10,12},{12,10},{14,16},{16,14},{18... | collective-permute-start | bytes 1671176 | tf_op jit(solution)/shard_map/ppermute | solution.py:22
  46.1 21.9 %collective-permute-start = (bf16[3,128,1152]{2,1,0:T(8,128)(2,1)S(1)}, bf16[3,128,1152]{2,1,0:T(8,128)(2,1)S(1)}, u32[]{:S(2)}, u32[]{:S(2)}) collective-permute-start(bf16[3,128,1152]{2,1,0:T(8,128)(2,1)S(1)} %get-tuple-element.13), channel_id=1, source_target_pairs={{0,1},{1,0},{2,3},{3,2},{4,5},{5,4},{6,7},{7,6},{8,9},{9,8},{10,11... | collective-permute-start | bytes 2654216 | tf_op jit(solution)/shard_map/ppermute | solution.py:35
  47.7 16.8 %collective-permute-start.9 = (bf16[2,17,64,128]{3,2,1,0:T(8,128)(2,1)S(1)}, bf16[2,17,64,128]{3,2,1,0:T(8,128)(2,1)S(1)}, u32[]{:S(2)}, u32[]{:S(2)}) collective-permute-start(bf16[2,17,64,128]{3,2,1,0:T(8,128)(2,1)S(1)} %get-tuple-element.20), channel_id=1, source_target_pairs={{0,2},{1,27},{2,8},{3,1},{4,6},{5,31},{6,12},{7,5},{8,10},{9,3},{1... | collective-permute-start | bytes 1671176 | tf_op jit(solution)/shard_map/ppermute | solution.py:31
  47.7 25.8 %collective-permute-start.3 = (bf16[3,17,64,128]{3,2,1,0:T(8,128)(2,1)S(1)}, bf16[3,17,64,128]{3,2,1,0:T(8,128)(2,1)S(1)}, u32[]{:S(2)}, u32[]{:S(2)}) collective-permute-start(bf16[3,17,64,128]{3,2,1,0:T(8,128)(2,1)S(1)} %get-tuple-element.16), channel_id=1, source_target_pairs={{0,30},{2,4},{4,2},{6,8},{8,6},{10,12},{12,10},{14,16},{16,14},{18... | collective-permute-start | bytes 2506760 | tf_op jit(solution)/shard_map/ppermute | solution.py:22
  58.7 16.1 %collective-permute-start.6 = (bf16[2,17,64,128]{3,2,1,0:T(8,128)(2,1)S(1)}, bf16[2,17,64,128]{3,2,1,0:T(8,128)(2,1)S(1)}, u32[]{:S(2)}, u32[]{:S(2)}) collective-permute-start(bf16[2,17,64,128]{3,2,1,0:T(8,128)(2,1)S(1)} %collective-permute-done.2.refs_1_), channel_id=1, source_target_pairs={{0,2},{1,27},{2,8},{3,1},{4,6},{5,31},{6,12},{7,5},{8,10},{9,3},{1... | collective-permute-start | bytes 1671176 | tf_op jit(solution)/shard_map/ppermute | solution.py:31
  64.5 6.5 %collective-permute-start.5 = (bf16[1,17,64,128]{3,2,1,0:T(8,128)(2,1)S(1)}, bf16[1,17,64,128]{3,2,1,0:T(8,128)(2,1)S(1)}, u32[]{:S(2)}, u32[]{:S(2)}) collective-permute-start(bf16[1,17,64,128]{3,2,1,0:T(8,128)(2,1)S(1)} %get-tuple-element.17), channel_id=1, source_target_pairs={{0,1},{1,0},{2,3},{3,2},{4,5},{5,4},{6,7},{7,6},{8,9},{9,8},{10,11... | collective-permute-start | bytes 835592 | tf_op jit(solution)/shard_map/ppermute | solution.py:35

commit v7 on v6

--- a/solution.py
+++ b/solution.py
@@ -10,6 +10,7 @@
 RING = ("row", "col")
 EVERY = ("row", "col", "rep")
 EXTRA_ROWS = 2
+PEER_ROWS = 2
 REST = 1
 VMEM_LIMIT = 24 * 2**20
 
@@ -80,56 +81,66 @@
     )(a_extent, a_blocks)
 
 
-def clear_absent(ref, at, extent, band):
-    half_band = (band - 1) // 2
-
-    def clear(offset, carry):
-        for b in (offset, band - 1 - offset):
-            ref[at(b)] = jnp.zeros(ref.shape[-2:], ref.dtype)
-        return carry
-
-    lax.fori_loop(0, half_band - extent, clear, 0)
-
-
-def pick_kernel(spans, masks, *refs):
+def pick_kernel(band, spans, masks, *refs):
     refs = list(refs)
     extent_ref = refs.pop(0) if masks else None
     x_ref, out_refs, sem = refs[0], refs[1:-1], refs[-1]
+    half_band = (band - 1) // 2
     rep = lax.axis_index("rep")
-    starts = [jnp.where(rep == 0, low, high) for low, high in spans]
 
     def copies():
         return [
-            pltpu.make_async_copy(x_ref.at[pl.ds(start, out_ref.shape[0])], out_ref, sem.at[i])
-            for i, (start, out_ref) in enumerate(zip(starts, out_refs))
+            pltpu.make_async_copy(
+                x_ref.at[pl.ds(jnp.where(rep == 0, low, high), out_ref.shape[0])],
+                out_ref,
+                sem.at[i],
+            )
+            for i, ((low, high), out_ref) in enumerate(zip(spans, out_refs))
         ]
+
+    def clear_row(out_ref, at, low, high, extent):
+        def clear(offset, carry):
+            if low <= 0:
+                out_ref[at + offset] = jnp.zeros(out_ref.shape[1:], out_ref.dtype)
+            if high >= band:
+                out_ref[at + band - 1 - offset] = jnp.zeros(out_ref.shape[1:], out_ref.dtype)
+            return carry
+
+        lax.fori_loop(0, half_band - extent, clear, 0)
 
     for copy in copies():
         copy.start()
     for copy in copies():
         copy.wait()
-    if masks:
-        for start, out_ref in zip(starts, out_refs):
-            for row in range(out_ref.shape[0]):
-                clear_absent(
-                    out_ref, lambda b, row=row: (row, b), extent_ref[start + row], out_ref.shape[1]
-                )
+    if not masks:
+        return
+    for rep_value in range(2):
+
+        @pl.when(rep == rep_value)
+        def _(rep_value=rep_value):
+            for span, out_ref in zip(spans, out_refs):
+                start = span[rep_value]
+                end = start + out_ref.shape[0]
+                for row in range(start // band, (end + band - 1) // band):
+                    at = row * band - start
+                    clear_row(out_ref, at, max(-at, 0), min(end - start - at, band), extent_ref[row])
 
 
 def picked(x, spans, sizes, extents=None):
+    rows, band, depth, block = x.shape
     masks = extents is not None
-    shapes = [jax.ShapeDtypeStruct((size, *x.shape[1:]), x.dtype) for size in sizes]
+    shapes = [jax.ShapeDtypeStruct((size, depth, block), x.dtype) for size in sizes]
     out_space = pltpu.VMEM if masks else pl.ANY
     in_specs = [pl.BlockSpec(memory_space=pltpu.SMEM)] if masks else []
     return pl.pallas_call(
-        functools.partial(pick_kernel, spans, masks),
+        functools.partial(pick_kernel, band, spans, masks),
         out_shape=shapes,
         in_specs=in_specs + [pl.BlockSpec(memory_space=pl.ANY)],
         out_specs=[pl.BlockSpec(memory_space=out_space)] * len(sizes),
         scratch_shapes=[pltpu.SemaphoreType.DMA((len(sizes),))],
         compiler_params=pltpu.CompilerParams(vmem_limit_bytes=(4 if masks else 1) * 2**20),
         cost_estimate=pl.CostEstimate(flops=0, bytes_accessed=0, transcendentals=0),
-    )(*([extents] if masks else []), x)
+    )(*([extents] if masks else []), x.reshape(rows * band, depth, block))
 
 
 def after(x, *others):
@@ -164,9 +175,11 @@
             left_sem.at[row],
         )
 
-    def row_copy(source, position, slot, index):
+    def row_copy(source, at, slot, first, count, index):
         return pltpu.make_async_copy(
-            source.at[position], window.at[pl.ds(slot, band), slot], row_sem.at[index]
+            source.at[pl.ds(at, count)],
+            window.at[pl.ds(slot + first, count), slot],
+            row_sem.at[index],
         )
 
     def out_copy(half, row):
@@ -189,10 +202,10 @@
                 left[lines, at + reach :] = jnp.zeros((block, width - at - reach), left.dtype)
 
     def place_rows(listed):
-        for index, (slot, source, position) in enumerate(listed):
-            row_copy(source_refs[source], position, slot, index).start()
+        for index, (slot, source, at, first, count) in enumerate(listed):
+            row_copy(source_refs[source], at, slot, first, count, index).start()
         blank = jnp.zeros((depth, block), window.dtype)
-        taken = {slot for slot, _, _ in listed}
+        taken = {slot for slot, *_ in listed}
         for pair in range(pairs):
             if 2 * pair + 1 in taken:
                 window[2 * pair, 2 * pair + 1] = blank
@@ -247,14 +260,14 @@
 
     for row in range(rows_out):
         left_copy(row, 0).wait()
-    for index in range(plan["taken"]):
-        row_copy(source_refs[0], 0, 0, index).wait()
+    for index, count in enumerate(plan["counts"]):
+        row_copy(source_refs[0], 0, 0, 0, count, index).wait()
     parts = [range(pairs)]
     if final:
         middle = (band - 1 + rows_out) // 2 + 1
         parts = [range(middle), range(middle, pairs)]
     for half, part in enumerate(parts):
-        if plan["taken"] == slots:
+        if len(plan["counts"]) == slots:
             multiply([(0, slots)], part)
         else:
             for rep_value in range(2):
@@ -262,7 +275,7 @@
 
                     @pl.when((rep == rep_value) & (core == core_value))
                     def _(rep_value=rep_value, core_value=core_value, part=part):
-                        taken = sorted(slot for slot, _, _ in plan["where"](rep_value, core_value))
+                        taken = sorted({slot for slot, *_ in plan["where"](rep_value, core_value)})
                         lows = [slot for slot in taken if slot - 1 not in taken]
                         highs = [slot + 1 for slot in taken if slot + 1 not in taken]
                         multiply(list(zip(lows, highs)), part)
@@ -276,16 +289,16 @@
                 out_copy(half, row).wait()
 
 
-def partial_product(turned, sources, where, partial, rows_out, kind):
-    band, depth, block = sources[0].shape[1:]
+def partial_product(turned, sources, where, partial, rows_out, band, kind):
+    depth, block = sources[0].shape[1:]
     slots = rows_out + band
     columns = slots + band - 1
-    taken = len(where(0, 0))
+    counts = [count for *_, count in where(0, 0)]
     final = kind is None
     plan = {
         "sources": len(sources),
         "where": where,
-        "taken": taken,
+        "counts": counts,
         "band": band,
         "rows_out": rows_out,
         "partial": partial is not None,
@@ -300,7 +313,7 @@
         pltpu.VMEM((rows_out * block, slots * depth), jnp.bfloat16),
         pltpu.VMEM((columns, slots, depth, block), jnp.bfloat16),
         pltpu.SemaphoreType.DMA((rows_out,)),
-        pltpu.SemaphoreType.DMA((taken,)),
+        pltpu.SemaphoreType.DMA((len(counts),)),
     ]
     if final:
         out_shape = jax.ShapeDtypeStruct((rows_out, 2 * band - 1, block, block), jnp.bfloat16)
@@ -327,15 +340,18 @@
     rows, band, depth, block = a_blocks.shape
     ring = lax.axis_size("row") * lax.axis_size("col")
     rows_out = rows // lax.axis_size("rep")
-
-    starts = ((rows - EXTRA_ROWS, REST, 0), (0, EXTRA_ROWS, rows - REST))
-    sizes = (EXTRA_ROWS, rows - EXTRA_ROWS - REST, REST)
+    half_band = (band - 1) // 2
+
+    def flat(x):
+        return x.reshape(-1, depth, block)
+
+    extra_size, rest_size = EXTRA_ROWS * band, REST * band + half_band
+    sizes = (extra_size, rows * band - extra_size - rest_size, rest_size)
+    starts = ((rows * band - extra_size, rest_size, 0), (0, extra_size, rows * band - rest_size))
     spans = list(zip(*starts))
 
-    half_band = (band - 1) // 2
     distance = jnp.abs(lax.broadcasted_iota(jnp.int32, b_blocks.shape, 1) - half_band)
     live = distance <= b_extent[:, None, None, None]
-
     b_own = b_blocks * live.astype(b_blocks.dtype)
     outer = to_outer_neighbour(b_own, ring)
     across = over_rep(b_blocks)
@@ -343,13 +359,19 @@
     turned, turned_send = turned_left(a_blocks, a_extent, rows_out)
     turned_across = over_rep(turned_send)
     across = after(across, turned_send)
-    *onward, across = picked(across, [*spans[:2], (0, 0)], [*sizes[:2], rows], b_extent)
+    parts = tuple(i * PEER_ROWS * band for i in range(rows // PEER_ROWS))
+    part_sizes = (PEER_ROWS * band,) * len(parts)
+    picks = picked(across, [*spans[:2], *zip(parts, parts)], [*sizes[:2], *part_sizes], b_extent)
+    onward, across_own = picks[:2], picks[2:]
     across_outer = [to_outer_neighbour(x, ring) for x in onward]
-    extra, rest = picked(outer, [spans[0], spans[2][::-1]], [sizes[0], sizes[2]])
+    extra, rest = picked(after(outer, peer), [spans[0], spans[2][::-1]], [sizes[0], sizes[2]])
     extra = to_second_neighbour(extra, ring)
     across_outer.append(over_rep(rest))
     across_extra = to_second_neighbour(across_outer[0], ring)
-    across_peer = to_chip_peer(across, ring)
+    across_peer = [
+        to_chip_peer(x if i == 0 else after(x, across_outer[0]), ring)
+        for i, x in enumerate(across_own)
+    ]
 
     def window_rows(rep_value, core_value):
         sides = ("outer", "peer") if core_value == 0 else ("peer", "outer")
@@ -363,39 +385,54 @@
             for slot, (kind, i) in enumerate(window_rows(rep_value, core_value)):
                 if kind not in index:
                     continue
-                source = index[kind]
-                if isinstance(source, tuple):
-                    spans = zip(starts[rep_value], sizes)
-                    piece = [low <= i < low + size for low, size in spans].index(True)
-                    found.append((slot, source[piece], i - starts[rep_value][piece]))
-                else:
-                    found.append((slot, source, i))
-            return found
+                sources, lows, counts = index[kind]
+                for source, low, count in zip(sources, lows[rep_value], counts):
+                    first = max(i * band, low)
+                    last = min((i + 1) * band, low + count)
+                    if first < last:
+                        found.append((slot, source, first - low, first - i * band, last - first))
+            return sorted(found, key=lambda piece: -piece[-1])
 
         return where
 
+    whole = ((0,), (0,)), (rows * band,)
+    only_extra = ((0,), (0,)), (extra_size,)
+    thirds = (parts, parts), part_sizes
+    count = len(parts)
     total = partial_product(
         turned,
-        [b_own, peer, outer, extra],
-        where_of({"own": 0, "peer": 1, "outer": 2, "extra": 3}),
+        [flat(b_own), flat(peer), flat(outer), extra],
+        where_of(
+            {
+                "own": ((0,), *whole),
+                "peer": ((1,), *whole),
+                "outer": ((2,), *whole),
+                "extra": ((3,), *only_extra),
+            }
+        ),
         None,
         rows_out,
+        band,
         jnp.bfloat16,
     )
     total = partial_product(
         turned_across,
-        [across, across_peer],
-        where_of({"own": 0, "peer": 1}),
+        [*across_own, *across_peer],
+        where_of(
+            {"own": (range(count), *thirds), "peer": (range(count, 2 * count), *thirds)}
+        ),
         total,
         rows_out,
+        band,
         jnp.float32,
     )
     return partial_product(
         turned_across,
         [*across_outer, across_extra],
-        where_of({"outer": (0, 1, 2), "extra": 3}),
+        where_of({"outer": ((0, 1, 2), starts, sizes), "extra": ((3,), *only_extra)}),
         total,
         rows_out,
+        band,
         None,
     )
 

time: 78.3 us -> 76.8 us (0.981)
  waiting for transfers between devices: 48.8 us -> 41.7 us
  starting transfers between devices: 15.4 us -> 20.6 us
    ppermute x3, waiting for transfers between devices: 12.9 us -> 8.48 us  [to_outer_neighbour(): lax.ppermute(x, RING, [(g, (g + 2 * (g % 2) - 1) % ring) for g in range(r...]
    ppermute x2, waiting for transfers between devices: 5.33 us -> 1.95 us  [to_second_neighbour(): return lax.ppermute(x, EVERY, pairs)]
    ppermute x2 -> x4, starting transfers between devices: 0.07 us -> 3.34 us  [to_chip_peer(): return lax.ppermute(x, RING, [(g, g ^ 1) for g in range(ring)])]
    ppermute x3, starting transfers between devices: 4.39 us -> 7.24 us  [over_rep(): return lax.ppermute(x, 'rep', [(0, 1), (1, 0)])]
    ppermute x2, starting transfers between devices: 1.74 us -> 0.06 us  [to_second_neighbour(): return lax.ppermute(x, EVERY, pairs)]
    ppermute x3, starting transfers between devices: 9.17 us -> 9.97 us  [to_outer_neighbour(): lax.ppermute(x, RING, [(g, (g + 2 * (g % 2) - 1) % ring) for g in range(r...]
  transfers between devices with their start and end apart: 10 -> 12, of which waited for: 6 -> 5; matrix products, arithmetic and copies ran while one was open for 2% -> 2% of each run, Pallas kernels for 11% -> 12%
where the time goes in v7:
time: 76.8 us; the launch traced here: 76.5 us
  waiting for transfers between devices  41.7 us (54%)
  starting transfers between devices  20.6 us (27%)
  Pallas kernels  12.2 us (16%)
  other arithmetic  1.77 us (2%)
    ppermute x3, waiting for transfers between devices, over_rep(): return lax.ppermute(x, 'rep', [(0, 1), (1, 0)])  31.2 us
    ppermute x3, starting transfers between devices, to_outer_neighbour(): lax.ppermute(x, RING, [(g, (g + 2 * (g % 2) - 1) % ring) for g in range(r...  9.97 us
    pallas_call x3, Pallas kernels, partial_product(): pl.pallas_call(functools.partial(product_kernel, plan), out_shape=out_sha...  9.22 us
    ppermute x3, waiting for transfers between devices, to_outer_neighbour(): lax.ppermute(x, RING, [(g, (g + 2 * (g % 2) - 1) % ring) for g in range(r...  8.48 us
    ppermute x3, starting transfers between devices, over_rep(): return lax.ppermute(x, 'rep', [(0, 1), (1, 0)])  7.24 us
    ppermute x4, starting transfers between devices, to_chip_peer(): return lax.ppermute(x, RING, [(g, g ^ 1) for g in range(ring)])  3.34 us
    ppermute x2, waiting for transfers between devices, to_second_neighbour(): return lax.ppermute(x, EVERY, pairs)  1.95 us
    pallas_call x2, Pallas kernels, picked(): pl.pallas_call(functools.partial(pick_kernel, band, spans, masks), out_sh...  1.89 us
  transfers between devices with their start and end apart: 12, of which 5 were waited for; matrix products, arithmetic and copies ran while one was open for 2% of the time, Pallas kernels for 12%

profile of v7, /device:TPU:0, one launch (start us, length us, event | category | flops | bytes accessed | tf_op | source)
XLA Modules:
  0.0 76.5 jit_solution(7311252946344566846)
XLA Ops:
  0.0 2.9 %collective-permute-start.1 = (bf16[6,17,64,128]{3,2,1,0:T(8,128)(2,1)}, bf16[6,17,64,128]{3,2,1,0:T(8,128)(2,1)S(1)}, u32[]{:S(2)}, u32[]{:S(2)}) collective-permute-start(bf16[6,17,64,128]{3,2,1,0:T(8,128)(2,1)} %param.5), channel_id=1, source_target_pairs={{0,1},{1,0},{2,3},{3,2},{4,5},{5,4},{6,7},{7,6},{8,9},{9,8},{10,11... | collective-permute-start | bytes 5013512 | tf_op jit(solution)/shard_map/ppermute | solution.py:36
  2.9 1.8 %compare_select_fusion = bf16[6,17,64,128]{3,2,1,0:T(8,128)(2,1)S(1)} fusion(bf16[6,17,64,128]{3,2,1,0:T(8,128)(2,1)} %param.5, s32[6]{0:T(128)} %refs_0_.1, s32[17]{0:T(128)S(1)} %add_abs_fusion), kind=kLoop, calls=%fused_computation | loop fusion | flops 1671168 | bytes 3342428 | tf_op jit(solution)/shard_map/mul | solution.py:355
  4.7 0.0 copy-start.1
  4.7 3.8 %collective-permute-start.4 = (bf16[6,17,64,128]{3,2,1,0:T(8,128)(2,1)S(1)}, bf16[6,17,64,128]{3,2,1,0:T(8,128)(2,1)S(1)}, u32[]{:S(2)}, u32[]{:S(2)}) collective-permute-start(bf16[6,17,64,128]{3,2,1,0:T(8,128)(2,1)S(1)} %compare_select_fusion), channel_id=1, source_target_pairs={{0,30},{2,4},{4,2},{6,8},{8,6},{10,12},{12,10},{14,16},{16,14},{18... | collective-permute-start | bytes 5013512 | tf_op jit(solution)/shard_map/ppermute | solution.py:23
  8.5 0.0 collective-permute-start.5
  8.5 1.1 %shard_map.46 = (bf16[3,128,1152]{2,1,0:T(8,128)(2,1)S(1)}, bf16[3,128,1152]{2,1,0:T(8,128)(2,1)S(1)}) custom-call(s32[6]{0:T(128)S(1)} %copy-done.2, bf16[6,17,64,128]{3,2,1,0:T(8,128)(2,1)S(1)} %copy-done), custom_call_target="tpu_custom_call" | custom-call | tf_op jit(solution)/shard_map/pallas_call | solution.py:71
  9.6 0.6 collective-permute-start
  10.2 30.3 %collective-permute-done.1 = bf16[6,17,64,128]{3,2,1,0:T(8,128)(2,1)S(1)} collective-permute-done((bf16[6,17,64,128]{3,2,1,0:T(8,128)(2,1)}, bf16[6,17,64,128]{3,2,1,0:T(8,128)(2,1)S(1)}, u32[]{:S(2)}, u32[]{:S(2)}) %collective-permute-start.1) | collective-permute-done | bytes 1671200 | tf_op jit(solution)/shard_map/ppermute | solution.py:36
  40.5 1.6 %shard_map.47 = (bf16[34,64,128]{2,1,0:T(8,128)(2,1)S(1)}, bf16[43,64,128]{2,1,0:T(8,128)(2,1)S(1)}, bf16[34,64,128]{2,1,0:T(8,128)(2,1)S(1)}, bf16[34,64,128]{2,1,0:T(8,128)(2,1)S(1)}, bf16[34,64,128]{2,1,0:T(8,128)(2,1)S(1)}) custom-call(s32[6]{0:T(128)S(1)} %copy-done.1, bf16[102,64,128]{2,1,0:T(8,128)(2,1)S(1)} %bitcast.9), custom_call_target="tpu_custom_call" | custom-call | tf_op jit(solution)/shard_map/pallas_call | solution.py:135
  42.1 2.6 %collective-permute-start.2 = (bf16[34,64,128]{2,1,0:T(8,128)(2,1)S(1)}, bf16[34,64,128]{2,1,0:T(8,128)(2,1)S(1)}, u32[]{:S(2)}, u32[]{:S(2)}) collective-permute-start(bf16[34,64,128]{2,1,0:T(8,128)(2,1)S(1)} %get-tuple-element.20), channel_id=1, source_target_pairs={{0,30},{2,4},{4,2},{6,8},{8,6},{10,12},{12,10},{14,16},{16,14},{18... | collective-permute-start | bytes 1671176 | tf_op jit(solution)/shard_map/ppermute | solution.py:23
  44.7 0.3 shard_map.48
  45.0 0.1 collective-permute-start.11
  45.0 0.1 collective-permute-start.8
  45.1 3.6 %collective-permute-start.3 = (bf16[43,64,128]{2,1,0:T(8,128)(2,1)S(1)}, bf16[43,64,128]{2,1,0:T(8,128)(2,1)S(1)}, u32[]{:S(2)}, u32[]{:S(2)}) collective-permute-start(bf16[43,64,128]{2,1,0:T(8,128)(2,1)S(1)} %get-tuple-element.21), channel_id=1, source_target_pairs={{0,30},{2,4},{4,2},{6,8},{8,6},{10,12},{12,10},{14,16},{16,14},{18... | collective-permute-start | bytes 2113544 | tf_op jit(solution)/shard_map/ppermute | solution.py:23
  48.7 8.5 %collective-permute-done.2.refs_1_ = bf16[34,64,128]{2,1,0:T(8,128)(2,1)S(1)} collective-permute-done((bf16[34,64,128]{2,1,0:T(8,128)(2,1)S(1)}, bf16[34,64,128]{2,1,0:T(8,128)(2,1)S(1)}, u32[]{:S(2)}, u32[]{:S(2)}) %collective-permute-start.2) | collective-permute-done | bytes 557088 | tf_op jit(solution)/shard_map/ppermute | solution.py:23
  57.2 3.3 %collective-permute-start.10 = (bf16[34,64,128]{2,1,0:T(8,128)(2,1)S(1)}, bf16[34,64,128]{2,1,0:T(8,128)(2,1)S(1)}, u32[]{:S(2)}, u32[]{:S(2)}) collective-permute-start(bf16[34,64,128]{2,1,0:T(8,128)(2,1)S(1)} %get-tuple-element.28.refs_3_), channel_id=1, source_target_pairs={{0,2},{2,0},{4,6},{6,4},{8,10},{10,8},{12,14},{14,12},{16,18},{18,... | collective-permute-start | bytes 1671176 | tf_op jit(solution)/shard_map/ppermute | solution.py:19
  60.5 0.0 collective-permute-start.9
  60.5 1.3 %collective-permute-done.11.refs_4_ = bf16[34,64,128]{2,1,0:T(8,128)(2,1)S(1)} collective-permute-done((bf16[34,64,128]{2,1,0:T(8,128)(2,1)S(1)}, bf16[34,64,128]{2,1,0:T(8,128)(2,1)S(1)}, u32[]{:S(2)}, u32[]{:S(2)}) %collective-permute-start.11) | collective-permute-done | bytes 557088 | tf_op jit(solution)/shard_map/ppermute | solution.py:32
  61.8 3.7 %collective-permute-start.6 = (bf16[25,64,128]{2,1,0:T(8,128)(2,1)S(1)}, bf16[25,64,128]{2,1,0:T(8,128)(2,1)S(1)}, u32[]{:S(2)}, u32[]{:S(2)}) collective-permute-start(bf16[25,64,128]{2,1,0:T(8,128)(2,1)S(1)} %get-tuple-element.23), channel_id=1, source_target_pairs={{0,1},{1,0},{2,3},{3,2},{4,5},{5,4},{6,7},{7,6},{8,9},{9,8},{10,11... | collective-permute-start | bytes 1228808 | tf_op jit(solution)/shard_map/ppermute | solution.py:36
  65.5 3.5 %shard_map.49.refs_7_ = bf16[18,384,256]{2,1,0:T(8,128)(2,1)S(1)} custom-call(bf16[3,128,1152]{2,1,0:T(8,128)(2,1)S(1)} %get-tuple-element.29.refs_0_, bf16[102,64,128]{2,1,0:T(8,128)(2,1)S(1)} %bitcast.5, bf16[102,64,128]{2,1,0:T(8,128)(2,1)S(1)} %bitcast.8, bf16[102,64,128]{2,1,0:T(8,128)(2,1)S(1)} %bitcast.7, ...), custom_call_target="tpu_custom_call" | custom-call | tf_op jit(solution)/shard_map/pallas_call | solution.py:328
  69.0 2.5 %shard_map.50.refs_5_ = f32[18,384,256]{2,1,0:T(8,128)S(1)} custom-call(bf16[3,128,1152]{2,1,0:T(8,128)(2,1)S(1)} %collective-permute-done.refs_0_, bf16[34,64,128]{2,1,0:T(8,128)(2,1)S(1)} %get-tuple-element.24.refs_1_, bf16[34,64,128]{2,1,0:T(8,128)(2,1)S(1)} %get-tuple-element.27.refs_2_, bf16[34,64,128]{2,1,0:T(8,128)(2,1)S(1)} %get-tuple-element.28.refs_3_, ...), custom_call_target="tpu_custom_call" | custom-call | tf_op jit(solution)/shard_map/pallas_call | solution.py:328
  71.5 0.9 %collective-permute-done.6.refs_3_ = bf16[25,64,128]{2,1,0:T(8,128)(2,1)S(1)} collective-permute-done((bf16[25,64,128]{2,1,0:T(8,128)(2,1)S(1)}, bf16[25,64,128]{2,1,0:T(8,128)(2,1)S(1)}, u32[]{:S(2)}, u32[]{:S(2)}) %collective-permute-start.6) | collective-permute-done | bytes 409632 | tf_op jit(solution)/shard_map/ppermute | solution.py:36
  72.5 0.6 collective-permute-done.7.refs_4_
  73.1 3.2 %shard_map.51 = bf16[3,33,128,128]{3,2,1,0:T(8,128)(2,1)} custom-call(bf16[3,128,1152]{2,1,0:T(8,128)(2,1)S(1)} %collective-permute-done.refs_0_, bf16[34,64,128]{2,1,0:T(8,128)(2,1)S(1)} %collective-permute-done.2.refs_1_, bf16[43,64,128]{2,1,0:T(8,128)(2,1)S(1)} %collective-permute-done.3.refs_2_, bf16[25,64,128]{2,1,0:T(8,128)(2,1)S(1)} %collective-permute-done.6.refs_3_, ...), custom_call_target="tpu_custom_call" | custom-call | tf_op jit(solution)/shard_map/pallas_call | solution.py:328
  (14 shorter events, 0.0 us)
Async XLA Ops:
  0.0 40.5 %collective-permute-start.1 = (bf16[6,17,64,128]{3,2,1,0:T(8,128)(2,1)}, bf16[6,17,64,128]{3,2,1,0:T(8,128)(2,1)S(1)}, u32[]{:S(2)}, u32[]{:S(2)}) collective-permute-start(bf16[6,17,64,128]{3,2,1,0:T(8,128)(2,1)} %param.5), channel_id=1, source_target_pairs={{0,1},{1,0},{2,3},{3,2},{4,5},{5,4},{6,7},{7,6},{8,9},{9,8},{10,11... | collective-permute-start | bytes 5013512 | tf_op jit(solution)/shard_map/ppermute | solution.py:36
  2.9 5.6 %copy-start = (bf16[6,17,64,128]{3,2,1,0:T(8,128)(2,1)S(1)}, bf16[6,17,64,128]{3,2,1,0:T(8,128)(2,1)}, u32[]{:S(2)}) copy-start(bf16[6,17,64,128]{3,2,1,0:T(8,128)(2,1)} %a_ref.1) | copy-start | bytes 5013508
  2.9 5.6 %copy-start.2 = (s32[6]{0:T(128)S(1)}, s32[6]{0:T(128)}, u32[]{:S(2)}) copy-start(s32[6]{0:T(128)} %extent_ref.1) | copy-start | bytes 76
  4.7 35.8 %copy-start.1 = (s32[6]{0:T(128)S(1)}, s32[6]{0:T(128)}, u32[]{:S(2)}) copy-start(s32[6]{0:T(128)} %refs_0_.1) | copy-start | bytes 76
  4.7 39.9 %collective-permute-start.4 = (bf16[6,17,64,128]{3,2,1,0:T(8,128)(2,1)S(1)}, bf16[6,17,64,128]{3,2,1,0:T(8,128)(2,1)S(1)}, u32[]{:S(2)}, u32[]{:S(2)}) collective-permute-start(bf16[6,17,64,128]{3,2,1,0:T(8,128)(2,1)S(1)} %compare_select_fusion), channel_id=1, source_target_pairs={{0,30},{2,4},{4,2},{6,8},{8,6},{10,12},{12,10},{14,16},{16,14},{18... | collective-permute-start | bytes 5013512 | tf_op jit(solution)/shard_map/ppermute | solution.py:23
  8.5 36.1 %collective-permute-start.5 = (bf16[6,17,64,128]{3,2,1,0:T(8,128)(2,1)S(1)}, bf16[6,17,64,128]{3,2,1,0:T(8,128)(2,1)S(1)}, u32[]{:S(2)}, u32[]{:S(2)}) collective-permute-start(bf16[6,17,64,128]{3,2,1,0:T(8,128)(2,1)S(1)} %compare_select_fusion), channel_id=1, source_target_pairs={{0,2},{2,0},{4,6},{6,4},{8,10},{10,8},{12,14},{14,12},{16,18},{18,... | collective-permute-start | bytes 5013512 | tf_op jit(solution)/shard_map/ppermute | solution.py:19
  9.6 50.9 %collective-permute-start = (bf16[3,128,1152]{2,1,0:T(8,128)(2,1)S(1)}, bf16[3,128,1152]{2,1,0:T(8,128)(2,1)S(1)}, u32[]{:S(2)}, u32[]{:S(2)}) collective-permute-start(bf16[3,128,1152]{2,1,0:T(8,128)(2,1)S(1)} %get-tuple-element.18), channel_id=1, source_target_pairs={{0,1},{1,0},{2,3},{3,2},{4,5},{5,4},{6,7},{7,6},{8,9},{9,8},{10,11... | collective-permute-start | bytes 2654216 | tf_op jit(solution)/shard_map/ppermute | solution.py:36
  42.1 15.1 %collective-permute-start.2 = (bf16[34,64,128]{2,1,0:T(8,128)(2,1)S(1)}, bf16[34,64,128]{2,1,0:T(8,128)(2,1)S(1)}, u32[]{:S(2)}, u32[]{:S(2)}) collective-permute-start(bf16[34,64,128]{2,1,0:T(8,128)(2,1)S(1)} %get-tuple-element.20), channel_id=1, source_target_pairs={{0,30},{2,4},{4,2},{6,8},{8,6},{10,12},{12,10},{14,16},{16,14},{18... | collective-permute-start | bytes 1671176 | tf_op jit(solution)/shard_map/ppermute | solution.py:23
  45.0 16.8 %collective-permute-start.11 = (bf16[34,64,128]{2,1,0:T(8,128)(2,1)S(1)}, bf16[34,64,128]{2,1,0:T(8,128)(2,1)S(1)}, u32[]{:S(2)}, u32[]{:S(2)}) collective-permute-start(bf16[34,64,128]{2,1,0:T(8,128)(2,1)S(1)} %get-tuple-element.30), channel_id=1, source_target_pairs={{0,2},{1,27},{2,8},{3,1},{4,6},{5,31},{6,12},{7,5},{8,10},{9,3},{1... | collective-permute-start | bytes 1671176 | tf_op jit(solution)/shard_map/ppermute | solution.py:32
  45.0 16.8 %collective-permute-start.8 = (bf16[34,64,128]{2,1,0:T(8,128)(2,1)S(1)}, bf16[34,64,128]{2,1,0:T(8,128)(2,1)S(1)}, u32[]{:S(2)}, u32[]{:S(2)}) collective-permute-start(bf16[34,64,128]{2,1,0:T(8,128)(2,1)S(1)} %get-tuple-element.24.refs_1_), channel_id=1, source_target_pairs={{0,2},{2,0},{4,6},{6,4},{8,10},{10,8},{12,14},{14,12},{16,18},{18,... | collective-permute-start | bytes 1671176 | tf_op jit(solution)/shard_map/ppermute | solution.py:19
  45.1 27.4 %collective-permute-start.3 = (bf16[43,64,128]{2,1,0:T(8,128)(2,1)S(1)}, bf16[43,64,128]{2,1,0:T(8,128)(2,1)S(1)}, u32[]{:S(2)}, u32[]{:S(2)}) collective-permute-start(bf16[43,64,128]{2,1,0:T(8,128)(2,1)S(1)} %get-tuple-element.21), channel_id=1, source_target_pairs={{0,30},{2,4},{4,2},{6,8},{8,6},{10,12},{12,10},{14,16},{16,14},{18... | collective-permute-start | bytes 2113544 | tf_op jit(solution)/shard_map/ppermute | solution.py:23
  57.2 11.8 %collective-permute-start.10 = (bf16[34,64,128]{2,1,0:T(8,128)(2,1)S(1)}, bf16[34,64,128]{2,1,0:T(8,128)(2,1)S(1)}, u32[]{:S(2)}, u32[]{:S(2)}) collective-permute-start(bf16[34,64,128]{2,1,0:T(8,128)(2,1)S(1)} %get-tuple-element.28.refs_3_), channel_id=1, source_target_pairs={{0,2},{2,0},{4,6},{6,4},{8,10},{10,8},{12,14},{14,12},{16,18},{18,... | collective-permute-start | bytes 1671176 | tf_op jit(solution)/shard_map/ppermute | solution.py:19
  60.5 8.6 %collective-permute-start.9 = (bf16[34,64,128]{2,1,0:T(8,128)(2,1)S(1)}, bf16[34,64,128]{2,1,0:T(8,128)(2,1)S(1)}, u32[]{:S(2)}, u32[]{:S(2)}) collective-permute-start(bf16[34,64,128]{2,1,0:T(8,128)(2,1)S(1)} %get-tuple-element.27.refs_2_), channel_id=1, source_target_pairs={{0,2},{2,0},{4,6},{6,4},{8,10},{10,8},{12,14},{14,12},{16,18},{18,... | collective-permute-start | bytes 1671176 | tf_op jit(solution)/shard_map/ppermute | solution.py:19
  61.8 11.3 %collective-permute-start.7 = (bf16[34,64,128]{2,1,0:T(8,128)(2,1)S(1)}, bf16[34,64,128]{2,1,0:T(8,128)(2,1)S(1)}, u32[]{:S(2)}, u32[]{:S(2)}) collective-permute-start(bf16[34,64,128]{2,1,0:T(8,128)(2,1)S(1)} %collective-permute-done.2.refs_1_), channel_id=1, source_target_pairs={{0,2},{1,27},{2,8},{3,1},{4,6},{5,31},{6,12},{7,5},{8,10},{9,3},{1... | collective-permute-start | bytes 1671176 | tf_op jit(solution)/shard_map/ppermute | solution.py:32
  61.8 10.7 %collective-permute-start.6 = (bf16[25,64,128]{2,1,0:T(8,128)(2,1)S(1)}, bf16[25,64,128]{2,1,0:T(8,128)(2,1)S(1)}, u32[]{:S(2)}, u32[]{:S(2)}) collective-permute-start(bf16[25,64,128]{2,1,0:T(8,128)(2,1)S(1)} %get-tuple-element.23), channel_id=1, source_target_pairs={{0,1},{1,0},{2,3},{3,2},{4,5},{5,4},{6,7},{7,6},{8,9},{9,8},{10,11... | collective-permute-start | bytes 1228808 | tf_op jit(solution)/shard_map/ppermute | solution.py:36

commit v8 on v7

--- a/solution.py
+++ b/solution.py
@@ -10,7 +10,8 @@
 RING = ("row", "col")
 EVERY = ("row", "col", "rep")
 EXTRA_ROWS = 2
-PEER_ROWS = 2
+EARLY_PEER_ROWS = 4
+OUT_PARTS = 3
 REST = 1
 VMEM_LIMIT = 24 * 2**20
 
@@ -182,13 +183,15 @@
             row_sem.at[index],
         )
 
-    def out_copy(half, row):
-        low = half * (band - 1)
-        count = band - 1 if half == 0 else band
+    bounds = [(2 * band - 1) * i // OUT_PARTS for i in range(OUT_PARTS + 1)]
+
+    def out_copy(part, row):
+        low = bounds[part]
+        count = bounds[part + 1] - low
         return pltpu.make_async_copy(
             result.at[row, pl.ds(first_slot(rep, row) + low, count)],
             out_ref.at[row, pl.ds(low, count)],
-            out_sem.at[half, row],
+            out_sem.at[part, row],
         )
 
     def place_left(rep_value):
@@ -264,29 +267,29 @@
         row_copy(source_refs[0], 0, 0, 0, count, index).wait()
     parts = [range(pairs)]
     if final:
-        middle = (band - 1 + rows_out) // 2 + 1
-        parts = [range(middle), range(middle, pairs)]
-    for half, part in enumerate(parts):
+        ends = [0, *((bound - 1 + rows_out) // 2 + 1 for bound in bounds[1:-1]), pairs]
+        parts = [range(low, high) for low, high in zip(ends, ends[1:])]
+    for part, some_pairs in enumerate(parts):
         if len(plan["counts"]) == slots:
-            multiply([(0, slots)], part)
+            multiply([(0, slots)], some_pairs)
         else:
             for rep_value in range(2):
                 for core_value in range(2):
 
                     @pl.when((rep == rep_value) & (core == core_value))
-                    def _(rep_value=rep_value, core_value=core_value, part=part):
+                    def _(rep_value=rep_value, core_value=core_value, some_pairs=some_pairs):
                         taken = sorted({slot for slot, *_ in plan["where"](rep_value, core_value)})
                         lows = [slot for slot in taken if slot - 1 not in taken]
                         highs = [slot + 1 for slot in taken if slot + 1 not in taken]
-                        multiply(list(zip(lows, highs)), part)
+                        multiply(list(zip(lows, highs)), some_pairs)
 
         if final:
             for row in range(rows_out):
-                out_copy(half, row).start()
+                out_copy(part, row).start()
     if final:
-        for half in range(2):
+        for part in range(OUT_PARTS):
             for row in range(rows_out):
-                out_copy(half, row).wait()
+                out_copy(part, row).wait()
 
 
 def partial_product(turned, sources, where, partial, rows_out, band, kind):
@@ -320,7 +323,7 @@
         out_spec = pl.BlockSpec(memory_space=pl.ANY)
         scratch += [
             pltpu.VMEM((rows_out, columns, block, block), jnp.bfloat16),
-            pltpu.SemaphoreType.DMA((2, rows_out)),
+            pltpu.SemaphoreType.DMA((OUT_PARTS, rows_out)),
         ]
     else:
         out_shape = pltpu.VMEM((columns // 2, rows_out * block, 2 * block), kind)
@@ -359,8 +362,8 @@
     turned, turned_send = turned_left(a_blocks, a_extent, rows_out)
     turned_across = over_rep(turned_send)
     across = after(across, turned_send)
-    parts = tuple(i * PEER_ROWS * band for i in range(rows // PEER_ROWS))
-    part_sizes = (PEER_ROWS * band,) * len(parts)
+    parts = (0, EARLY_PEER_ROWS * band)
+    part_sizes = (EARLY_PEER_ROWS * band, (rows - EARLY_PEER_ROWS) * band)
     picks = picked(across, [*spans[:2], *zip(parts, parts)], [*sizes[:2], *part_sizes], b_extent)
     onward, across_own = picks[:2], picks[2:]
     across_outer = [to_outer_neighbour(x, ring) for x in onward]
@@ -397,7 +400,7 @@
 
     whole = ((0,), (0,)), (rows * band,)
     only_extra = ((0,), (0,)), (extra_size,)
-    thirds = (parts, parts), part_sizes
+    pieces = (parts, parts), part_sizes
     count = len(parts)
     total = partial_product(
         turned,
@@ -419,7 +422,7 @@
         turned_across,
         [*across_own, *across_peer],
         where_of(
-            {"own": (range(count), *thirds), "peer": (range(count, 2 * count), *thirds)}
+            {"own": (range(count), *pieces), "peer": (range(count, 2 * count), *pieces)}
         ),
         total,
         rows_out,

time: 76.8 us -> 76.9 us (level)
    ppermute x3, waiting for transfers between devices: 8.48 us -> 6.87 us  [to_outer_neighbour(): lax.ppermute(x, RING, [(g, (g + 2 * (g % 2) - 1) % ring) for g in range(r...]
    ppermute x3, waiting for transfers between devices: 31.2 us -> 32.3 us  [over_rep(): return lax.ppermute(x, 'rep', [(0, 1), (1, 0)])]
    ppermute x3, starting transfers between devices: 7.24 us -> 6.37 us  [over_rep(): return lax.ppermute(x, 'rep', [(0, 1), (1, 0)])]
    ppermute x4 -> x3, starting transfers between devices: 3.34 us -> 4.06 us  [to_chip_peer(): return lax.ppermute(x, RING, [(g, g ^ 1) for g in range(ring)])]
  transfers between devices with their start and end apart: 12 -> 11, of which waited for: 5 -> 5; matrix products, arithmetic and copies ran while one was open for 2% -> 2% of each run, Pallas kernels for 12% -> 11%
where the time goes in v8:
time: 76.9 us; the launch traced here: 76.7 us
  waiting for transfers between devices  41.5 us (54%)
  starting transfers between devices  21.3 us (28%)
  Pallas kernels  11.9 us (15%)
  other arithmetic  1.77 us (2%)
    ppermute x3, waiting for transfers between devices, over_rep(): return lax.ppermute(x, 'rep', [(0, 1), (1, 0)])  32.3 us
    ppermute x3, starting transfers between devices, to_outer_neighbour(): lax.ppermute(x, RING, [(g, (g + 2 * (g % 2) - 1) % ring) for g in range(r...  10.3 us
    pallas_call x3, Pallas kernels, partial_product(): pl.pallas_call(functools.partial(product_kernel, plan), out_shape=out_sha...  9.16 us
    ppermute x3, waiting for transfers between devices, to_outer_neighbour(): lax.ppermute(x, RING, [(g, (g + 2 * (g % 2) - 1) % ring) for g in range(r...  6.87 us
    ppermute x3, starting transfers between devices, over_rep(): return lax.ppermute(x, 'rep', [(0, 1), (1, 0)])  6.37 us
    ppermute x3, starting transfers between devices, to_chip_peer(): return lax.ppermute(x, RING, [(g, g ^ 1) for g in range(ring)])  4.06 us
    ppermute x2, waiting for transfers between devices, to_second_neighbour(): return lax.ppermute(x, EVERY, pairs)  2.39 us
    mul x1, other arithmetic, local(): b_own = b_blocks * live.astype(b_blocks.dtype)  1.77 us
  transfers between devices with their start and end apart: 11, of which 5 were waited for; matrix products, arithmetic and copies ran while one was open for 2% of the time, Pallas kernels for 11%

profile of v8, /device:TPU:0, one launch (start us, length us, event | category | flops | bytes accessed | tf_op | source)
XLA Modules:
  0.0 76.7 jit_solution(8748577689825399500)
XLA Ops:
  0.0 2.9 %collective-permute-start.1 = (bf16[6,17,64,128]{3,2,1,0:T(8,128)(2,1)}, bf16[6,17,64,128]{3,2,1,0:T(8,128)(2,1)S(1)}, u32[]{:S(2)}, u32[]{:S(2)}) collective-permute-start(bf16[6,17,64,128]{3,2,1,0:T(8,128)(2,1)} %param.5), channel_id=1, source_target_pairs={{0,1},{1,0},{2,3},{3,2},{4,5},{5,4},{6,7},{7,6},{8,9},{9,8},{10,11... | collective-permute-start | bytes 5013512 | tf_op jit(solution)/shard_map/ppermute | solution.py:37
  2.9 1.8 %compare_select_fusion = bf16[6,17,64,128]{3,2,1,0:T(8,128)(2,1)S(1)} fusion(bf16[6,17,64,128]{3,2,1,0:T(8,128)(2,1)} %param.5, s32[6]{0:T(128)} %refs_0_.1, s32[17]{0:T(128)S(1)} %add_abs_fusion), kind=kLoop, calls=%fused_computation | loop fusion | flops 1671168 | bytes 3342428 | tf_op jit(solution)/shard_map/mul | solution.py:358
  4.7 0.0 copy-start.1
  4.7 3.8 %collective-permute-start.4 = (bf16[6,17,64,128]{3,2,1,0:T(8,128)(2,1)S(1)}, bf16[6,17,64,128]{3,2,1,0:T(8,128)(2,1)S(1)}, u32[]{:S(2)}, u32[]{:S(2)}) collective-permute-start(bf16[6,17,64,128]{3,2,1,0:T(8,128)(2,1)S(1)} %compare_select_fusion), channel_id=1, source_target_pairs={{0,30},{2,4},{4,2},{6,8},{8,6},{10,12},{12,10},{14,16},{16,14},{18... | collective-permute-start | bytes 5013512 | tf_op jit(solution)/shard_map/ppermute | solution.py:24
  8.5 0.0 collective-permute-start.5
  8.5 1.1 %shard_map.46 = (bf16[3,128,1152]{2,1,0:T(8,128)(2,1)S(1)}, bf16[3,128,1152]{2,1,0:T(8,128)(2,1)S(1)}) custom-call(s32[6]{0:T(128)S(1)} %copy-done.2, bf16[6,17,64,128]{3,2,1,0:T(8,128)(2,1)S(1)} %copy-done), custom_call_target="tpu_custom_call" | custom-call | tf_op jit(solution)/shard_map/pallas_call | solution.py:72
  9.6 0.6 collective-permute-start
  10.2 30.3 %collective-permute-done.1 = bf16[6,17,64,128]{3,2,1,0:T(8,128)(2,1)S(1)} collective-permute-done((bf16[6,17,64,128]{3,2,1,0:T(8,128)(2,1)}, bf16[6,17,64,128]{3,2,1,0:T(8,128)(2,1)S(1)}, u32[]{:S(2)}, u32[]{:S(2)}) %collective-permute-start.1) | collective-permute-done | bytes 1671200 | tf_op jit(solution)/shard_map/ppermute | solution.py:37
  40.5 1.3 %shard_map.47 = (bf16[34,64,128]{2,1,0:T(8,128)(2,1)S(1)}, bf16[43,64,128]{2,1,0:T(8,128)(2,1)S(1)}, bf16[68,64,128]{2,1,0:T(8,128)(2,1)S(1)}, bf16[34,64,128]{2,1,0:T(8,128)(2,1)S(1)}) custom-call(s32[6]{0:T(128)S(1)} %copy-done.1, bf16[102,64,128]{2,1,0:T(8,128)(2,1)S(1)} %bitcast.9), custom_call_target="tpu_custom_call" | custom-call | tf_op jit(solution)/shard_map/pallas_call | solution.py:136
  41.8 2.6 %collective-permute-start.2 = (bf16[34,64,128]{2,1,0:T(8,128)(2,1)S(1)}, bf16[34,64,128]{2,1,0:T(8,128)(2,1)S(1)}, u32[]{:S(2)}, u32[]{:S(2)}) collective-permute-start(bf16[34,64,128]{2,1,0:T(8,128)(2,1)S(1)} %get-tuple-element.18), channel_id=1, source_target_pairs={{0,30},{2,4},{4,2},{6,8},{8,6},{10,12},{12,10},{14,16},{16,14},{18... | collective-permute-start | bytes 1671176 | tf_op jit(solution)/shard_map/ppermute | solution.py:24
  44.4 0.0 collective-permute-start.8
  44.5 0.3 shard_map.48
  44.8 0.5 collective-permute-start.10
  45.3 3.9 %collective-permute-start.3 = (bf16[43,64,128]{2,1,0:T(8,128)(2,1)S(1)}, bf16[43,64,128]{2,1,0:T(8,128)(2,1)S(1)}, u32[]{:S(2)}, u32[]{:S(2)}) collective-permute-start(bf16[43,64,128]{2,1,0:T(8,128)(2,1)S(1)} %get-tuple-element.19), channel_id=1, source_target_pairs={{0,30},{2,4},{4,2},{6,8},{8,6},{10,12},{12,10},{14,16},{16,14},{18... | collective-permute-start | bytes 2113544 | tf_op jit(solution)/shard_map/ppermute | solution.py:24
  49.2 6.9 %collective-permute-done.2.refs_1_ = bf16[34,64,128]{2,1,0:T(8,128)(2,1)S(1)} collective-permute-done((bf16[34,64,128]{2,1,0:T(8,128)(2,1)S(1)}, bf16[34,64,128]{2,1,0:T(8,128)(2,1)S(1)}, u32[]{:S(2)}, u32[]{:S(2)}) %collective-permute-start.2) | collective-permute-done | bytes 557088 | tf_op jit(solution)/shard_map/ppermute | solution.py:24
  56.1 4.1 %collective-permute-start.9 = (bf16[34,64,128]{2,1,0:T(8,128)(2,1)S(1)}, bf16[34,64,128]{2,1,0:T(8,128)(2,1)S(1)}, u32[]{:S(2)}, u32[]{:S(2)}) collective-permute-start(bf16[34,64,128]{2,1,0:T(8,128)(2,1)S(1)} %get-tuple-element.24.refs_2_), channel_id=1, source_target_pairs={{0,2},{2,0},{4,6},{6,4},{8,10},{10,8},{12,14},{14,12},{16,18},{18,... | collective-permute-start | bytes 1671176 | tf_op jit(solution)/shard_map/ppermute | solution.py:20
  60.1 0.0 collective-permute-start.7
  60.2 1.5 %collective-permute-done.10.refs_4_ = bf16[34,64,128]{2,1,0:T(8,128)(2,1)S(1)} collective-permute-done((bf16[34,64,128]{2,1,0:T(8,128)(2,1)S(1)}, bf16[34,64,128]{2,1,0:T(8,128)(2,1)S(1)}, u32[]{:S(2)}, u32[]{:S(2)}) %collective-permute-start.10) | collective-permute-done | bytes 557088 | tf_op jit(solution)/shard_map/ppermute | solution.py:33
  61.6 2.8 %collective-permute-start.6 = (bf16[25,64,128]{2,1,0:T(8,128)(2,1)S(1)}, bf16[25,64,128]{2,1,0:T(8,128)(2,1)S(1)}, u32[]{:S(2)}, u32[]{:S(2)}) collective-permute-start(bf16[25,64,128]{2,1,0:T(8,128)(2,1)S(1)} %get-tuple-element.21), channel_id=1, source_target_pairs={{0,1},{1,0},{2,3},{3,2},{4,5},{5,4},{6,7},{7,6},{8,9},{9,8},{10,11... | collective-permute-start | bytes 1228808 | tf_op jit(solution)/shard_map/ppermute | solution.py:37
  64.5 3.5 %shard_map.49.refs_5_ = bf16[18,384,256]{2,1,0:T(8,128)(2,1)S(1)} custom-call(bf16[3,128,1152]{2,1,0:T(8,128)(2,1)S(1)} %get-tuple-element.25.refs_0_, bf16[102,64,128]{2,1,0:T(8,128)(2,1)S(1)} %bitcast.5, bf16[102,64,128]{2,1,0:T(8,128)(2,1)S(1)} %bitcast.8, bf16[102,64,128]{2,1,0:T(8,128)(2,1)S(1)} %bitcast.7, ...), custom_call_target="tpu_custom_call" | custom-call | tf_op jit(solution)/shard_map/pallas_call | solution.py:331
  68.0 2.5 %shard_map.50.refs_5_ = f32[18,384,256]{2,1,0:T(8,128)S(1)} custom-call(bf16[3,128,1152]{2,1,0:T(8,128)(2,1)S(1)} %collective-permute-done.refs_0_, bf16[68,64,128]{2,1,0:T(8,128)(2,1)S(1)} %get-tuple-element.22.refs_1_, bf16[34,64,128]{2,1,0:T(8,128)(2,1)S(1)} %get-tuple-element.24.refs_2_, bf16[68,64,128]{2,1,0:T(8,128)(2,1)S(1)} %collective-permute-done.8.refs_3_, ...), custom_call_target="tpu_custom_call" | custom-call | tf_op jit(solution)/shard_map/pallas_call | solution.py:331
  70.5 2.0 %collective-permute-done.6.refs_3_ = bf16[25,64,128]{2,1,0:T(8,128)(2,1)S(1)} collective-permute-done((bf16[25,64,128]{2,1,0:T(8,128)(2,1)S(1)}, bf16[25,64,128]{2,1,0:T(8,128)(2,1)S(1)}, u32[]{:S(2)}, u32[]{:S(2)}) %collective-permute-start.6) | collective-permute-done | bytes 409632 | tf_op jit(solution)/shard_map/ppermute | solution.py:37
  72.5 0.9 %collective-permute-done.7.refs_4_ = bf16[34,64,128]{2,1,0:T(8,128)(2,1)S(1)} collective-permute-done((bf16[34,64,128]{2,1,0:T(8,128)(2,1)S(1)}, bf16[34,64,128]{2,1,0:T(8,128)(2,1)S(1)}, u32[]{:S(2)}, u32[]{:S(2)}) %collective-permute-start.7) | collective-permute-done | bytes 557088 | tf_op jit(solution)/shard_map/ppermute | solution.py:33
  73.4 3.2 %shard_map.51 = bf16[3,33,128,128]{3,2,1,0:T(8,128)(2,1)} custom-call(bf16[3,128,1152]{2,1,0:T(8,128)(2,1)S(1)} %collective-permute-done.refs_0_, bf16[34,64,128]{2,1,0:T(8,128)(2,1)S(1)} %collective-permute-done.2.refs_1_, bf16[43,64,128]{2,1,0:T(8,128)(2,1)S(1)} %collective-permute-done.3.refs_2_, bf16[25,64,128]{2,1,0:T(8,128)(2,1)S(1)} %collective-permute-done.6.refs_3_, ...), custom_call_target="tpu_custom_call" | custom-call | tf_op jit(solution)/shard_map/pallas_call | solution.py:331
  (12 shorter events, 0.0 us)
Async XLA Ops:
  0.0 40.5 %collective-permute-start.1 = (bf16[6,17,64,128]{3,2,1,0:T(8,128)(2,1)}, bf16[6,17,64,128]{3,2,1,0:T(8,128)(2,1)S(1)}, u32[]{:S(2)}, u32[]{:S(2)}) collective-permute-start(bf16[6,17,64,128]{3,2,1,0:T(8,128)(2,1)} %param.5), channel_id=1, source_target_pairs={{0,1},{1,0},{2,3},{3,2},{4,5},{5,4},{6,7},{7,6},{8,9},{9,8},{10,11... | collective-permute-start | bytes 5013512 | tf_op jit(solution)/shard_map/ppermute | solution.py:37
  2.9 5.6 %copy-start = (bf16[6,17,64,128]{3,2,1,0:T(8,128)(2,1)S(1)}, bf16[6,17,64,128]{3,2,1,0:T(8,128)(2,1)}, u32[]{:S(2)}) copy-start(bf16[6,17,64,128]{3,2,1,0:T(8,128)(2,1)} %a_ref.1) | copy-start | bytes 5013508
  2.9 5.6 %copy-start.2 = (s32[6]{0:T(128)S(1)}, s32[6]{0:T(128)}, u32[]{:S(2)}) copy-start(s32[6]{0:T(128)} %extent_ref.1) | copy-start | bytes 76
  4.7 35.8 %copy-start.1 = (s32[6]{0:T(128)S(1)}, s32[6]{0:T(128)}, u32[]{:S(2)}) copy-start(s32[6]{0:T(128)} %refs_0_.1) | copy-start | bytes 76
  4.7 39.7 %collective-permute-start.4 = (bf16[6,17,64,128]{3,2,1,0:T(8,128)(2,1)S(1)}, bf16[6,17,64,128]{3,2,1,0:T(8,128)(2,1)S(1)}, u32[]{:S(2)}, u32[]{:S(2)}) collective-permute-start(bf16[6,17,64,128]{3,2,1,0:T(8,128)(2,1)S(1)} %compare_select_fusion), channel_id=1, source_target_pairs={{0,30},{2,4},{4,2},{6,8},{8,6},{10,12},{12,10},{14,16},{16,14},{18... | collective-permute-start | bytes 5013512 | tf_op jit(solution)/shard_map/ppermute | solution.py:24
  8.5 35.9 %collective-permute-start.5 = (bf16[6,17,64,128]{3,2,1,0:T(8,128)(2,1)S(1)}, bf16[6,17,64,128]{3,2,1,0:T(8,128)(2,1)S(1)}, u32[]{:S(2)}, u32[]{:S(2)}) collective-permute-start(bf16[6,17,64,128]{3,2,1,0:T(8,128)(2,1)S(1)} %compare_select_fusion), channel_id=1, source_target_pairs={{0,2},{2,0},{4,6},{6,4},{8,10},{10,8},{12,14},{14,12},{16,18},{18,... | collective-permute-start | bytes 5013512 | tf_op jit(solution)/shard_map/ppermute | solution.py:20
  9.6 50.5 %collective-permute-start = (bf16[3,128,1152]{2,1,0:T(8,128)(2,1)S(1)}, bf16[3,128,1152]{2,1,0:T(8,128)(2,1)S(1)}, u32[]{:S(2)}, u32[]{:S(2)}) collective-permute-start(bf16[3,128,1152]{2,1,0:T(8,128)(2,1)S(1)} %get-tuple-element.16), channel_id=1, source_target_pairs={{0,1},{1,0},{2,3},{3,2},{4,5},{5,4},{6,7},{7,6},{8,9},{9,8},{10,11... | collective-permute-start | bytes 2654216 | tf_op jit(solution)/shard_map/ppermute | solution.py:37
  41.8 14.3 %collective-permute-start.2 = (bf16[34,64,128]{2,1,0:T(8,128)(2,1)S(1)}, bf16[34,64,128]{2,1,0:T(8,128)(2,1)S(1)}, u32[]{:S(2)}, u32[]{:S(2)}) collective-permute-start(bf16[34,64,128]{2,1,0:T(8,128)(2,1)S(1)} %get-tuple-element.18), channel_id=1, source_target_pairs={{0,30},{2,4},{4,2},{6,8},{8,6},{10,12},{12,10},{14,16},{16,14},{18... | collective-permute-start | bytes 1671176 | tf_op jit(solution)/shard_map/ppermute | solution.py:24
  44.4 23.5 %collective-permute-start.8 = (bf16[68,64,128]{2,1,0:T(8,128)(2,1)S(1)}, bf16[68,64,128]{2,1,0:T(8,128)(2,1)S(1)}, u32[]{:S(2)}, u32[]{:S(2)}) collective-permute-start(bf16[68,64,128]{2,1,0:T(8,128)(2,1)S(1)} %get-tuple-element.22.refs_1_), channel_id=1, source_target_pairs={{0,2},{2,0},{4,6},{6,4},{8,10},{10,8},{12,14},{14,12},{16,18},{18,... | collective-permute-start | bytes 3342344 | tf_op jit(solution)/shard_map/ppermute | solution.py:20
  44.8 16.8 %collective-permute-start.10 = (bf16[34,64,128]{2,1,0:T(8,128)(2,1)S(1)}, bf16[34,64,128]{2,1,0:T(8,128)(2,1)S(1)}, u32[]{:S(2)}, u32[]{:S(2)}) collective-permute-start(bf16[34,64,128]{2,1,0:T(8,128)(2,1)S(1)} %get-tuple-element.26), channel_id=1, source_target_pairs={{0,2},{1,27},{2,8},{3,1},{4,6},{5,31},{6,12},{7,5},{8,10},{9,3},{1... | collective-permute-start | bytes 1671176 | tf_op jit(solution)/shard_map/ppermute | solution.py:33
  45.3 27.1 %collective-permute-start.3 = (bf16[43,64,128]{2,1,0:T(8,128)(2,1)S(1)}, bf16[43,64,128]{2,1,0:T(8,128)(2,1)S(1)}, u32[]{:S(2)}, u32[]{:S(2)}) collective-permute-start(bf16[43,64,128]{2,1,0:T(8,128)(2,1)S(1)} %get-tuple-element.19), channel_id=1, source_target_pairs={{0,30},{2,4},{4,2},{6,8},{8,6},{10,12},{12,10},{14,16},{16,14},{18... | collective-permute-start | bytes 2113544 | tf_op jit(solution)/shard_map/ppermute | solution.py:24
  56.1 11.9 %collective-permute-start.9 = (bf16[34,64,128]{2,1,0:T(8,128)(2,1)S(1)}, bf16[34,64,128]{2,1,0:T(8,128)(2,1)S(1)}, u32[]{:S(2)}, u32[]{:S(2)}) collective-permute-start(bf16[34,64,128]{2,1,0:T(8,128)(2,1)S(1)} %get-tuple-element.24.refs_2_), channel_id=1, source_target_pairs={{0,2},{2,0},{4,6},{6,4},{8,10},{10,8},{12,14},{14,12},{16,18},{18,... | collective-permute-start | bytes 1671176 | tf_op jit(solution)/shard_map/ppermute | solution.py:20
  60.1 13.2 %collective-permute-start.7 = (bf16[34,64,128]{2,1,0:T(8,128)(2,1)S(1)}, bf16[34,64,128]{2,1,0:T(8,128)(2,1)S(1)}, u32[]{:S(2)}, u32[]{:S(2)}) collective-permute-start(bf16[34,64,128]{2,1,0:T(8,128)(2,1)S(1)} %collective-permute-done.2.refs_1_), channel_id=1, source_target_pairs={{0,2},{1,27},{2,8},{3,1},{4,6},{5,31},{6,12},{7,5},{8,10},{9,3},{1... | collective-permute-start | bytes 1671176 | tf_op jit(solution)/shard_map/ppermute | solution.py:33
  61.6 10.8 %collective-permute-start.6 = (bf16[25,64,128]{2,1,0:T(8,128)(2,1)S(1)}, bf16[25,64,128]{2,1,0:T(8,128)(2,1)S(1)}, u32[]{:S(2)}, u32[]{:S(2)}) collective-permute-start(bf16[25,64,128]{2,1,0:T(8,128)(2,1)S(1)} %get-tuple-element.21), channel_id=1, source_target_pairs={{0,1},{1,0},{2,3},{3,2},{4,5},{5,4},{6,7},{7,6},{8,9},{9,8},{10,11... | collective-permute-start | bytes 1228808 | tf_op jit(solution)/shard_map/ppermute | solution.py:37

commit v9 on v8

--- a/solution.py
+++ b/solution.py
@@ -420,9 +420,13 @@
     )
     total = partial_product(
         turned_across,
-        [*across_own, *across_peer],
+        [*across_own, *across_peer, across_outer[0]],
         where_of(
-            {"own": (range(count), *pieces), "peer": (range(count, 2 * count), *pieces)}
+            {
+                "own": (range(count), *pieces),
+                "peer": (range(count, 2 * count), *pieces),
+                "outer": ((2 * count,), [x[:1] for x in starts], sizes[:1]),
+            }
         ),
         total,
         rows_out,
@@ -431,8 +435,13 @@
     )
     return partial_product(
         turned_across,
-        [*across_outer, across_extra],
-        where_of({"outer": ((0, 1, 2), starts, sizes), "extra": ((3,), *only_extra)}),
+        [*across_outer[1:], across_extra],
+        where_of(
+            {
+                "outer": ((0, 1), [x[1:] for x in starts], sizes[1:]),
+                "extra": ((2,), *only_extra),
+            }
+        ),
         total,
         rows_out,
         band,

time: 76.9 us -> 76.5 us (level)
  transfers between devices with their start and end apart: 11 -> 11, of which waited for: 5 -> 5; matrix products, arithmetic and copies ran while one was open for 2% -> 2% of each run, Pallas kernels for 11% -> 12%
where the time goes in v9:
time: 76.5 us
  waiting for transfers between devices  41.4 us (54%)
  starting transfers between devices  20.9 us (27%)
  Pallas kernels  12.2 us (16%)
  other arithmetic  1.77 us (2%)
    ppermute x3, waiting for transfers between devices, over_rep(): return lax.ppermute(x, 'rep', [(0, 1), (1, 0)])  32.1 us
    ppermute x3, starting transfers between devices, to_outer_neighbour(): lax.ppermute(x, RING, [(g, (g + 2 * (g % 2) - 1) % ring) for g in range(r...  10.2 us
    pallas_call x3, Pallas kernels, partial_product(): pl.pallas_call(functools.partial(product_kernel, plan), out_shape=out_sha...  9.34 us
    ppermute x3, waiting for transfers between devices, to_outer_neighbour(): lax.ppermute(x, RING, [(g, (g + 2 * (g % 2) - 1) % ring) for g in range(r...  6.9 us
    ppermute x3, starting transfers between devices, over_rep(): return lax.ppermute(x, 'rep', [(0, 1), (1, 0)])  6.01 us
    ppermute x3, starting transfers between devices, to_chip_peer(): return lax.ppermute(x, RING, [(g, g ^ 1) for g in range(ring)])  4.12 us
    ppermute x2, waiting for transfers between devices, to_second_neighbour(): return lax.ppermute(x, EVERY, pairs)  2.34 us
    mul x1, other arithmetic, local(): b_own = b_blocks * live.astype(b_blocks.dtype)  1.77 us
  transfers between devices with their start and end apart: 11, of which 5 were waited for; matrix products, arithmetic and copies ran while one was open for 2% of the time, Pallas kernels for 12%

profile of v9, /device:TPU:0, one launch (start us, length us, event | category | flops | bytes accessed | tf_op | source)
XLA Modules:
  0.0 76.5 jit_solution(590666935160283841)
XLA Ops:
  0.0 2.9 %collective-permute-start.1 = (bf16[6,17,64,128]{3,2,1,0:T(8,128)(2,1)}, bf16[6,17,64,128]{3,2,1,0:T(8,128)(2,1)S(1)}, u32[]{:S(2)}, u32[]{:S(2)}) collective-permute-start(bf16[6,17,64,128]{3,2,1,0:T(8,128)(2,1)} %param.5), channel_id=1, source_target_pairs={{0,1},{1,0},{2,3},{3,2},{4,5},{5,4},{6,7},{7,6},{8,9},{9,8},{10,11... | collective-permute-start | bytes 5013512 | tf_op jit(solution)/shard_map/ppermute | solution.py:37
  2.9 1.8 %compare_select_fusion = bf16[6,17,64,128]{3,2,1,0:T(8,128)(2,1)S(1)} fusion(bf16[6,17,64,128]{3,2,1,0:T(8,128)(2,1)} %param.5, s32[6]{0:T(128)} %refs_0_.1, s32[17]{0:T(128)S(1)} %add_abs_fusion), kind=kLoop, calls=%fused_computation | loop fusion | flops 1671168 | bytes 3342428 | tf_op jit(solution)/shard_map/mul | solution.py:358
  4.7 0.0 copy-start.1
  4.7 3.8 %collective-permute-start.3 = (bf16[6,17,64,128]{3,2,1,0:T(8,128)(2,1)S(1)}, bf16[6,17,64,128]{3,2,1,0:T(8,128)(2,1)S(1)}, u32[]{:S(2)}, u32[]{:S(2)}) collective-permute-start(bf16[6,17,64,128]{3,2,1,0:T(8,128)(2,1)S(1)} %compare_select_fusion), channel_id=1, source_target_pairs={{0,30},{2,4},{4,2},{6,8},{8,6},{10,12},{12,10},{14,16},{16,14},{18... | collective-permute-start | bytes 5013512 | tf_op jit(solution)/shard_map/ppermute | solution.py:24
  8.5 1.1 %shard_map.46 = (bf16[3,128,1152]{2,1,0:T(8,128)(2,1)S(1)}, bf16[3,128,1152]{2,1,0:T(8,128)(2,1)S(1)}) custom-call(s32[6]{0:T(128)S(1)} %copy-done.2, bf16[6,17,64,128]{3,2,1,0:T(8,128)(2,1)S(1)} %copy-done), custom_call_target="tpu_custom_call" | custom-call | tf_op jit(solution)/shard_map/pallas_call | solution.py:72
  9.6 0.6 collective-permute-start
  10.2 30.3 %collective-permute-done.1 = bf16[6,17,64,128]{3,2,1,0:T(8,128)(2,1)S(1)} collective-permute-done((bf16[6,17,64,128]{3,2,1,0:T(8,128)(2,1)}, bf16[6,17,64,128]{3,2,1,0:T(8,128)(2,1)S(1)}, u32[]{:S(2)}, u32[]{:S(2)}) %collective-permute-start.1) | collective-permute-done | bytes 1671200 | tf_op jit(solution)/shard_map/ppermute | solution.py:37
  40.5 1.4 %shard_map.47 = (bf16[34,64,128]{2,1,0:T(8,128)(2,1)S(1)}, bf16[43,64,128]{2,1,0:T(8,128)(2,1)S(1)}, bf16[68,64,128]{2,1,0:T(8,128)(2,1)S(1)}, bf16[34,64,128]{2,1,0:T(8,128)(2,1)S(1)}) custom-call(s32[6]{0:T(128)S(1)} %copy-done.1, bf16[102,64,128]{2,1,0:T(8,128)(2,1)S(1)} %bitcast.9), custom_call_target="tpu_custom_call" | custom-call | tf_op jit(solution)/shard_map/pallas_call | solution.py:136
  41.9 2.5 %collective-permute-start.6 = (bf16[34,64,128]{2,1,0:T(8,128)(2,1)S(1)}, bf16[34,64,128]{2,1,0:T(8,128)(2,1)S(1)}, u32[]{:S(2)}, u32[]{:S(2)}) collective-permute-start(bf16[34,64,128]{2,1,0:T(8,128)(2,1)S(1)} %get-tuple-element.21), channel_id=1, source_target_pairs={{0,30},{2,4},{4,2},{6,8},{8,6},{10,12},{12,10},{14,16},{16,14},{18... | collective-permute-start | bytes 1671176 | tf_op jit(solution)/shard_map/ppermute | solution.py:24
  44.4 0.0 collective-permute-start.8
  44.4 0.0 collective-permute-done.3
  44.5 0.3 shard_map.48
  44.8 0.5 collective-permute-start.10
  45.3 3.9 %collective-permute-start.2 = (bf16[43,64,128]{2,1,0:T(8,128)(2,1)S(1)}, bf16[43,64,128]{2,1,0:T(8,128)(2,1)S(1)}, u32[]{:S(2)}, u32[]{:S(2)}) collective-permute-start(bf16[43,64,128]{2,1,0:T(8,128)(2,1)S(1)} %get-tuple-element.18), channel_id=1, source_target_pairs={{0,30},{2,4},{4,2},{6,8},{8,6},{10,12},{12,10},{14,16},{16,14},{18... | collective-permute-start | bytes 2113544 | tf_op jit(solution)/shard_map/ppermute | solution.py:24
  49.3 6.9 %collective-permute-done.6.refs_5_ = bf16[34,64,128]{2,1,0:T(8,128)(2,1)S(1)} collective-permute-done((bf16[34,64,128]{2,1,0:T(8,128)(2,1)S(1)}, bf16[34,64,128]{2,1,0:T(8,128)(2,1)S(1)}, u32[]{:S(2)}, u32[]{:S(2)}) %collective-permute-start.6) | collective-permute-done | bytes 557088 | tf_op jit(solution)/shard_map/ppermute | solution.py:24
  56.2 4.1 %collective-permute-start.9 = (bf16[34,64,128]{2,1,0:T(8,128)(2,1)S(1)}, bf16[34,64,128]{2,1,0:T(8,128)(2,1)S(1)}, u32[]{:S(2)}, u32[]{:S(2)}) collective-permute-start(bf16[34,64,128]{2,1,0:T(8,128)(2,1)S(1)} %get-tuple-element.24.refs_2_), channel_id=1, source_target_pairs={{0,2},{2,0},{4,6},{6,4},{8,10},{10,8},{12,14},{14,12},{16,18},{18,... | collective-permute-start | bytes 1671176 | tf_op jit(solution)/shard_map/ppermute | solution.py:20
  60.3 0.0 collective-permute-start.7
  60.3 1.3 %collective-permute-done.10.refs_4_ = bf16[34,64,128]{2,1,0:T(8,128)(2,1)S(1)} collective-permute-done((bf16[34,64,128]{2,1,0:T(8,128)(2,1)S(1)}, bf16[34,64,128]{2,1,0:T(8,128)(2,1)S(1)}, u32[]{:S(2)}, u32[]{:S(2)}) %collective-permute-start.10) | collective-permute-done | bytes 557088 | tf_op jit(solution)/shard_map/ppermute | solution.py:33
  61.6 2.5 %collective-permute-start.5 = (bf16[25,64,128]{2,1,0:T(8,128)(2,1)S(1)}, bf16[25,64,128]{2,1,0:T(8,128)(2,1)S(1)}, u32[]{:S(2)}, u32[]{:S(2)}) collective-permute-start(bf16[25,64,128]{2,1,0:T(8,128)(2,1)S(1)} %get-tuple-element.20), channel_id=1, source_target_pairs={{0,1},{1,0},{2,3},{3,2},{4,5},{5,4},{6,7},{7,6},{8,9},{9,8},{10,11... | collective-permute-start | bytes 1228808 | tf_op jit(solution)/shard_map/ppermute | solution.py:37
  64.1 3.5 %shard_map.49.refs_6_ = bf16[18,384,256]{2,1,0:T(8,128)(2,1)S(1)} custom-call(bf16[3,128,1152]{2,1,0:T(8,128)(2,1)S(1)} %get-tuple-element.25.refs_0_, bf16[102,64,128]{2,1,0:T(8,128)(2,1)S(1)} %bitcast.5, bf16[102,64,128]{2,1,0:T(8,128)(2,1)S(1)} %bitcast.8, bf16[102,64,128]{2,1,0:T(8,128)(2,1)S(1)} %bitcast.7, ...), custom_call_target="tpu_custom_call" | custom-call | tf_op jit(solution)/shard_map/pallas_call | solution.py:331
  67.6 2.8 %shard_map.50.refs_4_ = f32[18,384,256]{2,1,0:T(8,128)S(1)} custom-call(bf16[3,128,1152]{2,1,0:T(8,128)(2,1)S(1)} %collective-permute-done.refs_0_, bf16[68,64,128]{2,1,0:T(8,128)(2,1)S(1)} %get-tuple-element.22.refs_1_, bf16[34,64,128]{2,1,0:T(8,128)(2,1)S(1)} %get-tuple-element.24.refs_2_, bf16[68,64,128]{2,1,0:T(8,128)(2,1)S(1)} %collective-permute-done.8.refs_3_, ...), custom_call_target="tpu_custom_call" | custom-call | tf_op jit(solution)/shard_map/pallas_call | solution.py:331
  70.4 1.8 %collective-permute-done.5.refs_2_ = bf16[25,64,128]{2,1,0:T(8,128)(2,1)S(1)} collective-permute-done((bf16[25,64,128]{2,1,0:T(8,128)(2,1)S(1)}, bf16[25,64,128]{2,1,0:T(8,128)(2,1)S(1)}, u32[]{:S(2)}, u32[]{:S(2)}) %collective-permute-start.5) | collective-permute-done | bytes 409632 | tf_op jit(solution)/shard_map/ppermute | solution.py:37
  72.3 1.0 %collective-permute-done.7.refs_3_ = bf16[34,64,128]{2,1,0:T(8,128)(2,1)S(1)} collective-permute-done((bf16[34,64,128]{2,1,0:T(8,128)(2,1)S(1)}, bf16[34,64,128]{2,1,0:T(8,128)(2,1)S(1)}, u32[]{:S(2)}, u32[]{:S(2)}) %collective-permute-start.7) | collective-permute-done | bytes 557088 | tf_op jit(solution)/shard_map/ppermute | solution.py:33
  73.3 3.0 %shard_map.51 = bf16[3,33,128,128]{3,2,1,0:T(8,128)(2,1)} custom-call(bf16[3,128,1152]{2,1,0:T(8,128)(2,1)S(1)} %collective-permute-done.refs_0_, bf16[43,64,128]{2,1,0:T(8,128)(2,1)S(1)} %collective-permute-done.2.refs_1_, bf16[25,64,128]{2,1,0:T(8,128)(2,1)S(1)} %collective-permute-done.5.refs_2_, bf16[34,64,128]{2,1,0:T(8,128)(2,1)S(1)} %collective-permute-done.7.refs_3_, ...), custom_call_target="tpu_custom_call" | custom-call | tf_op jit(solution)/shard_map/pallas_call | solution.py:331
  (12 shorter events, 0.0 us)
Async XLA Ops:
  0.0 40.5 %collective-permute-start.1 = (bf16[6,17,64,128]{3,2,1,0:T(8,128)(2,1)}, bf16[6,17,64,128]{3,2,1,0:T(8,128)(2,1)S(1)}, u32[]{:S(2)}, u32[]{:S(2)}) collective-permute-start(bf16[6,17,64,128]{3,2,1,0:T(8,128)(2,1)} %param.5), channel_id=1, source_target_pairs={{0,1},{1,0},{2,3},{3,2},{4,5},{5,4},{6,7},{7,6},{8,9},{9,8},{10,11... | collective-permute-start | bytes 5013512 | tf_op jit(solution)/shard_map/ppermute | solution.py:37
  2.9 5.6 %copy-start = (bf16[6,17,64,128]{3,2,1,0:T(8,128)(2,1)S(1)}, bf16[6,17,64,128]{3,2,1,0:T(8,128)(2,1)}, u32[]{:S(2)}) copy-start(bf16[6,17,64,128]{3,2,1,0:T(8,128)(2,1)} %a_ref.1) | copy-start | bytes 5013508
  2.9 5.6 %copy-start.2 = (s32[6]{0:T(128)S(1)}, s32[6]{0:T(128)}, u32[]{:S(2)}) copy-start(s32[6]{0:T(128)} %extent_ref.1) | copy-start | bytes 76
  4.7 35.8 %copy-start.1 = (s32[6]{0:T(128)S(1)}, s32[6]{0:T(128)}, u32[]{:S(2)}) copy-start(s32[6]{0:T(128)} %refs_0_.1) | copy-start | bytes 76
  4.7 39.7 %collective-permute-start.3 = (bf16[6,17,64,128]{3,2,1,0:T(8,128)(2,1)S(1)}, bf16[6,17,64,128]{3,2,1,0:T(8,128)(2,1)S(1)}, u32[]{:S(2)}, u32[]{:S(2)}) collective-permute-start(bf16[6,17,64,128]{3,2,1,0:T(8,128)(2,1)S(1)} %compare_select_fusion), channel_id=1, source_target_pairs={{0,30},{2,4},{4,2},{6,8},{8,6},{10,12},{12,10},{14,16},{16,14},{18... | collective-permute-start | bytes 5013512 | tf_op jit(solution)/shard_map/ppermute | solution.py:24
  8.5 35.9 %collective-permute-start.4 = (bf16[6,17,64,128]{3,2,1,0:T(8,128)(2,1)S(1)}, bf16[6,17,64,128]{3,2,1,0:T(8,128)(2,1)S(1)}, u32[]{:S(2)}, u32[]{:S(2)}) collective-permute-start(bf16[6,17,64,128]{3,2,1,0:T(8,128)(2,1)S(1)} %compare_select_fusion), channel_id=1, source_target_pairs={{0,2},{2,0},{4,6},{6,4},{8,10},{10,8},{12,14},{14,12},{16,18},{18,... | collective-permute-start | bytes 5013512 | tf_op jit(solution)/shard_map/ppermute | solution.py:20
  9.6 50.7 %collective-permute-start = (bf16[3,128,1152]{2,1,0:T(8,128)(2,1)S(1)}, bf16[3,128,1152]{2,1,0:T(8,128)(2,1)S(1)}, u32[]{:S(2)}, u32[]{:S(2)}) collective-permute-start(bf16[3,128,1152]{2,1,0:T(8,128)(2,1)S(1)} %get-tuple-element.16), channel_id=1, source_target_pairs={{0,1},{1,0},{2,3},{3,2},{4,5},{5,4},{6,7},{7,6},{8,9},{9,8},{10,11... | collective-permute-start | bytes 2654216 | tf_op jit(solution)/shard_map/ppermute | solution.py:37
  41.9 14.2 %collective-permute-start.6 = (bf16[34,64,128]{2,1,0:T(8,128)(2,1)S(1)}, bf16[34,64,128]{2,1,0:T(8,128)(2,1)S(1)}, u32[]{:S(2)}, u32[]{:S(2)}) collective-permute-start(bf16[34,64,128]{2,1,0:T(8,128)(2,1)S(1)} %get-tuple-element.21), channel_id=1, source_target_pairs={{0,30},{2,4},{4,2},{6,8},{8,6},{10,12},{12,10},{14,16},{16,14},{18... | collective-permute-start | bytes 1671176 | tf_op jit(solution)/shard_map/ppermute | solution.py:24
  44.4 23.2 %collective-permute-start.8 = (bf16[68,64,128]{2,1,0:T(8,128)(2,1)S(1)}, bf16[68,64,128]{2,1,0:T(8,128)(2,1)S(1)}, u32[]{:S(2)}, u32[]{:S(2)}) collective-permute-start(bf16[68,64,128]{2,1,0:T(8,128)(2,1)S(1)} %get-tuple-element.22.refs_1_), channel_id=1, source_target_pairs={{0,2},{2,0},{4,6},{6,4},{8,10},{10,8},{12,14},{14,12},{16,18},{18,... | collective-permute-start | bytes 3342344 | tf_op jit(solution)/shard_map/ppermute | solution.py:20
  44.8 16.8 %collective-permute-start.10 = (bf16[34,64,128]{2,1,0:T(8,128)(2,1)S(1)}, bf16[34,64,128]{2,1,0:T(8,128)(2,1)S(1)}, u32[]{:S(2)}, u32[]{:S(2)}) collective-permute-start(bf16[34,64,128]{2,1,0:T(8,128)(2,1)S(1)} %get-tuple-element.26), channel_id=1, source_target_pairs={{0,2},{1,27},{2,8},{3,1},{4,6},{5,31},{6,12},{7,5},{8,10},{9,3},{1... | collective-permute-start | bytes 1671176 | tf_op jit(solution)/shard_map/ppermute | solution.py:33
  45.3 27.0 %collective-permute-start.2 = (bf16[43,64,128]{2,1,0:T(8,128)(2,1)S(1)}, bf16[43,64,128]{2,1,0:T(8,128)(2,1)S(1)}, u32[]{:S(2)}, u32[]{:S(2)}) collective-permute-start(bf16[43,64,128]{2,1,0:T(8,128)(2,1)S(1)} %get-tuple-element.18), channel_id=1, source_target_pairs={{0,30},{2,4},{4,2},{6,8},{8,6},{10,12},{12,10},{14,16},{16,14},{18... | collective-permute-start | bytes 2113544 | tf_op jit(solution)/shard_map/ppermute | solution.py:24
  56.2 11.4 %collective-permute-start.9 = (bf16[34,64,128]{2,1,0:T(8,128)(2,1)S(1)}, bf16[34,64,128]{2,1,0:T(8,128)(2,1)S(1)}, u32[]{:S(2)}, u32[]{:S(2)}) collective-permute-start(bf16[34,64,128]{2,1,0:T(8,128)(2,1)S(1)} %get-tuple-element.24.refs_2_), channel_id=1, source_target_pairs={{0,2},{2,0},{4,6},{6,4},{8,10},{10,8},{12,14},{14,12},{16,18},{18,... | collective-permute-start | bytes 1671176 | tf_op jit(solution)/shard_map/ppermute | solution.py:20
  60.3 13.0 %collective-permute-start.7 = (bf16[34,64,128]{2,1,0:T(8,128)(2,1)S(1)}, bf16[34,64,128]{2,1,0:T(8,128)(2,1)S(1)}, u32[]{:S(2)}, u32[]{:S(2)}) collective-permute-start(bf16[34,64,128]{2,1,0:T(8,128)(2,1)S(1)} %collective-permute-done.6.refs_5_), channel_id=1, source_target_pairs={{0,2},{1,27},{2,8},{3,1},{4,6},{5,31},{6,12},{7,5},{8,10},{9,3},{1... | collective-permute-start | bytes 1671176 | tf_op jit(solution)/shard_map/ppermute | solution.py:33
  61.6 10.7 %collective-permute-start.5 = (bf16[25,64,128]{2,1,0:T(8,128)(2,1)S(1)}, bf16[25,64,128]{2,1,0:T(8,128)(2,1)S(1)}, u32[]{:S(2)}, u32[]{:S(2)}) collective-permute-start(bf16[25,64,128]{2,1,0:T(8,128)(2,1)S(1)} %get-tuple-element.20), channel_id=1, source_target_pairs={{0,1},{1,0},{2,3},{3,2},{4,5},{5,4},{6,7},{7,6},{8,9},{9,8},{10,11... | collective-permute-start | bytes 1228808 | tf_op jit(solution)/shard_map/ppermute | solution.py:37
